TPU v7x, 128 devices: a whole 4x4x4 slice. The times are simulated.
128 devices in a mesh: wide: 16 (over y, z), narrow: 8 (over x, core).
Axes of the slice: x: 4, y: 4, z: 4, core: 2. Of those that a mesh axis runs over, the one named last changes fastest.
Arguments:
- queries: bfloat16 [32, 128, 2304], P('wide'), may hold values from -112 to 112
- new_kv: bfloat16 [32, 2, 128, 2304], P('wide', None, 'narrow'), may hold values from -4 to 4
- cache_pool: bfloat16 [32, 32, 2, 128, 2304], P('wide', 'narrow'), may hold values from -4 to 4
- page_table: int32 [32, 32], P('wide'), may hold values from 0 to 31, as said below
- cached_len: int32 [32], P('wide'), may hold values from 0 to 4096, as said below
- residual: bfloat16 [4096, 2304], P('wide'), may hold values from -0.1796875 to 0.1796875
- norm_gain: float32 [2304], replicated, may hold values from 0.1 to 1.9
- expert_ids: int32 [4096, 2], P('wide'), may hold values from 0 to 7, all different within a row; in each aligned block of 256 rows (0 to 255, 256 to 511, ...) at most 80 rows name the same one
- route_weight: float32 [4096, 2], P('wide'), may hold values from 0.1 to 1
- w_gate_up: bfloat16 [8, 2304, 2, 5760], P(None, 'narrow', None, 'wide'), may hold values from -0.125 to 0.125
- w_down: bfloat16 [8, 5760, 2304], P(None, 'wide', 'narrow'), may hold values from -0.078125 to 0.078125
Outputs:
- layer_out: bfloat16 [4096, 2304], P('wide', 'narrow')
Inputs may be any that keep to these rules, and one draw needn't show every extreme that they name: `page_table`: for each request the 32 entries are distinct, and entry j lies in (j % 8) * 4 to (j % 8) * 4 + 3. `cached_len`: some request has exactly 4096 cached tokens. `expert_ids`: A token's two experts differ; among the 256 tokens of one index of wide no expert is named more than 80 times.
All inputs are finite; a program needn't handle non-finite values.
Results may differ from a plain program's by a relative error of at most 0.035.
Values may be sent and summed in bfloat16 or wider, within the bound.
No kernel may reach another device: no remote copies, remote signals or barrier semaphores. Data moves between devices by JAX's collectives and lax.ppermute only.
A program may use at most 192 MiB of HBM per device.

v0:
```python
import functools

import jax
import jax.numpy as jnp
from jax import lax
from jax.experimental import pallas as pl
from jax.experimental.pallas import tpu as pltpu
from jax.sharding import PartitionSpec as P


HD = 64
CAP = 80
NEG_FILL = -(2.0**100)
SCORE_SCALE = 0.125
EPSILON = 1e-05
STAT_ROWS = 16
RING = 4
STEPS = (2, 1, -1)


F32 = jnp.float32
BF16 = jnp.bfloat16


def nt_dot(a, b):
    return lax.dot_general(a, b, (((1,), (1,)), ((), ())), preferred_element_type=F32)


def tn_dot(a, b):
    return lax.dot_general(a, b, (((0,), (0,)), ((), ())), preferred_element_type=F32)


def attend_kernel(table, length, place, q_ref, k_ref, v_ref, nk_ref, nv_ref, out_ref, top_sc, den_sc, *, share):
    groups = out_ref.shape[0]
    req, group = pl.program_id(0), pl.program_id(1)
    new_len = q_ref.shape[1]
    pages, page_len = k_ref.shape[1], k_ref.shape[3]
    local_new = nk_ref.shape[2]
    pairs = q_ref.shape[2] // 128
    lane_at = pl.multiple_of(req * new_len, new_len)
    col = lax.broadcasted_iota(jnp.int32, (new_len, 128), 1)
    row = lax.broadcasted_iota(jnp.int32, (128, new_len), 0)
    page_row = lax.broadcasted_iota(jnp.int32, (page_len, 2 * new_len), 0)
    new_row = lax.broadcasted_iota(jnp.int32, (local_new, 2 * new_len), 0) + place[0] * local_new
    new_col = lax.broadcasted_iota(jnp.int32, (local_new, 2 * new_len), 1) % new_len
    new_valid = new_row <= new_col
    logical = [place[0] + i * groups for i in range(pages)]
    places = [table[req, j] - place[0] * pages for j in logical]
    limits = [length[req] - j * page_len for j in logical]

    @pl.when((req == 0) & (group == 0))
    def _():
        top_sc[...] = jnp.zeros_like(top_sc)
        den_sc[...] = jnp.zeros_like(den_sc)

    for pair in range(pairs):
        at = slice(pair * 128, pair * 128 + 128)
        q = q_ref[0, :, at].astype(F32) * SCORE_SCALE
        both = jnp.concatenate([jnp.where(col < HD, q, 0.0), jnp.where(col < HD, 0.0, q)], axis=0).astype(BF16)
        parts = [
            jnp.where(page_row < limits[i], nt_dot(k_ref[0, places[i], 0, :, at], both), NEG_FILL) for i in range(pages)
        ]
        parts.append(jnp.where(new_valid, nt_dot(nk_ref[0, 0, :, at], both), NEG_FILL))
        top = functools.reduce(jnp.maximum, [jnp.max(s, axis=0, keepdims=True) for s in parts])
        top = top.astype(BF16).astype(F32)
        weights = [jnp.exp(s - top) for s in parts]
        den = functools.reduce(jnp.add, [jnp.sum(w, axis=0, keepdims=True) for w in weights])
        low = jnp.concatenate([w.astype(BF16) for w in weights[:-1]], axis=0)
        values = jnp.concatenate([v_ref[0, places[i], 0, :, at] for i in range(pages)], axis=0)
        num = tn_dot(values, low) + tn_dot(nv_ref[0, 0, :, at], weights[-1].astype(BF16))
        num = jnp.where(row < HD, num[:, :new_len], num[:, new_len:]).astype(BF16)
        for piece in range(4):
            index = (group * pairs + pair) * 4 + piece
            dest = index // (share // 32)
            offset = pl.multiple_of((index - dest * (share // 32)) * 32, 32)
            out_ref[dest, pl.ds(offset, 32), pl.ds(lane_at, new_len)] = num[piece * 32 : piece * 32 + 32]
        head = (group * pairs + pair) * 2
        for half in range(2):
            lanes = slice(half * new_len, half * new_len + new_len)
            top_sc[head + half, :, pl.ds(lane_at, new_len)] = top[:, lanes]
            den_sc[head + half, :, pl.ds(lane_at, new_len)] = den[:, lanes]

    @pl.when((req == pl.num_programs(0) - 1) & (group == pl.num_programs(1) - 1))
    def _():
        for dest in range(out_ref.shape[0]):
            first = dest * share // HD
            stats = jnp.concatenate([top_sc[first : first + 8, 0, :], den_sc[first : first + 8, 0, :]], axis=0)
            out_ref[dest, share : share + STAT_ROWS, :] = stats.astype(BF16)


def attend(table, length, place, queries, cache_pool, new_kv, dests):
    req_here, new_len, width = queries.shape
    pages, page_len = cache_pool.shape[1], cache_pool.shape[3]
    local_new = new_kv.shape[2]
    share = width // dests
    groups = 3
    block = width // groups
    heads = width // HD
    keys = pages * page_len + local_new
    return pl.pallas_call(
        functools.partial(attend_kernel, share=share),
        grid_spec=pltpu.PrefetchScalarGridSpec(
            num_scalar_prefetch=3,
            grid=(req_here, groups),
            in_specs=[
                pl.BlockSpec((1, new_len, block), lambda r, g, *_: (r, 0, g)),
                pl.BlockSpec((1, pages, 1, page_len, block), lambda r, g, *_: (r, 0, 0, 0, g)),
                pl.BlockSpec((1, pages, 1, page_len, block), lambda r, g, *_: (r, 0, 1, 0, g)),
                pl.BlockSpec((1, 1, local_new, block), lambda r, g, *_: (r, 0, 0, g)),
                pl.BlockSpec((1, 1, local_new, block), lambda r, g, *_: (r, 1, 0, g)),
            ],
            out_specs=pl.BlockSpec((dests, share + STAT_ROWS, req_here * new_len), lambda r, g, *_: (0, 0, 0)),
            scratch_shapes=[pltpu.VMEM((heads + 12, 1, req_here * new_len), F32)] * 2,
        ),
        out_shape=jax.ShapeDtypeStruct((dests, share + STAT_ROWS, req_here * new_len), BF16),
        cost_estimate=pl.CostEstimate(
            flops=4 * req_here * new_len * width * keys,
            bytes_accessed=cache_pool.size * 2 + queries.size * 2,
            transcendentals=req_here * heads * new_len * keys,
        ),
        compiler_params=pltpu.CompilerParams(vmem_limit_bytes=60 << 20),
        name="attend",
    )(table, length, place, queries, cache_pool, cache_pool, new_kv, new_kv)


def join_kernel(place, recv_ref, res_ref, gain_ref, slot_ref, placed_ref, hidden_ref, spread_sc, *, share):
    groups = recv_ref.shape[0]
    tokens = recv_ref.shape[2]
    slots = placed_ref.shape[0] * placed_ref.shape[1]
    padded = placed_ref.shape[2]
    tops = [recv_ref[g, share : share + 8, :].astype(F32) for g in range(groups)]
    top = functools.reduce(jnp.maximum, tops)
    scales = [jnp.exp(t - top) for t in tops]
    den = functools.reduce(jnp.add, [s * recv_ref[g, share + 8 : share + 16, :].astype(F32) for g, s in enumerate(scales)])
    offset = pl.multiple_of(place[0] % 2 * (HD // 2), HD // 2)
    total = res_ref[...]
    for g in range(groups):
        factor = scales[g] / den
        for head in range(5):
            spread_sc[g, head * HD : head * HD + HD, :] = jnp.broadcast_to(factor[head : head + 1, :], (HD, tokens))
        total = total + recv_ref[g, :share, :].astype(F32) * spread_sc[g, pl.ds(offset, share), :]
    hidden_ref[...] = total
    square = jnp.sum(total * total, axis=0, keepdims=True)
    high = square.astype(BF16).astype(F32)
    row = lax.broadcasted_iota(jnp.int32, (padded - share, tokens), 0)
    tail = jnp.where(row == 0, high, jnp.where(row == 1, square - high, 0.0)).astype(BF16)
    rows = jnp.concatenate([(total * gain_ref[...]).astype(BF16), tail], axis=0)
    at = lax.broadcasted_iota(jnp.int32, (slots, tokens), 0)
    picks = (at == slot_ref[0:1, :]) | (at == slot_ref[1:2, :])
    placed = nt_dot(jnp.where(picks, 1.0, 0.0).astype(BF16), rows)
    placed_ref[...] = placed.astype(BF16).reshape(placed_ref.shape)


def join(place, recv, residual, gain, slots, experts):
    groups, rows, tokens = recv.shape
    share = rows - STAT_ROWS
    padded = -(-(share + 2) // 128) * 128
    whole = lambda *shape: pl.BlockSpec(shape, lambda i, *_: (0,) * len(shape))
    return pl.pallas_call(
        functools.partial(join_kernel, share=share),
        grid_spec=pltpu.PrefetchScalarGridSpec(
            num_scalar_prefetch=1,
            grid=(1,),
            in_specs=[
                whole(groups, rows, tokens),
                whole(share, tokens),
                whole(share, 1),
                whole(2, tokens),
            ],
            out_specs=[whole(experts, CAP, padded), whole(share, tokens)],
            scratch_shapes=[pltpu.VMEM((groups, 5 * HD, tokens), F32)],
        ),
        out_shape=[
            jax.ShapeDtypeStruct((experts, CAP, padded), BF16),
            jax.ShapeDtypeStruct((share, tokens), F32),
        ],
        cost_estimate=pl.CostEstimate(
            flops=2 * experts * CAP * padded * tokens, bytes_accessed=recv.size * 2 + experts * CAP * padded * 2, transcendentals=0
        ),
        compiler_params=pltpu.CompilerParams(vmem_limit_bytes=10 << 20),
        name="join",
    )(place, recv, residual, gain, slots)


def norm_kernel(recv_ref, out_ref, *, share):
    groups, _, _ = recv_ref.shape
    blocks = [recv_ref[g].astype(F32) for g in range(groups)]
    square = functools.reduce(jnp.add, [b[:, share : share + 1] + b[:, share + 1 : share + 2] for b in blocks])
    scale = lax.rsqrt(square / (groups * share) + EPSILON)
    out_ref[...] = jnp.concatenate([b[:, :share] * scale for b in blocks], axis=1).astype(BF16)


def norm_rows(recv, share):
    groups, rows, _ = recv.shape
    return pl.pallas_call(
        functools.partial(norm_kernel, share=share),
        out_shape=jax.ShapeDtypeStruct((rows, groups * share), BF16),
        cost_estimate=pl.CostEstimate(flops=0, bytes_accessed=recv.size * 4, transcendentals=0),
        compiler_params=pltpu.CompilerParams(vmem_limit_bytes=4 << 20),
        name="norm_rows",
    )(recv)


def stack_kernel(*refs):
    blocks, outs = refs[:4], refs[4:]
    for i, ref in enumerate(blocks):
        outs[i // 2][i % 2] = ref[...]


def stack(blocks):
    rows, width = blocks[0].shape
    pairs = pl.pallas_call(
        stack_kernel,
        out_shape=[jax.ShapeDtypeStruct((2, rows, width), BF16)] * 2,
        cost_estimate=pl.CostEstimate(flops=0, bytes_accessed=16 * rows * width, transcendentals=0),
        compiler_params=pltpu.CompilerParams(vmem_limit_bytes=4 << 20),
        name="stack",
    )(*blocks)
    return [pair.reshape(2 * rows, width) for pair in pairs]


def expert_kernel(*refs, count):
    blocks, gate_up_ref, down_ref = refs[:count], refs[count], refs[count + 1]
    outs, (x_sc, weight_sc, both_sc, y_sc, sems) = refs[count + 2 : 2 * count + 2], refs[2 * count + 2 :]
    rows = blocks[0].shape[0]
    groups, _, units = gate_up_ref.shape
    share = x_sc.shape[1] // groups
    half = weight_sc.shape[1] // 2
    tile = 256
    loads = [pltpu.make_async_copy(b, x_sc.at[pl.ds(i * rows, rows)], sems.at[i]) for i, b in enumerate(blocks)]
    stores = [pltpu.make_async_copy(y_sc.at[pl.ds(i * rows, rows)], o, sems.at[count + i]) for i, o in enumerate(outs)]
    for load in loads:
        load.start()
    for g in range(groups):
        weight_sc[g * share : g * share + share, :units] = gate_up_ref[g, :share]
        weight_sc[g * share : g * share + share, half : half + units] = gate_up_ref[g, share:]
    for load in loads:
        load.wait()

    @pl.loop(0, 2 * half // tile)
    def _(j):
        lanes = pl.ds(pl.multiple_of(j * tile, tile), tile)
        both_sc[:, lanes] = jnp.dot(x_sc[...], weight_sc[:, lanes], preferred_element_type=F32)

    gate, up = both_sc[:, :units], both_sc[:, half : half + units]
    act = (gate / (1.0 + jnp.exp(-gate)) * up).astype(BF16)

    @pl.loop(0, down_ref.shape[0] // tile)
    def _(j):
        lanes = pl.ds(pl.multiple_of(j * tile, tile), tile)
        y_sc[:, lanes] = nt_dot(act, down_ref[lanes, :]).astype(BF16)

    for copy in stores:
        copy.start()
    for copy in stores:
        copy.wait()


def expert(blocks, gate_up, down):
    rows, width = blocks[0].shape
    units = down.shape[1]
    count = len(blocks)
    total = count * rows
    packed = 2 * (-(-units // 128) * 128)
    held = pl.BlockSpec(memory_space=pltpu.VMEM)
    anywhere = pl.BlockSpec(memory_space=pl.ANY)
    return pl.pallas_call(
        functools.partial(expert_kernel, count=count),
        in_specs=[anywhere] * count + [held] * 2,
        out_specs=[anywhere] * count,
        out_shape=[jax.ShapeDtypeStruct((rows, width), BF16)] * count,
        scratch_shapes=[
            pltpu.VMEM((total, width), BF16),
            pltpu.VMEM((width, packed), BF16),
            pltpu.VMEM((total, packed), F32),
            pltpu.VMEM((total, width), BF16),
            pltpu.SemaphoreType.DMA((2 * count,)),
        ],
        cost_estimate=pl.CostEstimate(
            flops=6 * total * width * units,
            bytes_accessed=4 * total * width + 6 * width * units,
            transcendentals=total * units,
        ),
        compiler_params=pltpu.CompilerParams(vmem_limit_bytes=26 << 20),
        name="expert",
    )(*blocks, gate_up, down)


def total_of(refs):
    return functools.reduce(jnp.add, [ref[...].astype(F32) for ref in refs])


def add_kernel(*refs):
    outs = refs[6:]
    rows = outs[0].shape[0]
    for i, out in enumerate(outs):
        at = slice(i % 2 * rows, i % 2 * rows + rows)
        some = refs[:3] if i < 2 else refs[3:6]
        out[...] = functools.reduce(jnp.add, [ref[at, :].astype(F32) for ref in some]).astype(BF16)


def add_blocks(low, high):
    rows, width = low[0].shape
    return pl.pallas_call(
        add_kernel,
        out_shape=[jax.ShapeDtypeStruct((rows // 2, width), BF16)] * 4,
        cost_estimate=pl.CostEstimate(flops=0, bytes_accessed=16 * rows * width, transcendentals=0),
        compiler_params=pltpu.CompilerParams(vmem_limit_bytes=8 << 20),
        name="add_blocks",
    )(*low, *high)


def finish_kernel(*refs):
    out_ref = refs[-1]
    groups, _, share = out_ref.shape
    both = jnp.concatenate([total_of(refs[:4]), total_of(refs[4:8])], axis=0).astype(BF16)
    for g in range(groups):
        out_ref[g] = both[:, g * share : (g + 1) * share]


def finish(blocks, groups):
    rows, width = blocks[0].shape
    return pl.pallas_call(
        finish_kernel,
        out_shape=jax.ShapeDtypeStruct((groups, 2 * rows, width // groups), BF16),
        cost_estimate=pl.CostEstimate(flops=0, bytes_accessed=20 * rows * width, transcendentals=0),
        compiler_params=pltpu.CompilerParams(vmem_limit_bytes=8 << 20),
        name="finish",
    )(*blocks)


def mix_kernel(rows_ref, slot_ref, weight_ref, hidden_ref, out_ref):
    tokens = out_ref.shape[1]
    slots = rows_ref.shape[0]
    at = lax.broadcasted_iota(jnp.int32, (slots, tokens), 0)
    table = jnp.where(at == slot_ref[0:1, :], weight_ref[0:1, :], 0.0)
    table = table + jnp.where(at == slot_ref[1:2, :], weight_ref[1:2, :], 0.0)
    high = table.astype(BF16)
    low = (table - high.astype(F32)).astype(BF16)
    rows = rows_ref[...]
    out_ref[...] = (hidden_ref[...] + (tn_dot(rows, high) + tn_dot(rows, low))).astype(BF16)


def mix(rows, slots, weights, hidden):
    return pl.pallas_call(
        mix_kernel,
        out_shape=jax.ShapeDtypeStruct(hidden.shape, BF16),
        cost_estimate=pl.CostEstimate(flops=4 * hidden.size * rows.shape[0], bytes_accessed=rows.size * 2 + hidden.size * 6, transcendentals=0),
        compiler_params=pltpu.CompilerParams(vmem_limit_bytes=6 << 20),
        name="mix",
    )(rows, slots, weights, hidden)


def ring_pairs(axis, step):
    pairs = []
    for index in range(RING * RING):
        y, z = divmod(index, RING)
        if axis == "y":
            y = (y + step) % RING
        else:
            z = (z + step) % RING
        pairs.append((index, y * RING + z))
    return pairs


def shift(x, axis, step):
    return lax.ppermute(x, "wide", ring_pairs(axis, step))


def local(
    queries,
    new_kv,
    cache_pool,
    page_table,
    cached_len,
    residual,
    norm_gain,
    expert_ids,
    route_weight,
    w_gate_up,
    w_down,
):
    narrow_count = lax.axis_size("narrow")
    narrow_pos = lax.axis_index("narrow").astype(jnp.int32)
    _, _, width = queries.shape
    token_rows = expert_ids.shape[0]
    expert_count = w_gate_up.shape[0]
    units = w_down.shape[1]
    share = width // narrow_count

    def exchange(x):
        return lax.all_to_all(x, "narrow", 0, 0, tiled=True)

    down_all = exchange(jnp.transpose(w_down, (0, 2, 1)))
    place = narrow_pos.reshape(1)
    sums = attend(page_table, cached_len, place, queries, cache_pool, new_kv, narrow_count)
    sums, down_all, w_gate_up = lax.optimization_barrier((sums, down_all, w_gate_up))
    later = jnp.concatenate([w_gate_up[:, :, 0], w_gate_up[:, :, 1]], axis=1)
    sums = exchange(sums)

    flat_ids = expert_ids.reshape(token_rows * 2)
    onehot = (flat_ids[:, None] == jnp.arange(expert_count, dtype=jnp.int32)[None, :]).astype(BF16)
    order = jnp.arange(token_rows * 2, dtype=jnp.int32)
    earlier = jnp.dot((order[:, None] > order[None, :]).astype(BF16), onehot, preferred_element_type=F32)
    position = jnp.sum(earlier * onehot.astype(F32), axis=1).astype(jnp.int32)
    slots = (flat_ids * CAP + position).reshape(token_rows, 2)

    res_share = lax.dynamic_slice_in_dim(residual, narrow_pos * share, share, 1).astype(F32).T
    gain_share = lax.dynamic_slice_in_dim(norm_gain, narrow_pos * share, share, 0)[:, None]
    placed, hidden = join(place, sums, res_share, gain_share, slots.T, expert_count)
    placed = exchange(placed)
    later, placed = lax.optimization_barrier((later, placed))
    later = exchange(later)
    down_all = down_all.reshape(width, units)
    rows = norm_rows(placed, share)

    half = CAP // 2

    def around(block, axis):
        return [block, *(shift(block, axis, step) for step in STEPS)]

    near, far = [], []
    for first, second, block in (("z", "y", rows[:half]), ("y", "z", rows[half:])):
        low, high = stack(around(block, first))
        before_low, after_high = shift(low, second, 1), shift(high, second, -1)
        before_high, after_low = shift(high, second, 1), shift(low, second, -1)
        near += [low, high, before_low, before_high, after_low, after_high]
        far += [shift(before_low, second, 1), shift(after_high, second, -1)]
    near = list(expert(near, later, down_all))
    near[0], *far = lax.optimization_barrier((near[0], *far))
    far = expert(far, later, down_all)

    def back(blocks, axis):
        return [blocks[0], *(shift(block, axis, -step) for block, step in zip(blocks[1:], STEPS))]

    def joined(a, b):
        return (a.astype(F32) + b.astype(F32)).astype(BF16)

    four = []
    for color, second in enumerate(("y", "z")):
        low, high, before_low, before_high, after_low, after_high = near[6 * color : 6 * color + 6]
        got_low = shift(before_low, second, -1)
        got_high = shift(after_high, second, 1)
        via_low, via_high = shift(far[2 * color], second, 1), shift(far[2 * color + 1], second, -1)
        more_low, more_high = shift(joined(after_low, via_low), second, 1), shift(joined(before_high, via_high), second, -1)
        four.append(add_blocks([low, got_low, more_low], [high, got_high, more_high]))
    out_rows = finish([*back(four[0], "z"), *back(four[1], "y")], narrow_count)
    out_rows = exchange(out_rows)
    return mix(out_rows.reshape(expert_count * CAP, share), slots.T, route_weight.T, hidden).T


def solution(mesh):
    return jax.shard_map(
        local,
        mesh=mesh,
        in_specs=(
            P("wide", None, None),
            P("wide", None, "narrow", None),
            P("wide", "narrow", None, None, None),
            P("wide", None),
            P("wide"),
            P("wide", None),
            P(),
            P("wide", None),
            P("wide", None),
            P(None, "narrow", None, "wide"),
            P(None, "wide", "narrow"),
        ),
        out_specs=P("wide", "narrow"),
        check_vma=False,
    )
```

profile of v0, /device:TPU:1, one launch (start us, length us, event | category | flops | bytes accessed | tf_op | source)
XLA Modules:
  0.0 217.3 jit_solution(3178225222951273322)
XLA Ops:
  0.0 5.9 %all-to-all-start = ((bf16[8,288,360]{2,1,0:T(8,128)(2,1)}), bf16[8,288,360]{2,1,0:T(8,128)(2,1)S(1)}, u32[]{:S(2)}, u32[]{:S(2)}) async-start(bf16[8,288,360]{2,1,0:T(8,128)(2,1)} %bitcast.34), calls=%async_computation | async-start | bytes 3538944 | tf_op jit(solution)/shard_map/all_to_all | solution.py:392
  5.9 18.1 %attend.1 = bf16[8,304,256]{2,1,0:T(8,128)(2,1)} custom-call(s32[2,32]{1,0:T(2,128)} %table.1, s32[2]{0:T(128)} %length.1, s32[1]{0:T(128)} %bitcast.place, bf16[2,128,2304]{2,1,0:T(8,128)(2,1)} %q_ref.1, bf16[2,4,2,128,2304]{4,3,2,1,0:T(8,128)(2,1)} %v_ref.1, bf16[2,4,2,128,2304]{4,3,2,1,0:T(8,128)(2,1)} %v_ref.1, bf16[2,2,16,2304]{3,2,1,0:T(8,128)(2,1)} %nv_ref.1, ...), custom_call_target="tpu_custom_call" | custom-call | flops 1245708288 | bytes 10616832 | tf_op jit(solution)/shard_map/attend/pallas_call | solution.py:100
  24.0 4.6 %all-to-all-done = bf16[8,288,360]{2,1,0:T(8,128)(2,1)S(1)} async-done(((bf16[8,288,360]{2,1,0:T(8,128)(2,1)}), bf16[8,288,360]{2,1,0:T(8,128)(2,1)S(1)}, u32[]{:S(2)}, u32[]{:S(2)}) %all-to-all-start) | async-done | bytes 1658912 | tf_op jit(solution)/shard_map/all_to_all | solution.py:392
  28.6 5.1 %all-to-all-start.1 = ((bf16[8,304,256]{2,1,0:T(8,128)(2,1)}), bf16[8,304,256]{2,1,0:T(8,128)(2,1)}, u32[]{:S(2)}, u32[]{:S(2)}) async-start(bf16[8,304,256]{2,1,0:T(8,128)(2,1)} %attend.1), calls=%async_computation.1 | async-start | bytes 2490368 | tf_op jit(solution)/shard_map/all_to_all | solution.py:392
  35.7 4.2 %copy.15 = bf16[8,288,2,360]{3,1,0,2:T(8,128)(2,1)} copy(bf16[8,288,2,360]{3,2,1,0:T(2,128)(2,1)} %param.20) | data formatting | bytes 6635520 | tf_op jit(solution)/shard_map/optimization_barrier | solution.py:397
  39.9 11.0 %all-to-all-done.1.recv_ref = bf16[8,304,256]{2,1,0:T(8,128)(2,1)} async-done(((bf16[8,304,256]{2,1,0:T(8,128)(2,1)}), bf16[8,304,256]{2,1,0:T(8,128)(2,1)}, u32[]{:S(2)}, u32[]{:S(2)}) %all-to-all-start.1) | async-done | bytes 1245216 | tf_op jit(solution)/shard_map/all_to_all | solution.py:392
  50.9 2.2 %join.1 = (bf16[8,80,384]{2,1,0:T(8,128)(2,1)S(1)}, f32[288,256]{1,0:T(8,128)S(1)}) custom-call(s32[1]{0:T(128)} %bitcast.place, bf16[8,304,256]{2,1,0:T(8,128)(2,1)} %all-to-all-done.1.recv_ref, f32[288,256]{1,0:T(8,128)S(1)} %convert_bitcast_fusion.res_ref, f32[288,1]{1,0:T(8,128)S(1)} %broadcast_in_dim.3.gain_ref, s32[2,256]{1,0:T(2,128)S(1)} %add_bitcast_fusion.slot_ref), custom_call_target="tpu_custom_call" | custom-call | flops 125829120 | bytes 1736704 | tf_op jit(solution)/shard_map/join/pallas_call | solution.py:159
  54.6 4.4 %all-to-all-start.2 = ((bf16[8,80,384]{2,1,0:T(8,128)(2,1)}), bf16[8,80,384]{2,1,0:T(8,128)(2,1)S(1)}, u32[]{:S(2)}, u32[]{:S(2)}) async-start(bf16[8,80,384]{2,1,0:T(8,128)(2,1)} %copy-done.1), calls=%async_computation.2 | async-start | bytes 983040 | tf_op jit(solution)/shard_map/all_to_all | solution.py:392
  59.0 2.4 %slice_bitcast_fusion.1 = (bf16[8,288,360]{2,1,0:T(8,128)(2,1)S(1)}, bf16[8,288,360]{2,1,0:T(8,128)(2,1)S(1)}) fusion(bf16[8,288,2,360]{3,1,0,2:T(8,128)(2,1)} %copy.15), kind=kLoop, calls=%fused_computation.2 | loop fusion | bytes 6635520 | tf_op jit(solution)/shard_map/squeeze | solution.py:398
  61.4 2.2 %pad_maximum_fusion = bf16[8,576,360]{2,1,0:T(8,128)(2,1)} fusion(bf16[8,288,360]{2,1,0:T(8,128)(2,1)S(1)} %get-tuple-element.86, bf16[8,288,360]{2,1,0:T(8,128)(2,1)S(1)} %get-tuple-element.85), kind=kLoop, calls=%fused_computation | loop fusion | flops 6635520 | bytes 6635520 | tf_op jit(solution)/shard_map/concatenate | solution.py:398
  63.6 4.4 %all-to-all-done.2.recv_ref = bf16[8,80,384]{2,1,0:T(8,128)(2,1)S(1)} async-done(((bf16[8,80,384]{2,1,0:T(8,128)(2,1)}), bf16[8,80,384]{2,1,0:T(8,128)(2,1)S(1)}, u32[]{:S(2)}, u32[]{:S(2)}) %all-to-all-start.2) | async-done | bytes 491552 | tf_op jit(solution)/shard_map/all_to_all | solution.py:392
  68.0 5.3 %all-to-all-start.3 = ((bf16[8,576,360]{2,1,0:T(8,128)(2,1)}), bf16[8,576,360]{2,1,0:T(8,128)(2,1)}, u32[]{:S(2)}, u32[]{:S(2)}) async-start(bf16[8,576,360]{2,1,0:T(8,128)(2,1)} %pad_maximum_fusion), calls=%async_computation.3 | async-start | bytes 7077888 | tf_op jit(solution)/shard_map/all_to_all | solution.py:392
  73.7 3.0 %collective-permute-start.7 = (bf16[40,2304]{1,0:T(8,128)(2,1)S(1)}, bf16[40,2304]{1,0:T(8,128)(2,1)S(1)}, u32[]{:S(2)}, u32[]{:S(2)}) collective-permute-start(bf16[40,2304]{1,0:T(8,128)(2,1)S(1)} %get-tuple-element.87.refs_0_), channel_id=1, source_target_pairs={{0,64},{8,72},{16,80},{24,88},{32,96},{40,104},{48,112},{56,120},{... | collective-permute-start | bytes 552968 | tf_op jit(solution)/shard_map/ppermute | solution.py:367
  77.1 2.3 %collective-permute-start.9 = (bf16[40,2304]{1,0:T(8,128)(2,1)S(1)}, bf16[40,2304]{1,0:T(8,128)(2,1)S(1)}, u32[]{:S(2)}, u32[]{:S(2)}) collective-permute-start(bf16[40,2304]{1,0:T(8,128)(2,1)S(1)} %get-tuple-element.87.refs_0_), channel_id=1, source_target_pairs={{0,96},{8,104},{16,112},{24,120},{32,0},{40,8},{48,16},{56,24},{64... | collective-permute-start | bytes 552968 | tf_op jit(solution)/shard_map/ppermute | solution.py:367
  79.4 3.6 %collective-permute-start = (bf16[40,2304]{1,0:T(8,128)(2,1)S(1)}, bf16[40,2304]{1,0:T(8,128)(2,1)S(1)}, u32[]{:S(2)}, u32[]{:S(2)}) collective-permute-start(bf16[40,2304]{1,0:T(8,128)(2,1)S(1)} %get-tuple-element.88.refs_0_), channel_id=1, source_target_pairs={{0,16},{8,24},{16,0},{24,8},{32,48},{40,56},{48,32},{56,40},{64,80... | collective-permute-start | bytes 552968 | tf_op jit(solution)/shard_map/ppermute | solution.py:367
  87.7 2.2 %collective-permute-start.13 = (bf16[80,2304]{1,0:T(8,128)(2,1)S(1)}, bf16[80,2304]{1,0:T(8,128)(2,1)}, u32[]{:S(2)}, u32[]{:S(2)}) collective-permute-start(bf16[80,2304]{1,0:T(8,128)(2,1)S(1)} %bitcast.25), channel_id=1, source_target_pairs={{0,24},{8,0},{16,8},{24,16},{32,56},{40,32},{48,40},{56,48},{64,88... | collective-permute-start | bytes 1105928 | tf_op jit(solution)/shard_map/ppermute | solution.py:367
  91.7 2.7 %collective-permute-start.6 = (bf16[80,2304]{1,0:T(8,128)(2,1)S(1)}, bf16[80,2304]{1,0:T(8,128)(2,1)}, u32[]{:S(2)}, u32[]{:S(2)}) collective-permute-start(bf16[80,2304]{1,0:T(8,128)(2,1)S(1)} %bitcast.31), channel_id=1, source_target_pairs={{0,96},{8,104},{16,112},{24,120},{32,0},{40,8},{48,16},{56,24},{64... | collective-permute-start | bytes 1105928 | tf_op jit(solution)/shard_map/ppermute | solution.py:367
  95.9 3.5 %collective-permute-done.10.refs_8_ = bf16[80,2304]{1,0:T(8,128)(2,1)} collective-permute-done((bf16[80,2304]{1,0:T(8,128)(2,1)S(1)}, bf16[80,2304]{1,0:T(8,128)(2,1)}, u32[]{:S(2)}, u32[]{:S(2)}) %collective-permute-start.10) | collective-permute-done | bytes 368672 | tf_op jit(solution)/shard_map/ppermute | solution.py:367
  123.0 15.1 %expert.2 = (bf16[80,2304]{1,0:T(8,128)(2,1)S(1)}, bf16[80,2304]{1,0:T(8,128)(2,1)S(1)}, bf16[80,2304]{1,0:T(8,128)(2,1)S(1)}, bf16[80,2304]{1,0:T(8,128)(2,1)S(...) custom-call(bf16[80,2304]{1,0:T(8,128)(2,1)S(1)} %bitcast.30, ...), custom_call_target="tpu_custom_call" | custom-call | flops 4777574400 | bytes 13824000 | tf_op jit(solution)/shard_map/expert/pallas_call | solution.py:267
  138.2 8.3 %expert.3 = (bf16[80,2304]{1,0:T(8,128)(2,1)S(1)}, bf16[80,2304]{1,0:T(8,128)(2,1)S(1)}, bf16[80,2304]{1,0:T(8,128)(2,1)S(1)}, bf16[80,2304]{1,0:T(8,128)(2,1)S(1)}) custom-call(bf16[80,2304]{1,0:T(8,128)(2,1)} %collective-permute-done.14.refs_0_, bf16[80,2304]{1,0:T(8,128)(2,1)} %collective-permute-done.15.refs_1_, ...), custom_call_target="tpu_custom_call" | custom-call | flops 1592524800 | bytes 7925760 | tf_op jit(solution)/shard_map/expert/pallas_call | solution.py:267
  146.5 3.8 %collective-permute-start.31 = (bf16[80,2304]{1,0:T(8,128)(2,1)S(1)}, bf16[80,2304]{1,0:T(8,128)(2,1)S(1)}, u32[]{:S(2)}, u32[]{:S(2)}) collective-permute-start(bf16[80,2304]{1,0:T(8,128)(2,1)S(1)} %get-tuple-element.79), channel_id=1, source_target_pairs={{0,24},{8,0},{16,8},{24,16},{32,56},{40,32},{48,40},{56,48},{64,88... | collective-permute-start | bytes 1105928 | tf_op jit(solution)/shard_map/ppermute | solution.py:367
  150.3 2.7 %collective-permute-start.27 = (bf16[80,2304]{1,0:T(8,128)(2,1)S(1)}, bf16[80,2304]{1,0:T(8,128)(2,1)S(1)}, u32[]{:S(2)}, u32[]{:S(2)}) collective-permute-start(bf16[80,2304]{1,0:T(8,128)(2,1)S(1)} %get-tuple-element.73), channel_id=1, source_target_pairs={{0,24},{8,0},{16,8},{24,16},{32,56},{40,32},{48,40},{56,48},{64,88... | collective-permute-start | bytes 1105928 | tf_op jit(solution)/shard_map/ppermute | solution.py:367
  153.0 2.7 %collective-permute-start.22 = (bf16[80,2304]{1,0:T(8,128)(2,1)S(1)}, bf16[80,2304]{1,0:T(8,128)(2,1)S(1)}, u32[]{:S(2)}, u32[]{:S(2)}) collective-permute-start(bf16[80,2304]{1,0:T(8,128)(2,1)S(1)} %get-tuple-element.67), channel_id=1, source_target_pairs={{0,96},{8,104},{16,112},{24,120},{32,0},{40,8},{48,16},{56,24},{64... | collective-permute-start | bytes 1105928 | tf_op jit(solution)/shard_map/ppermute | solution.py:367
  160.4 2.8 %collective-permute-start.18 = (bf16[80,2304]{1,0:T(8,128)(2,1)S(1)}, bf16[80,2304]{1,0:T(8,128)(2,1)S(1)}, u32[]{:S(2)}, u32[]{:S(2)}) collective-permute-start(bf16[80,2304]{1,0:T(8,128)(2,1)S(1)} %get-tuple-element.57), channel_id=1, source_target_pairs={{0,96},{8,104},{16,112},{24,120},{32,0},{40,8},{48,16},{56,24},{64... | collective-permute-start | bytes 1105928 | tf_op jit(solution)/shard_map/ppermute | solution.py:367
  168.3 2.8 %collective-permute-start.23 = (bf16[80,2304]{1,0:T(8,128)(2,1)S(1)}, bf16[80,2304]{1,0:T(8,128)(2,1)S(1)}, u32[]{:S(2)}, u32[]{:S(2)}) collective-permute-start(bf16[80,2304]{1,0:T(8,128)(2,1)S(1)} %add_convert_fusion.2), channel_id=1, source_target_pairs={{0,96},{8,104},{16,112},{24,120},{32,0},{40,8},{48,16},{56,24},{64... | collective-permute-start | bytes 1105928 | tf_op jit(solution)/shard_map/ppermute | solution.py:367
  171.0 2.3 %collective-permute-start.20 = (bf16[80,2304]{1,0:T(8,128)(2,1)S(1)}, bf16[80,2304]{1,0:T(8,128)(2,1)S(1)}, u32[]{:S(2)}, u32[]{:S(2)}) collective-permute-start(bf16[80,2304]{1,0:T(8,128)(2,1)S(1)} %add_convert_fusion.3), channel_id=1, source_target_pairs={{0,32},{8,40},{16,48},{24,56},{32,64},{40,72},{48,80},{56,88},{64,... | collective-permute-start | bytes 1105928 | tf_op jit(solution)/shard_map/ppermute | solution.py:367
  174.1 3.9 %collective-permute-start.33 = (bf16[40,2304]{1,0:T(8,128)(2,1)S(1)}, bf16[40,2304]{1,0:T(8,128)(2,1)S(1)}, u32[]{:S(2)}, u32[]{:S(2)}) collective-permute-start(bf16[40,2304]{1,0:T(8,128)(2,1)S(1)} %get-tuple-element.81), channel_id=1, source_target_pairs={{0,64},{8,72},{16,80},{24,88},{32,96},{40,104},{48,112},{56,120},{... | collective-permute-start | bytes 552968 | tf_op jit(solution)/shard_map/ppermute | solution.py:367
  179.5 3.1 %collective-permute-done.20.refs_2_ = bf16[80,2304]{1,0:T(8,128)(2,1)S(1)} collective-permute-done((bf16[80,2304]{1,0:T(8,128)(2,1)S(1)}, bf16[80,2304]{1,0:T(8,128)(2,1)S(1)}, u32[]{:S(2)}, u32[]{:S(2)}) %collective-permute-start.20) | collective-permute-done | bytes 368672 | tf_op jit(solution)/shard_map/ppermute | solution.py:367
  182.9 2.7 %collective-permute-start.24 = (bf16[40,2304]{1,0:T(8,128)(2,1)S(1)}, bf16[40,2304]{1,0:T(8,128)(2,1)S(1)}, u32[]{:S(2)}, u32[]{:S(2)}) collective-permute-start(bf16[40,2304]{1,0:T(8,128)(2,1)S(1)} %get-tuple-element.69), channel_id=1, source_target_pairs={{0,16},{8,24},{16,0},{24,8},{32,48},{40,56},{48,32},{56,40},{64,80... | collective-permute-start | bytes 552968 | tf_op jit(solution)/shard_map/ppermute | solution.py:367
  189.4 2.4 %collective-permute-done.25.refs_2_ = bf16[40,2304]{1,0:T(8,128)(2,1)S(1)} collective-permute-done((bf16[40,2304]{1,0:T(8,128)(2,1)S(1)}, bf16[40,2304]{1,0:T(8,128)(2,1)S(1)}, u32[]{:S(2)}, u32[]{:S(2)}) %collective-permute-start.25) | collective-permute-done | bytes 184352 | tf_op jit(solution)/shard_map/ppermute | solution.py:367
  191.8 2.1 collective-permute-done.26.refs_3_
  194.2 22.0 %all_to_all.25 = bf16[8,80,288]{2,1,0:T(8,128)(2,1)S(1)} all-to-all(bf16[8,80,288]{2,1,0:T(8,128)(2,1)S(1)} %finish.1), channel_id=1, replica_groups=mesh['wide'=16,'narrow'=8] {'narrow'}, dimensions={0} | all-to-all | bytes 737280 | tf_op jit(solution)/shard_map/all_to_all | solution.py:392
  (124 shorter events, 53.3 us)
Async XLA Ops:
  0.0 28.6 %all-to-all-start = ((bf16[8,288,360]{2,1,0:T(8,128)(2,1)}), bf16[8,288,360]{2,1,0:T(8,128)(2,1)S(1)}, u32[]{:S(2)}, u32[]{:S(2)}) async-start(bf16[8,288,360]{2,1,0:T(8,128)(2,1)} %bitcast.34), calls=%async_computation | async-start | bytes 3538944 | tf_op jit(solution)/shard_map/all_to_all | solution.py:392
  28.6 22.3 %all-to-all-start.1 = ((bf16[8,304,256]{2,1,0:T(8,128)(2,1)}), bf16[8,304,256]{2,1,0:T(8,128)(2,1)}, u32[]{:S(2)}, u32[]{:S(2)}) async-start(bf16[8,304,256]{2,1,0:T(8,128)(2,1)} %attend.1), calls=%async_computation.1 | async-start | bytes 2490368 | tf_op jit(solution)/shard_map/all_to_all | solution.py:392
  54.6 13.4 %all-to-all-start.2 = ((bf16[8,80,384]{2,1,0:T(8,128)(2,1)}), bf16[8,80,384]{2,1,0:T(8,128)(2,1)S(1)}, u32[]{:S(2)}, u32[]{:S(2)}) async-start(bf16[8,80,384]{2,1,0:T(8,128)(2,1)} %copy-done.1), calls=%async_computation.2 | async-start | bytes 983040 | tf_op jit(solution)/shard_map/all_to_all | solution.py:392
  68.0 47.1 %all-to-all-start.3 = ((bf16[8,576,360]{2,1,0:T(8,128)(2,1)}), bf16[8,576,360]{2,1,0:T(8,128)(2,1)}, u32[]{:S(2)}, u32[]{:S(2)}) async-start(bf16[8,576,360]{2,1,0:T(8,128)(2,1)} %pad_maximum_fusion), calls=%async_computation.3 | async-start | bytes 7077888 | tf_op jit(solution)/shard_map/all_to_all | solution.py:392
  73.7 10.0 %collective-permute-start.7 = (bf16[40,2304]{1,0:T(8,128)(2,1)S(1)}, bf16[40,2304]{1,0:T(8,128)(2,1)S(1)}, u32[]{:S(2)}, u32[]{:S(2)}) collective-permute-start(bf16[40,2304]{1,0:T(8,128)(2,1)S(1)} %get-tuple-element.87.refs_0_), channel_id=1, source_target_pairs={{0,64},{8,72},{16,80},{24,88},{32,96},{40,104},{48,112},{56,120},{... | collective-permute-start | bytes 552968 | tf_op jit(solution)/shard_map/ppermute | solution.py:367
  76.7 9.2 %collective-permute-start.8 = (bf16[40,2304]{1,0:T(8,128)(2,1)S(1)}, bf16[40,2304]{1,0:T(8,128)(2,1)S(1)}, u32[]{:S(2)}, u32[]{:S(2)}) collective-permute-start(bf16[40,2304]{1,0:T(8,128)(2,1)S(1)} %get-tuple-element.87.refs_0_), channel_id=1, source_target_pairs={{0,32},{8,40},{16,48},{24,56},{32,64},{40,72},{48,80},{56,88},{64,... | collective-permute-start | bytes 552968 | tf_op jit(solution)/shard_map/ppermute | solution.py:367
  77.1 8.8 %collective-permute-start.9 = (bf16[40,2304]{1,0:T(8,128)(2,1)S(1)}, bf16[40,2304]{1,0:T(8,128)(2,1)S(1)}, u32[]{:S(2)}, u32[]{:S(2)}) collective-permute-start(bf16[40,2304]{1,0:T(8,128)(2,1)S(1)} %get-tuple-element.87.refs_0_), channel_id=1, source_target_pairs={{0,96},{8,104},{16,112},{24,120},{32,0},{40,8},{48,16},{56,24},{64... | collective-permute-start | bytes 552968 | tf_op jit(solution)/shard_map/ppermute | solution.py:367
  79.4 10.5 %collective-permute-start = (bf16[40,2304]{1,0:T(8,128)(2,1)S(1)}, bf16[40,2304]{1,0:T(8,128)(2,1)S(1)}, u32[]{:S(2)}, u32[]{:S(2)}) collective-permute-start(bf16[40,2304]{1,0:T(8,128)(2,1)S(1)} %get-tuple-element.88.refs_0_), channel_id=1, source_target_pairs={{0,16},{8,24},{16,0},{24,8},{32,48},{40,56},{48,32},{56,40},{64,80... | collective-permute-start | bytes 552968 | tf_op jit(solution)/shard_map/ppermute | solution.py:367
  83.0 8.5 %collective-permute-start.1 = (bf16[40,2304]{1,0:T(8,128)(2,1)S(1)}, bf16[40,2304]{1,0:T(8,128)(2,1)S(1)}, u32[]{:S(2)}, u32[]{:S(2)}) collective-permute-start(bf16[40,2304]{1,0:T(8,128)(2,1)S(1)} %get-tuple-element.88.refs_0_), channel_id=1, source_target_pairs={{0,8},{8,16},{16,24},{24,0},{32,40},{40,48},{48,56},{56,32},{64,72... | collective-permute-start | bytes 552968 | tf_op jit(solution)/shard_map/ppermute | solution.py:367
  86.0 13.3 %collective-permute-start.10 = (bf16[80,2304]{1,0:T(8,128)(2,1)S(1)}, bf16[80,2304]{1,0:T(8,128)(2,1)}, u32[]{:S(2)}, u32[]{:S(2)}) collective-permute-start(bf16[80,2304]{1,0:T(8,128)(2,1)S(1)} %bitcast.22), channel_id=1, source_target_pairs={{0,8},{8,16},{16,24},{24,0},{32,40},{40,48},{48,56},{56,32},{64,72... | collective-permute-start | bytes 1105928 | tf_op jit(solution)/shard_map/ppermute | solution.py:367
  87.7 11.7 %collective-permute-start.13 = (bf16[80,2304]{1,0:T(8,128)(2,1)S(1)}, bf16[80,2304]{1,0:T(8,128)(2,1)}, u32[]{:S(2)}, u32[]{:S(2)}) collective-permute-start(bf16[80,2304]{1,0:T(8,128)(2,1)S(1)} %bitcast.25), channel_id=1, source_target_pairs={{0,24},{8,0},{16,8},{24,16},{32,56},{40,32},{48,40},{56,48},{64,88... | collective-permute-start | bytes 1105928 | tf_op jit(solution)/shard_map/ppermute | solution.py:367
  91.6 10.0 %collective-permute-start.3 = (bf16[80,2304]{1,0:T(8,128)(2,1)S(1)}, bf16[80,2304]{1,0:T(8,128)(2,1)}, u32[]{:S(2)}, u32[]{:S(2)}) collective-permute-start(bf16[80,2304]{1,0:T(8,128)(2,1)S(1)} %bitcast.28), channel_id=1, source_target_pairs={{0,32},{8,40},{16,48},{24,56},{32,64},{40,72},{48,80},{56,88},{64,... | collective-permute-start | bytes 1105928 | tf_op jit(solution)/shard_map/ppermute | solution.py:367
  91.7 12.1 %collective-permute-start.6 = (bf16[80,2304]{1,0:T(8,128)(2,1)S(1)}, bf16[80,2304]{1,0:T(8,128)(2,1)}, u32[]{:S(2)}, u32[]{:S(2)}) collective-permute-start(bf16[80,2304]{1,0:T(8,128)(2,1)S(1)} %bitcast.31), channel_id=1, source_target_pairs={{0,96},{8,104},{16,112},{24,120},{32,0},{40,8},{48,16},{56,24},{64... | collective-permute-start | bytes 1105928 | tf_op jit(solution)/shard_map/ppermute | solution.py:367
  94.4 11.5 %collective-permute-start.11 = (bf16[80,2304]{1,0:T(8,128)(2,1)S(1)}, bf16[80,2304]{1,0:T(8,128)(2,1)S(1)}, u32[]{:S(2)}, u32[]{:S(2)}) collective-permute-start(bf16[80,2304]{1,0:T(8,128)(2,1)S(1)} %bitcast.26), channel_id=1, source_target_pairs={{0,8},{8,16},{16,24},{24,0},{32,40},{40,48},{48,56},{56,32},{64,72... | collective-permute-start | bytes 1105928 | tf_op jit(solution)/shard_map/ppermute | solution.py:367
  99.5 10.9 %collective-permute-start.4 = (bf16[80,2304]{1,0:T(8,128)(2,1)S(1)}, bf16[80,2304]{1,0:T(8,128)(2,1)S(1)}, u32[]{:S(2)}, u32[]{:S(2)}) collective-permute-start(bf16[80,2304]{1,0:T(8,128)(2,1)S(1)} %bitcast.32), channel_id=1, source_target_pairs={{0,32},{8,40},{16,48},{24,56},{32,64},{40,72},{48,80},{56,88},{64,... | collective-permute-start | bytes 1105928 | tf_op jit(solution)/shard_map/ppermute | solution.py:367
  101.6 10.9 %collective-permute-start.5 = (bf16[80,2304]{1,0:T(8,128)(2,1)S(1)}, bf16[80,2304]{1,0:T(8,128)(2,1)S(1)}, u32[]{:S(2)}, u32[]{:S(2)}) collective-permute-start(bf16[80,2304]{1,0:T(8,128)(2,1)S(1)} %bitcast.29), channel_id=1, source_target_pairs={{0,96},{8,104},{16,112},{24,120},{32,0},{40,8},{48,16},{56,24},{64... | collective-permute-start | bytes 1105928 | tf_op jit(solution)/shard_map/ppermute | solution.py:367
  103.8 34.4 %collective-permute-start.16 = (bf16[80,2304]{1,0:T(8,128)(2,1)}, bf16[80,2304]{1,0:T(8,128)(2,1)S(1)}, u32[]{:S(2)}, u32[]{:S(2)}) collective-permute-start(bf16[80,2304]{1,0:T(8,128)(2,1)} %collective-permute-done.10.refs_8_), channel_id=1, source_target_pairs={{0,8},{8,16},{16,24},{24,0},{32,40},{40,48},{48,56},{56,32},{64,72... | collective-permute-start | bytes 1105928 | tf_op jit(solution)/shard_map/ppermute | solution.py:367
  106.6 31.6 %collective-permute-start.17 = (bf16[80,2304]{1,0:T(8,128)(2,1)}, bf16[80,2304]{1,0:T(8,128)(2,1)}, u32[]{:S(2)}, u32[]{:S(2)}) collective-permute-start(bf16[80,2304]{1,0:T(8,128)(2,1)} %collective-permute-done.13.refs_11_), channel_id=1, source_target_pairs={{0,24},{8,0},{16,8},{24,16},{32,56},{40,32},{48,40},{56,48},{64,88... | collective-permute-start | bytes 1105928 | tf_op jit(solution)/shard_map/ppermute | solution.py:367
  108.2 30.0 %collective-permute-start.14 = (bf16[80,2304]{1,0:T(8,128)(2,1)}, bf16[80,2304]{1,0:T(8,128)(2,1)}, u32[]{:S(2)}, u32[]{:S(2)}) collective-permute-start(bf16[80,2304]{1,0:T(8,128)(2,1)} %collective-permute-done.3.refs_2_), channel_id=1, source_target_pairs={{0,32},{8,40},{16,48},{24,56},{32,64},{40,72},{48,80},{56,88},{64,... | collective-permute-start | bytes 1105928 | tf_op jit(solution)/shard_map/ppermute | solution.py:367
  111.1 27.1 %collective-permute-start.15 = (bf16[80,2304]{1,0:T(8,128)(2,1)}, bf16[80,2304]{1,0:T(8,128)(2,1)}, u32[]{:S(2)}, u32[]{:S(2)}) collective-permute-start(bf16[80,2304]{1,0:T(8,128)(2,1)} %collective-permute-done.6.refs_5_), channel_id=1, source_target_pairs={{0,96},{8,104},{16,112},{24,120},{32,0},{40,8},{48,16},{56,24},{64... | collective-permute-start | bytes 1105928 | tf_op jit(solution)/shard_map/ppermute | solution.py:367
  146.5 10.8 %collective-permute-start.31 = (bf16[80,2304]{1,0:T(8,128)(2,1)S(1)}, bf16[80,2304]{1,0:T(8,128)(2,1)S(1)}, u32[]{:S(2)}, u32[]{:S(2)}) collective-permute-start(bf16[80,2304]{1,0:T(8,128)(2,1)S(1)} %get-tuple-element.79), channel_id=1, source_target_pairs={{0,24},{8,0},{16,8},{24,16},{32,56},{40,32},{48,40},{56,48},{64,88... | collective-permute-start | bytes 1105928 | tf_op jit(solution)/shard_map/ppermute | solution.py:367
  150.3 10.1 %collective-permute-start.28 = (bf16[80,2304]{1,0:T(8,128)(2,1)S(1)}, bf16[80,2304]{1,0:T(8,128)(2,1)S(1)}, u32[]{:S(2)}, u32[]{:S(2)}) collective-permute-start(bf16[80,2304]{1,0:T(8,128)(2,1)S(1)} %get-tuple-element.75), channel_id=1, source_target_pairs={{0,8},{8,16},{16,24},{24,0},{32,40},{40,48},{48,56},{56,32},{64,72... | collective-permute-start | bytes 1105928 | tf_op jit(solution)/shard_map/ppermute | solution.py:367
  150.3 16.1 %collective-permute-start.27 = (bf16[80,2304]{1,0:T(8,128)(2,1)S(1)}, bf16[80,2304]{1,0:T(8,128)(2,1)S(1)}, u32[]{:S(2)}, u32[]{:S(2)}) collective-permute-start(bf16[80,2304]{1,0:T(8,128)(2,1)S(1)} %get-tuple-element.73), channel_id=1, source_target_pairs={{0,24},{8,0},{16,8},{24,16},{32,56},{40,32},{48,40},{56,48},{64,88... | collective-permute-start | bytes 1105928 | tf_op jit(solution)/shard_map/ppermute | solution.py:367
  152.9 15.3 %collective-permute-start.30 = (bf16[80,2304]{1,0:T(8,128)(2,1)S(1)}, bf16[80,2304]{1,0:T(8,128)(2,1)S(1)}, u32[]{:S(2)}, u32[]{:S(2)}) collective-permute-start(bf16[80,2304]{1,0:T(8,128)(2,1)S(1)} %get-tuple-element.77), channel_id=1, source_target_pairs={{0,8},{8,16},{16,24},{24,0},{32,40},{40,48},{48,56},{56,32},{64,72... | collective-permute-start | bytes 1105928 | tf_op jit(solution)/shard_map/ppermute | solution.py:367
  153.0 10.3 %collective-permute-start.22 = (bf16[80,2304]{1,0:T(8,128)(2,1)S(1)}, bf16[80,2304]{1,0:T(8,128)(2,1)S(1)}, u32[]{:S(2)}, u32[]{:S(2)}) collective-permute-start(bf16[80,2304]{1,0:T(8,128)(2,1)S(1)} %get-tuple-element.67), channel_id=1, source_target_pairs={{0,96},{8,104},{16,112},{24,120},{32,0},{40,8},{48,16},{56,24},{64... | collective-permute-start | bytes 1105928 | tf_op jit(solution)/shard_map/ppermute | solution.py:367
  160.4 17.6 %collective-permute-start.18 = (bf16[80,2304]{1,0:T(8,128)(2,1)S(1)}, bf16[80,2304]{1,0:T(8,128)(2,1)S(1)}, u32[]{:S(2)}, u32[]{:S(2)}) collective-permute-start(bf16[80,2304]{1,0:T(8,128)(2,1)S(1)} %get-tuple-element.57), channel_id=1, source_target_pairs={{0,96},{8,104},{16,112},{24,120},{32,0},{40,8},{48,16},{56,24},{64... | collective-permute-start | bytes 1105928 | tf_op jit(solution)/shard_map/ppermute | solution.py:367
  166.4 12.4 %collective-permute-start.21 = (bf16[80,2304]{1,0:T(8,128)(2,1)S(1)}, bf16[80,2304]{1,0:T(8,128)(2,1)S(1)}, u32[]{:S(2)}, u32[]{:S(2)}) collective-permute-start(bf16[80,2304]{1,0:T(8,128)(2,1)S(1)} %get-tuple-element.65), channel_id=1, source_target_pairs={{0,32},{8,40},{16,48},{24,56},{32,64},{40,72},{48,80},{56,88},{64,... | collective-permute-start | bytes 1105928 | tf_op jit(solution)/shard_map/ppermute | solution.py:367
  168.3 11.2 %collective-permute-start.23 = (bf16[80,2304]{1,0:T(8,128)(2,1)S(1)}, bf16[80,2304]{1,0:T(8,128)(2,1)S(1)}, u32[]{:S(2)}, u32[]{:S(2)}) collective-permute-start(bf16[80,2304]{1,0:T(8,128)(2,1)S(1)} %add_convert_fusion.2), channel_id=1, source_target_pairs={{0,96},{8,104},{16,112},{24,120},{32,0},{40,8},{48,16},{56,24},{64... | collective-permute-start | bytes 1105928 | tf_op jit(solution)/shard_map/ppermute | solution.py:367
  171.0 11.6 %collective-permute-start.20 = (bf16[80,2304]{1,0:T(8,128)(2,1)S(1)}, bf16[80,2304]{1,0:T(8,128)(2,1)S(1)}, u32[]{:S(2)}, u32[]{:S(2)}) collective-permute-start(bf16[80,2304]{1,0:T(8,128)(2,1)S(1)} %add_convert_fusion.3), channel_id=1, source_target_pairs={{0,32},{8,40},{16,48},{24,56},{32,64},{40,72},{48,80},{56,88},{64,... | collective-permute-start | bytes 1105928 | tf_op jit(solution)/shard_map/ppermute | solution.py:367
  174.1 13.0 %collective-permute-start.33 = (bf16[40,2304]{1,0:T(8,128)(2,1)S(1)}, bf16[40,2304]{1,0:T(8,128)(2,1)S(1)}, u32[]{:S(2)}, u32[]{:S(2)}) collective-permute-start(bf16[40,2304]{1,0:T(8,128)(2,1)S(1)} %get-tuple-element.81), channel_id=1, source_target_pairs={{0,64},{8,72},{16,80},{24,88},{32,96},{40,104},{48,112},{56,120},{... | collective-permute-start | bytes 552968 | tf_op jit(solution)/shard_map/ppermute | solution.py:367
  178.0 11.2 %collective-permute-start.34 = (bf16[40,2304]{1,0:T(8,128)(2,1)S(1)}, bf16[40,2304]{1,0:T(8,128)(2,1)S(1)}, u32[]{:S(2)}, u32[]{:S(2)}) collective-permute-start(bf16[40,2304]{1,0:T(8,128)(2,1)S(1)} %get-tuple-element.82), channel_id=1, source_target_pairs={{0,96},{8,104},{16,112},{24,120},{32,0},{40,8},{48,16},{56,24},{64... | collective-permute-start | bytes 552968 | tf_op jit(solution)/shard_map/ppermute | solution.py:367
  178.8 10.6 %collective-permute-start.35 = (bf16[40,2304]{1,0:T(8,128)(2,1)S(1)}, bf16[40,2304]{1,0:T(8,128)(2,1)S(1)}, u32[]{:S(2)}, u32[]{:S(2)}) collective-permute-start(bf16[40,2304]{1,0:T(8,128)(2,1)S(1)} %get-tuple-element.83), channel_id=1, source_target_pairs={{0,32},{8,40},{16,48},{24,56},{32,64},{40,72},{48,80},{56,88},{64,... | collective-permute-start | bytes 552968 | tf_op jit(solution)/shard_map/ppermute | solution.py:367
  (30 other events, 223.0 us)
where the time goes:
time: 218 us; the launch traced here: 217 us
  starting transfers between devices  81.1 us (37%)
  Pallas kernels  46 us (21%)
  waiting for transfers between devices  42.8 us (20%)
  local copies, waits for them, and re-layouts  22.2 us (10%)
  blocking collectives  22 us (10%)
  other arithmetic  2.66 us (1%)
    ppermute x36, starting transfers between devices, shift(): return lax.ppermute(x, 'wide', ring_pairs(axis, step))  60.4 us
    pallas_call x2, Pallas kernels, expert(): pl.pallas_call(functools.partial(expert_kernel, count=count), in_specs=[a...  23.4 us
    all_to_all x4, waiting for transfers between devices, exchange(): return lax.all_to_all(x, 'narrow', 0, 0, tiled=True)  22 us
    all_to_all x1, blocking collectives, exchange(): return lax.all_to_all(x, 'narrow', 0, 0, tiled=True)  22 us
    ppermute x36, waiting for transfers between devices, shift(): return lax.ppermute(x, 'wide', ring_pairs(axis, step))  20.8 us
    all_to_all x4, starting transfers between devices, exchange(): return lax.all_to_all(x, 'narrow', 0, 0, tiled=True)  20.7 us
    pallas_call x1, Pallas kernels, attend(): pl.pallas_call(functools.partial(attend_kernel, share=share), grid_spec=p...  18.1 us
    unnamed x46, local copies, waits for them, and re-layouts  14.2 us
  transfers between devices with their start and end apart: 40, of which 19 were waited for; matrix products, arithmetic and copies ran while one was open for 5% of the time, Pallas kernels for 16%

commit v1 on v0

--- a/solution.py
+++ b/solution.py
@@ -220,8 +220,8 @@
 
 
 def expert_kernel(*refs, count):
-    blocks, gate_up_ref, down_ref = refs[:count], refs[count], refs[count + 1]
-    outs, (x_sc, weight_sc, both_sc, y_sc, sems) = refs[count + 2 : 2 * count + 2], refs[2 * count + 2 :]
+    blocks, gate_up_hbm, down_hbm = refs[:count], refs[count], refs[count + 1]
+    outs, (x_sc, gate_up_ref, down_ref, weight_sc, both_sc, y_sc, sems) = refs[count + 2 : 2 * count + 2], refs[2 * count + 2 :]
     rows = blocks[0].shape[0]
     groups, _, units = gate_up_ref.shape
     share = x_sc.shape[1] // groups
@@ -229,9 +229,12 @@
     tile = 256
     loads = [pltpu.make_async_copy(b, x_sc.at[pl.ds(i * rows, rows)], sems.at[i]) for i, b in enumerate(blocks)]
     stores = [pltpu.make_async_copy(y_sc.at[pl.ds(i * rows, rows)], o, sems.at[count + i]) for i, o in enumerate(outs)]
-    for load in loads:
+    parts = [pltpu.make_async_copy(gate_up_hbm.at[g], gate_up_ref.at[g], sems.at[2 * count + g]) for g in range(groups)]
+    down_load = pltpu.make_async_copy(down_hbm, down_ref, sems.at[2 * count + groups])
+    for load in (*parts, *loads, down_load):
         load.start()
     for g in range(groups):
+        parts[g].wait()
         weight_sc[g * share : g * share + share, :units] = gate_up_ref[g, :share]
         weight_sc[g * share : g * share + share, half : half + units] = gate_up_ref[g, share:]
     for load in loads:
@@ -244,6 +247,7 @@
 
     gate, up = both_sc[:, :units], both_sc[:, half : half + units]
     act = (gate / (1.0 + jnp.exp(-gate)) * up).astype(BF16)
+    down_load.wait()
 
     @pl.loop(0, down_ref.shape[0] // tile)
     def _(j):
@@ -262,26 +266,27 @@
     count = len(blocks)
     total = count * rows
     packed = 2 * (-(-units // 128) * 128)
-    held = pl.BlockSpec(memory_space=pltpu.VMEM)
-    anywhere = pl.BlockSpec(memory_space=pl.ANY)
+    anywhere = pl.BlockSpec(memory_space=pltpu.HBM)
     return pl.pallas_call(
         functools.partial(expert_kernel, count=count),
-        in_specs=[anywhere] * count + [held] * 2,
+        in_specs=[anywhere] * (count + 2),
         out_specs=[anywhere] * count,
         out_shape=[jax.ShapeDtypeStruct((rows, width), BF16)] * count,
         scratch_shapes=[
             pltpu.VMEM((total, width), BF16),
+            pltpu.VMEM(gate_up.shape, BF16),
+            pltpu.VMEM(down.shape, BF16),
             pltpu.VMEM((width, packed), BF16),
             pltpu.VMEM((total, packed), F32),
             pltpu.VMEM((total, width), BF16),
-            pltpu.SemaphoreType.DMA((2 * count,)),
+            pltpu.SemaphoreType.DMA((2 * count + gate_up.shape[0] + 1,)),
         ],
         cost_estimate=pl.CostEstimate(
             flops=6 * total * width * units,
             bytes_accessed=4 * total * width + 6 * width * units,
             transcendentals=total * units,
         ),
-        compiler_params=pltpu.CompilerParams(vmem_limit_bytes=26 << 20),
+        compiler_params=pltpu.CompilerParams(vmem_limit_bytes=60 << 20),
         name="expert",
     )(*blocks, gate_up, down)
 
@@ -419,16 +424,17 @@
     def around(block, axis):
         return [block, *(shift(block, axis, step) for step in STEPS)]
 
-    near, far = [], []
+    early, late = [], []
     for first, second, block in (("z", "y", rows[:half]), ("y", "z", rows[half:])):
         low, high = stack(around(block, first))
         before_low, after_high = shift(low, second, 1), shift(high, second, -1)
         before_high, after_low = shift(high, second, 1), shift(low, second, -1)
-        near += [low, high, before_low, before_high, after_low, after_high]
-        far += [shift(before_low, second, 1), shift(after_high, second, -1)]
-    near = list(expert(near, later, down_all))
-    near[0], *far = lax.optimization_barrier((near[0], *far))
-    far = expert(far, later, down_all)
+        far_low, far_high = shift(before_low, second, 1), shift(after_high, second, -1)
+        early += [before_low, after_high, far_low, far_high]
+        late += [low, high, after_low, before_high]
+    early = list(expert(early, later, down_all))
+    early[0], *late = lax.optimization_barrier((early[0], *late))
+    late = expert(late, later, down_all)
 
     def back(blocks, axis):
         return [blocks[0], *(shift(block, axis, -step) for block, step in zip(blocks[1:], STEPS))]
@@ -438,12 +444,13 @@
 
     four = []
     for color, second in enumerate(("y", "z")):
-        low, high, before_low, before_high, after_low, after_high = near[6 * color : 6 * color + 6]
-        got_low = shift(before_low, second, -1)
-        got_high = shift(after_high, second, 1)
-        via_low, via_high = shift(far[2 * color], second, 1), shift(far[2 * color + 1], second, -1)
-        more_low, more_high = shift(joined(after_low, via_low), second, 1), shift(joined(before_high, via_high), second, -1)
-        four.append(add_blocks([low, got_low, more_low], [high, got_high, more_high]))
+        before_low, after_high, far_low, far_high = early[4 * color : 4 * color + 4]
+        low, high, after_low, before_high = late[4 * color : 4 * color + 4]
+        got = []
+        for block, step in zip((far_low, far_high, before_low, after_high), (1, -1, -1, 1)):
+            got.append(shift(block, second, step))
+        more_low, more_high = shift(joined(after_low, got[0]), second, 1), shift(joined(before_high, got[1]), second, -1)
+        four.append(add_blocks([low, got[2], more_low], [high, got[3], more_high]))
     out_rows = finish([*back(four[0], "z"), *back(four[1], "y")], narrow_count)
     out_rows = exchange(out_rows)
     return mix(out_rows.reshape(expert_count * CAP, share), slots.T, route_weight.T, hidden).T

time: 218 us -> 208 us (0.954)
  local copies, waits for them, and re-layouts: 22.2 us -> 9.61 us
  starting transfers between devices: 81.1 us -> 72 us
  waiting for transfers between devices: 42.8 us -> 50.4 us
  blocking collectives: 22 us -> 25.3 us
    unnamed x46, local copies, waits for them, and re-layouts: 14.2 us -> 1.65 us
    ppermute x36, waiting for transfers between devices: 20.8 us -> 30.4 us  [shift(): return lax.ppermute(x, 'wide', ring_pairs(axis, step))]
    ppermute x36, starting transfers between devices: 60.4 us -> 51.9 us  [shift(): return lax.ppermute(x, 'wide', ring_pairs(axis, step))]
    all_to_all x1, blocking collectives: 22 us -> 25.3 us  [exchange(): return lax.all_to_all(x, 'narrow', 0, 0, tiled=True)]
  transfers between devices with their start and end apart: 40 -> 40, of which waited for: 19 -> 16; matrix products, arithmetic and copies ran while one was open for 5% -> 6% of each run, Pallas kernels for 16% -> 20%
where the time goes in v1:
time: 208 us; the launch traced here: 207 us
  starting transfers between devices  72 us (35%)
  waiting for transfers between devices  50.4 us (24%)
  Pallas kernels  44.3 us (21%)
  blocking collectives  25.3 us (12%)
  local copies, waits for them, and re-layouts  9.61 us (5%)
  other arithmetic  4.6 us (2%)
    ppermute x36, starting transfers between devices, shift(): return lax.ppermute(x, 'wide', ring_pairs(axis, step))  51.9 us
    ppermute x36, waiting for transfers between devices, shift(): return lax.ppermute(x, 'wide', ring_pairs(axis, step))  30.4 us
    all_to_all x1, blocking collectives, exchange(): return lax.all_to_all(x, 'narrow', 0, 0, tiled=True)  25.3 us
    pallas_call x2, Pallas kernels, expert(): pl.pallas_call(functools.partial(expert_kernel, count=count), in_specs=[a...  22.2 us
    all_to_all x4, starting transfers between devices, exchange(): return lax.all_to_all(x, 'narrow', 0, 0, tiled=True)  20.1 us
    all_to_all x4, waiting for transfers between devices, exchange(): return lax.all_to_all(x, 'narrow', 0, 0, tiled=True)  20 us
    pallas_call x1, Pallas kernels, attend(): pl.pallas_call(functools.partial(attend_kernel, share=share), grid_spec=p...  18.1 us
    optimization_barrier x1, local copies, waits for them, and re-layouts, local(): lax.optimization_barrier((sums, down_all, w_gate_up))  4.21 us
  transfers between devices with their start and end apart: 40, of which 16 were waited for; matrix products, arithmetic and copies ran while one was open for 6% of the time, Pallas kernels for 20%

profile of v1, /device:TPU:1, one launch (start us, length us, event | category | flops | bytes accessed | tf_op | source)
XLA Modules:
  0.0 206.9 jit_solution(15598313075291187509)
XLA Ops:
  0.0 5.9 %all-to-all-start = ((bf16[8,288,360]{2,1,0:T(8,128)(2,1)}), bf16[8,288,360]{2,1,0:T(8,128)(2,1)S(1)}, u32[]{:S(2)}, u32[]{:S(2)}) async-start(bf16[8,288,360]{2,1,0:T(8,128)(2,1)} %bitcast.32), calls=%async_computation | async-start | bytes 3538944 | tf_op jit(solution)/shard_map/all_to_all | solution.py:397
  5.9 18.1 %attend.1 = bf16[8,304,256]{2,1,0:T(8,128)(2,1)} custom-call(s32[2,32]{1,0:T(2,128)} %table.1, s32[2]{0:T(128)} %length.1, s32[1]{0:T(128)} %bitcast.place, bf16[2,128,2304]{2,1,0:T(8,128)(2,1)} %q_ref.1, bf16[2,4,2,128,2304]{4,3,2,1,0:T(8,128)(2,1)} %v_ref.1, bf16[2,4,2,128,2304]{4,3,2,1,0:T(8,128)(2,1)} %v_ref.1, bf16[2,2,16,2304]{3,2,1,0:T(8,128)(2,1)} %nv_ref.1, ...), custom_call_target="tpu_custom_call" | custom-call | flops 1245708288 | bytes 10616832 | tf_op jit(solution)/shard_map/attend/pallas_call | solution.py:100
  24.0 4.6 %all-to-all-done = bf16[8,288,360]{2,1,0:T(8,128)(2,1)S(1)} async-done(((bf16[8,288,360]{2,1,0:T(8,128)(2,1)}), bf16[8,288,360]{2,1,0:T(8,128)(2,1)S(1)}, u32[]{:S(2)}, u32[]{:S(2)}) %all-to-all-start) | async-done | bytes 1658912 | tf_op jit(solution)/shard_map/all_to_all | solution.py:397
  29.9 4.4 %all-to-all-start.1 = ((bf16[8,304,256]{2,1,0:T(8,128)(2,1)}), bf16[8,304,256]{2,1,0:T(8,128)(2,1)S(1)}, u32[]{:S(2)}, u32[]{:S(2)}) async-start(bf16[8,304,256]{2,1,0:T(8,128)(2,1)} %attend.1), calls=%async_computation.1 | async-start | bytes 2490368 | tf_op jit(solution)/shard_map/all_to_all | solution.py:397
  36.4 4.2 %copy.15 = bf16[8,288,2,360]{3,1,0,2:T(8,128)(2,1)} copy(bf16[8,288,2,360]{3,2,1,0:T(2,128)(2,1)} %param.20) | data formatting | bytes 6635520 | tf_op jit(solution)/shard_map/optimization_barrier | solution.py:402
  40.6 10.9 %all-to-all-done.1.recv_ref = bf16[8,304,256]{2,1,0:T(8,128)(2,1)S(1)} async-done(((bf16[8,304,256]{2,1,0:T(8,128)(2,1)}), bf16[8,304,256]{2,1,0:T(8,128)(2,1)S(1)}, u32[]{:S(2)}, u32[]{:S(2)}) %all-to-all-start.1) | async-done | bytes 1245216 | tf_op jit(solution)/shard_map/all_to_all | solution.py:397
  53.1 4.3 %all-to-all-start.2 = ((bf16[8,80,384]{2,1,0:T(8,128)(2,1)}), bf16[8,80,384]{2,1,0:T(8,128)(2,1)S(1)}, u32[]{:S(2)}, u32[]{:S(2)}) async-start(bf16[8,80,384]{2,1,0:T(8,128)(2,1)} %get-tuple-element.51), calls=%async_computation.2 | async-start | bytes 983040 | tf_op jit(solution)/shard_map/all_to_all | solution.py:397
  57.5 2.4 %slice_bitcast_fusion.1 = (bf16[8,288,360]{2,1,0:T(8,128)(2,1)S(1)}, bf16[8,288,360]{2,1,0:T(8,128)(2,1)S(1)}) fusion(bf16[8,288,2,360]{3,1,0,2:T(8,128)(2,1)} %copy.15), kind=kLoop, calls=%fused_computation.2 | loop fusion | bytes 6635520 | tf_op jit(solution)/shard_map/squeeze | solution.py:403
  62.0 4.5 %all-to-all-done.2.recv_ref = bf16[8,80,384]{2,1,0:T(8,128)(2,1)S(1)} async-done(((bf16[8,80,384]{2,1,0:T(8,128)(2,1)}), bf16[8,80,384]{2,1,0:T(8,128)(2,1)S(1)}, u32[]{:S(2)}, u32[]{:S(2)}) %all-to-all-start.2) | async-done | bytes 491552 | tf_op jit(solution)/shard_map/all_to_all | solution.py:397
  66.5 5.3 %all-to-all-start.3 = ((bf16[8,576,360]{2,1,0:T(8,128)(2,1)}), bf16[8,576,360]{2,1,0:T(8,128)(2,1)}, u32[]{:S(2)}, u32[]{:S(2)}) async-start(bf16[8,576,360]{2,1,0:T(8,128)(2,1)} %pad_maximum_fusion), calls=%async_computation.3 | async-start | bytes 7077888 | tf_op jit(solution)/shard_map/all_to_all | solution.py:397
  72.2 3.8 %collective-permute-start.2 = (bf16[40,2304]{1,0:T(8,128)(2,1)S(1)}, bf16[40,2304]{1,0:T(8,128)(2,1)S(1)}, u32[]{:S(2)}, u32[]{:S(2)}) collective-permute-start(bf16[40,2304]{1,0:T(8,128)(2,1)S(1)} %get-tuple-element.96.refs_0_), channel_id=1, source_target_pairs={{0,24},{8,0},{16,8},{24,16},{32,56},{40,32},{48,40},{56,48},{64,88... | collective-permute-start | bytes 552968 | tf_op jit(solution)/shard_map/ppermute | solution.py:372
  77.4 2.7 %collective-permute-start.9 = (bf16[40,2304]{1,0:T(8,128)(2,1)S(1)}, bf16[40,2304]{1,0:T(8,128)(2,1)S(1)}, u32[]{:S(2)}, u32[]{:S(2)}) collective-permute-start(bf16[40,2304]{1,0:T(8,128)(2,1)S(1)} %get-tuple-element.95.refs_0_), channel_id=1, source_target_pairs={{0,96},{8,104},{16,112},{24,120},{32,0},{40,8},{48,16},{56,24},{64... | collective-permute-start | bytes 552968 | tf_op jit(solution)/shard_map/ppermute | solution.py:372
  80.1 2.6 %collective-permute-start.7 = (bf16[40,2304]{1,0:T(8,128)(2,1)S(1)}, bf16[40,2304]{1,0:T(8,128)(2,1)S(1)}, u32[]{:S(2)}, u32[]{:S(2)}) collective-permute-start(bf16[40,2304]{1,0:T(8,128)(2,1)S(1)} %get-tuple-element.95.refs_0_), channel_id=1, source_target_pairs={{0,64},{8,72},{16,80},{24,88},{32,96},{40,104},{48,112},{56,120},{... | collective-permute-start | bytes 552968 | tf_op jit(solution)/shard_map/ppermute | solution.py:372
  82.7 4.3 %collective-permute-done.1.refs_2_ = bf16[40,2304]{1,0:T(8,128)(2,1)S(1)} collective-permute-done((bf16[40,2304]{1,0:T(8,128)(2,1)S(1)}, bf16[40,2304]{1,0:T(8,128)(2,1)S(1)}, u32[]{:S(2)}, u32[]{:S(2)}) %collective-permute-start.1) | collective-permute-done | bytes 184352 | tf_op jit(solution)/shard_map/ppermute | solution.py:372
  87.1 2.8 %collective-permute-start.4 = (bf16[80,2304]{1,0:T(8,128)(2,1)S(1)}, bf16[80,2304]{1,0:T(8,128)(2,1)S(1)}, u32[]{:S(2)}, u32[]{:S(2)}) collective-permute-start(bf16[80,2304]{1,0:T(8,128)(2,1)S(1)} %bitcast.23), channel_id=1, source_target_pairs={{0,96},{8,104},{16,112},{24,120},{32,0},{40,8},{48,16},{56,24},{64... | collective-permute-start | bytes 1105928 | tf_op jit(solution)/shard_map/ppermute | solution.py:372
  90.0 4.4 %collective-permute-start.11 = (bf16[80,2304]{1,0:T(8,128)(2,1)S(1)}, bf16[80,2304]{1,0:T(8,128)(2,1)S(1)}, u32[]{:S(2)}, u32[]{:S(2)}) collective-permute-start(bf16[80,2304]{1,0:T(8,128)(2,1)S(1)} %bitcast.29), channel_id=1, source_target_pairs={{0,24},{8,0},{16,8},{24,16},{32,56},{40,32},{48,40},{56,48},{64,88... | collective-permute-start | bytes 1105928 | tf_op jit(solution)/shard_map/ppermute | solution.py:372
  94.3 4.3 %collective-permute-done.4.refs_1_ = bf16[80,2304]{1,0:T(8,128)(2,1)S(1)} collective-permute-done((bf16[80,2304]{1,0:T(8,128)(2,1)S(1)}, bf16[80,2304]{1,0:T(8,128)(2,1)S(1)}, u32[]{:S(2)}, u32[]{:S(2)}) %collective-permute-start.4) | collective-permute-done | bytes 368672 | tf_op jit(solution)/shard_map/ppermute | solution.py:372
  98.6 3.5 %collective-permute-start.6 = (bf16[80,2304]{1,0:T(8,128)(2,1)S(1)}, bf16[80,2304]{1,0:T(8,128)(2,1)S(1)}, u32[]{:S(2)}, u32[]{:S(2)}) collective-permute-start(bf16[80,2304]{1,0:T(8,128)(2,1)S(1)} %collective-permute-done.4.refs_1_), channel_id=1, source_target_pairs={{0,96},{8,104},{16,112},{24,120},{32,0},{40,8},{48,16},{56,24},{64... | collective-permute-start | bytes 1105928 | tf_op jit(solution)/shard_map/ppermute | solution.py:372
  102.2 4.1 %collective-permute-start.13 = (bf16[80,2304]{1,0:T(8,128)(2,1)S(1)}, bf16[80,2304]{1,0:T(8,128)(2,1)S(1)}, u32[]{:S(2)}, u32[]{:S(2)}) collective-permute-start(bf16[80,2304]{1,0:T(8,128)(2,1)S(1)} %collective-permute-done.11.refs_5_), channel_id=1, source_target_pairs={{0,24},{8,0},{16,8},{24,16},{32,56},{40,32},{48,40},{56,48},{64,88... | collective-permute-start | bytes 1105928 | tf_op jit(solution)/shard_map/ppermute | solution.py:372
  106.4 2.6 %collective-permute-done.6.refs_3_ = bf16[80,2304]{1,0:T(8,128)(2,1)S(1)} collective-permute-done((bf16[80,2304]{1,0:T(8,128)(2,1)S(1)}, bf16[80,2304]{1,0:T(8,128)(2,1)S(1)}, u32[]{:S(2)}, u32[]{:S(2)}) %collective-permute-start.6) | collective-permute-done | bytes 368672 | tf_op jit(solution)/shard_map/ppermute | solution.py:372
  109.0 3.5 %collective-permute-start.14 = (bf16[80,2304]{1,0:T(8,128)(2,1)S(1)}, bf16[80,2304]{1,0:T(8,128)(2,1)}, u32[]{:S(2)}, u32[]{:S(2)}) collective-permute-start(bf16[80,2304]{1,0:T(8,128)(2,1)S(1)} %bitcast.21), channel_id=1, source_target_pairs={{0,96},{8,104},{16,112},{24,120},{32,0},{40,8},{48,16},{56,24},{64... | collective-permute-start | bytes 1105928 | tf_op jit(solution)/shard_map/ppermute | solution.py:372
  113.6 3.8 %collective-permute-start.16 = (bf16[80,2304]{1,0:T(8,128)(2,1)S(1)}, bf16[80,2304]{1,0:T(8,128)(2,1)}, u32[]{:S(2)}, u32[]{:S(2)}) collective-permute-start(bf16[80,2304]{1,0:T(8,128)(2,1)S(1)} %bitcast.27), channel_id=1, source_target_pairs={{0,24},{8,0},{16,8},{24,16},{32,56},{40,32},{48,40},{56,48},{64,88... | collective-permute-start | bytes 1105928 | tf_op jit(solution)/shard_map/ppermute | solution.py:372
  117.4 11.1 %expert.2 = (bf16[80,2304]{1,0:T(8,128)(2,1)}, bf16[80,2304]{1,0:T(8,128)(2,1)}, bf16[80,2304]{1,0:T(8,128)(2,1)}, bf16[80,2304]{1,0:T(8,128)(2,1)}, bf16[80,230...) custom-call(bf16[80,2304]{1,0:T(8,128)(2,1)} %copy-done.16, ...), custom_call_target="tpu_custom_call" | custom-call | flops 3185049600 | bytes 10874880 | tf_op jit(solution)/shard_map/expert/pallas_call | solution.py:270
  128.7 2.7 %collective-permute-start.18 = (bf16[80,2304]{1,0:T(8,128)(2,1)}, bf16[80,2304]{1,0:T(8,128)(2,1)S(1)}, u32[]{:S(2)}, u32[]{:S(2)}) collective-permute-start(bf16[80,2304]{1,0:T(8,128)(2,1)} %get-tuple-element.69), channel_id=1, source_target_pairs={{0,96},{8,104},{16,112},{24,120},{32,0},{40,8},{48,16},{56,24},{64... | collective-permute-start | bytes 1105928 | tf_op jit(solution)/shard_map/ppermute | solution.py:372
  131.4 2.7 %collective-permute-start.22 = (bf16[80,2304]{1,0:T(8,128)(2,1)}, bf16[80,2304]{1,0:T(8,128)(2,1)S(1)}, u32[]{:S(2)}, u32[]{:S(2)}) collective-permute-start(bf16[80,2304]{1,0:T(8,128)(2,1)} %get-tuple-element.75), channel_id=1, source_target_pairs={{0,96},{8,104},{16,112},{24,120},{32,0},{40,8},{48,16},{56,24},{64... | collective-permute-start | bytes 1105928 | tf_op jit(solution)/shard_map/ppermute | solution.py:372
  135.5 11.1 %expert.3 = (bf16[80,2304]{1,0:T(8,128)(2,1)}, bf16[80,2304]{1,0:T(8,128)(2,1)}, bf16[80,2304]{1,0:T(8,128)(2,1)}, bf16[80,2304]{1,0:T(8,128)(2,1)}, bf16[80,230...) custom-call(bf16[80,2304]{1,0:T(8,128)(2,1)} %bitcast.22, ...), custom_call_target="tpu_custom_call" | custom-call | flops 3185049600 | bytes 10874880 | tf_op jit(solution)/shard_map/expert/pallas_call | solution.py:270
  147.9 2.6 %collective-permute-start.31 = (bf16[80,2304]{1,0:T(8,128)(2,1)}, bf16[80,2304]{1,0:T(8,128)(2,1)S(1)}, u32[]{:S(2)}, u32[]{:S(2)}) collective-permute-start(bf16[80,2304]{1,0:T(8,128)(2,1)} %get-tuple-element.87), channel_id=1, source_target_pairs={{0,24},{8,0},{16,8},{24,16},{32,56},{40,32},{48,40},{56,48},{64,88... | collective-permute-start | bytes 1105928 | tf_op jit(solution)/shard_map/ppermute | solution.py:372
  151.7 2.8 %collective-permute-done.28 = bf16[80,2304]{1,0:T(8,128)(2,1)S(1)} collective-permute-done((bf16[80,2304]{1,0:T(8,128)(2,1)}, bf16[80,2304]{1,0:T(8,128)(2,1)S(1)}, u32[]{:S(2)}, u32[]{:S(2)}) %collective-permute-start.28) | collective-permute-done | bytes 368672 | tf_op jit(solution)/shard_map/ppermute | solution.py:372
  157.7 4.4 %collective-permute-done.20.refs_2_ = bf16[80,2304]{1,0:T(8,128)(2,1)S(1)} collective-permute-done((bf16[80,2304]{1,0:T(8,128)(2,1)S(1)}, bf16[80,2304]{1,0:T(8,128)(2,1)S(1)}, u32[]{:S(2)}, u32[]{:S(2)}) %collective-permute-start.20) | collective-permute-done | bytes 368672 | tf_op jit(solution)/shard_map/ppermute | solution.py:372
  166.3 4.7 %collective-permute-done.29.refs_2_ = bf16[80,2304]{1,0:T(8,128)(2,1)S(1)} collective-permute-done((bf16[80,2304]{1,0:T(8,128)(2,1)S(1)}, bf16[80,2304]{1,0:T(8,128)(2,1)S(1)}, u32[]{:S(2)}, u32[]{:S(2)}) %collective-permute-start.29) | collective-permute-done | bytes 368672 | tf_op jit(solution)/shard_map/ppermute | solution.py:372
  177.5 2.7 %collective-permute-done.35.refs_7_ = bf16[40,2304]{1,0:T(8,128)(2,1)S(1)} collective-permute-done((bf16[40,2304]{1,0:T(8,128)(2,1)S(1)}, bf16[40,2304]{1,0:T(8,128)(2,1)S(1)}, u32[]{:S(2)}, u32[]{:S(2)}) %collective-permute-start.35) | collective-permute-done | bytes 184352 | tf_op jit(solution)/shard_map/ppermute | solution.py:372
  180.5 25.3 %all_to_all.25 = bf16[8,80,288]{2,1,0:T(8,128)(2,1)S(1)} all-to-all(bf16[8,80,288]{2,1,0:T(8,128)(2,1)S(1)} %finish.1), channel_id=1, replica_groups=mesh['wide'=16,'narrow'=8] {'narrow'}, dimensions={0} | all-to-all | bytes 737280 | tf_op jit(solution)/shard_map/all_to_all | solution.py:397
  (124 shorter events, 29.1 us)
Async XLA Ops:
  0.0 28.6 %all-to-all-start = ((bf16[8,288,360]{2,1,0:T(8,128)(2,1)}), bf16[8,288,360]{2,1,0:T(8,128)(2,1)S(1)}, u32[]{:S(2)}, u32[]{:S(2)}) async-start(bf16[8,288,360]{2,1,0:T(8,128)(2,1)} %bitcast.32), calls=%async_computation | async-start | bytes 3538944 | tf_op jit(solution)/shard_map/all_to_all | solution.py:397
  29.9 21.5 %all-to-all-start.1 = ((bf16[8,304,256]{2,1,0:T(8,128)(2,1)}), bf16[8,304,256]{2,1,0:T(8,128)(2,1)S(1)}, u32[]{:S(2)}, u32[]{:S(2)}) async-start(bf16[8,304,256]{2,1,0:T(8,128)(2,1)} %attend.1), calls=%async_computation.1 | async-start | bytes 2490368 | tf_op jit(solution)/shard_map/all_to_all | solution.py:397
  53.1 13.4 %all-to-all-start.2 = ((bf16[8,80,384]{2,1,0:T(8,128)(2,1)}), bf16[8,80,384]{2,1,0:T(8,128)(2,1)S(1)}, u32[]{:S(2)}, u32[]{:S(2)}) async-start(bf16[8,80,384]{2,1,0:T(8,128)(2,1)} %get-tuple-element.51), calls=%async_computation.2 | async-start | bytes 983040 | tf_op jit(solution)/shard_map/all_to_all | solution.py:397
  66.5 50.9 %all-to-all-start.3 = ((bf16[8,576,360]{2,1,0:T(8,128)(2,1)}), bf16[8,576,360]{2,1,0:T(8,128)(2,1)}, u32[]{:S(2)}, u32[]{:S(2)}) async-start(bf16[8,576,360]{2,1,0:T(8,128)(2,1)} %pad_maximum_fusion), calls=%async_computation.3 | async-start | bytes 7077888 | tf_op jit(solution)/shard_map/all_to_all | solution.py:397
  76.0 10.9 %collective-permute-start.1 = (bf16[40,2304]{1,0:T(8,128)(2,1)S(1)}, bf16[40,2304]{1,0:T(8,128)(2,1)S(1)}, u32[]{:S(2)}, u32[]{:S(2)}) collective-permute-start(bf16[40,2304]{1,0:T(8,128)(2,1)S(1)} %get-tuple-element.96.refs_0_), channel_id=1, source_target_pairs={{0,8},{8,16},{16,24},{24,0},{32,40},{40,48},{48,56},{56,32},{64,72... | collective-permute-start | bytes 552968 | tf_op jit(solution)/shard_map/ppermute | solution.py:372
  76.1 10.9 %collective-permute-start = (bf16[40,2304]{1,0:T(8,128)(2,1)S(1)}, bf16[40,2304]{1,0:T(8,128)(2,1)S(1)}, u32[]{:S(2)}, u32[]{:S(2)}) collective-permute-start(bf16[40,2304]{1,0:T(8,128)(2,1)S(1)} %get-tuple-element.96.refs_0_), channel_id=1, source_target_pairs={{0,16},{8,24},{16,0},{24,8},{32,48},{40,56},{48,32},{56,40},{64,80... | collective-permute-start | bytes 552968 | tf_op jit(solution)/shard_map/ppermute | solution.py:372
  77.4 12.5 %collective-permute-start.9 = (bf16[40,2304]{1,0:T(8,128)(2,1)S(1)}, bf16[40,2304]{1,0:T(8,128)(2,1)S(1)}, u32[]{:S(2)}, u32[]{:S(2)}) collective-permute-start(bf16[40,2304]{1,0:T(8,128)(2,1)S(1)} %get-tuple-element.95.refs_0_), channel_id=1, source_target_pairs={{0,96},{8,104},{16,112},{24,120},{32,0},{40,8},{48,16},{56,24},{64... | collective-permute-start | bytes 552968 | tf_op jit(solution)/shard_map/ppermute | solution.py:372
  80.1 9.8 %collective-permute-start.8 = (bf16[40,2304]{1,0:T(8,128)(2,1)S(1)}, bf16[40,2304]{1,0:T(8,128)(2,1)S(1)}, u32[]{:S(2)}, u32[]{:S(2)}) collective-permute-start(bf16[40,2304]{1,0:T(8,128)(2,1)S(1)} %get-tuple-element.95.refs_0_), channel_id=1, source_target_pairs={{0,32},{8,40},{16,48},{24,56},{32,64},{40,72},{48,80},{56,88},{64,... | collective-permute-start | bytes 552968 | tf_op jit(solution)/shard_map/ppermute | solution.py:372
  80.1 9.8 %collective-permute-start.7 = (bf16[40,2304]{1,0:T(8,128)(2,1)S(1)}, bf16[40,2304]{1,0:T(8,128)(2,1)S(1)}, u32[]{:S(2)}, u32[]{:S(2)}) collective-permute-start(bf16[40,2304]{1,0:T(8,128)(2,1)S(1)} %get-tuple-element.95.refs_0_), channel_id=1, source_target_pairs={{0,64},{8,72},{16,80},{24,88},{32,96},{40,104},{48,112},{56,120},{... | collective-permute-start | bytes 552968 | tf_op jit(solution)/shard_map/ppermute | solution.py:372
  87.1 11.6 %collective-permute-start.4 = (bf16[80,2304]{1,0:T(8,128)(2,1)S(1)}, bf16[80,2304]{1,0:T(8,128)(2,1)S(1)}, u32[]{:S(2)}, u32[]{:S(2)}) collective-permute-start(bf16[80,2304]{1,0:T(8,128)(2,1)S(1)} %bitcast.23), channel_id=1, source_target_pairs={{0,96},{8,104},{16,112},{24,120},{32,0},{40,8},{48,16},{56,24},{64... | collective-permute-start | bytes 1105928 | tf_op jit(solution)/shard_map/ppermute | solution.py:372
  89.9 12.3 %collective-permute-start.3 = (bf16[80,2304]{1,0:T(8,128)(2,1)S(1)}, bf16[80,2304]{1,0:T(8,128)(2,1)S(1)}, u32[]{:S(2)}, u32[]{:S(2)}) collective-permute-start(bf16[80,2304]{1,0:T(8,128)(2,1)S(1)} %bitcast.20), channel_id=1, source_target_pairs={{0,32},{8,40},{16,48},{24,56},{32,64},{40,72},{48,80},{56,88},{64,... | collective-permute-start | bytes 1105928 | tf_op jit(solution)/shard_map/ppermute | solution.py:372
  90.0 12.2 %collective-permute-start.11 = (bf16[80,2304]{1,0:T(8,128)(2,1)S(1)}, bf16[80,2304]{1,0:T(8,128)(2,1)S(1)}, u32[]{:S(2)}, u32[]{:S(2)}) collective-permute-start(bf16[80,2304]{1,0:T(8,128)(2,1)S(1)} %bitcast.29), channel_id=1, source_target_pairs={{0,24},{8,0},{16,8},{24,16},{32,56},{40,32},{48,40},{56,48},{64,88... | collective-permute-start | bytes 1105928 | tf_op jit(solution)/shard_map/ppermute | solution.py:372
  94.3 12.0 %collective-permute-start.10 = (bf16[80,2304]{1,0:T(8,128)(2,1)S(1)}, bf16[80,2304]{1,0:T(8,128)(2,1)S(1)}, u32[]{:S(2)}, u32[]{:S(2)}) collective-permute-start(bf16[80,2304]{1,0:T(8,128)(2,1)S(1)} %bitcast.26), channel_id=1, source_target_pairs={{0,8},{8,16},{16,24},{24,0},{32,40},{40,48},{48,56},{56,32},{64,72... | collective-permute-start | bytes 1105928 | tf_op jit(solution)/shard_map/ppermute | solution.py:372
  98.6 10.3 %collective-permute-start.6 = (bf16[80,2304]{1,0:T(8,128)(2,1)S(1)}, bf16[80,2304]{1,0:T(8,128)(2,1)S(1)}, u32[]{:S(2)}, u32[]{:S(2)}) collective-permute-start(bf16[80,2304]{1,0:T(8,128)(2,1)S(1)} %collective-permute-done.4.refs_1_), channel_id=1, source_target_pairs={{0,96},{8,104},{16,112},{24,120},{32,0},{40,8},{48,16},{56,24},{64... | collective-permute-start | bytes 1105928 | tf_op jit(solution)/shard_map/ppermute | solution.py:372
  102.2 10.3 %collective-permute-start.5 = (bf16[80,2304]{1,0:T(8,128)(2,1)S(1)}, bf16[80,2304]{1,0:T(8,128)(2,1)S(1)}, u32[]{:S(2)}, u32[]{:S(2)}) collective-permute-start(bf16[80,2304]{1,0:T(8,128)(2,1)S(1)} %collective-permute-done.3.refs_0_), channel_id=1, source_target_pairs={{0,32},{8,40},{16,48},{24,56},{32,64},{40,72},{48,80},{56,88},{64,... | collective-permute-start | bytes 1105928 | tf_op jit(solution)/shard_map/ppermute | solution.py:372
  102.2 11.4 %collective-permute-start.13 = (bf16[80,2304]{1,0:T(8,128)(2,1)S(1)}, bf16[80,2304]{1,0:T(8,128)(2,1)S(1)}, u32[]{:S(2)}, u32[]{:S(2)}) collective-permute-start(bf16[80,2304]{1,0:T(8,128)(2,1)S(1)} %collective-permute-done.11.refs_5_), channel_id=1, source_target_pairs={{0,24},{8,0},{16,8},{24,16},{32,56},{40,32},{48,40},{56,48},{64,88... | collective-permute-start | bytes 1105928 | tf_op jit(solution)/shard_map/ppermute | solution.py:372
  106.3 11.1 %collective-permute-start.12 = (bf16[80,2304]{1,0:T(8,128)(2,1)S(1)}, bf16[80,2304]{1,0:T(8,128)(2,1)}, u32[]{:S(2)}, u32[]{:S(2)}) collective-permute-start(bf16[80,2304]{1,0:T(8,128)(2,1)S(1)} %collective-permute-done.10.refs_4_), channel_id=1, source_target_pairs={{0,8},{8,16},{16,24},{24,0},{32,40},{40,48},{48,56},{56,32},{64,72... | collective-permute-start | bytes 1105928 | tf_op jit(solution)/shard_map/ppermute | solution.py:372
  106.3 22.3 %collective-permute-start.15 = (bf16[80,2304]{1,0:T(8,128)(2,1)S(1)}, bf16[80,2304]{1,0:T(8,128)(2,1)}, u32[]{:S(2)}, u32[]{:S(2)}) collective-permute-start(bf16[80,2304]{1,0:T(8,128)(2,1)S(1)} %bitcast.24), channel_id=1, source_target_pairs={{0,32},{8,40},{16,48},{24,56},{32,64},{40,72},{48,80},{56,88},{64,... | collective-permute-start | bytes 1105928 | tf_op jit(solution)/shard_map/ppermute | solution.py:372
  109.0 19.7 %collective-permute-start.14 = (bf16[80,2304]{1,0:T(8,128)(2,1)S(1)}, bf16[80,2304]{1,0:T(8,128)(2,1)}, u32[]{:S(2)}, u32[]{:S(2)}) collective-permute-start(bf16[80,2304]{1,0:T(8,128)(2,1)S(1)} %bitcast.21), channel_id=1, source_target_pairs={{0,96},{8,104},{16,112},{24,120},{32,0},{40,8},{48,16},{56,24},{64... | collective-permute-start | bytes 1105928 | tf_op jit(solution)/shard_map/ppermute | solution.py:372
  112.5 16.2 %collective-permute-start.17 = (bf16[80,2304]{1,0:T(8,128)(2,1)S(1)}, bf16[80,2304]{1,0:T(8,128)(2,1)}, u32[]{:S(2)}, u32[]{:S(2)}) collective-permute-start(bf16[80,2304]{1,0:T(8,128)(2,1)S(1)} %bitcast.30), channel_id=1, source_target_pairs={{0,8},{8,16},{16,24},{24,0},{32,40},{40,48},{48,56},{56,32},{64,72... | collective-permute-start | bytes 1105928 | tf_op jit(solution)/shard_map/ppermute | solution.py:372
  113.6 15.1 %collective-permute-start.16 = (bf16[80,2304]{1,0:T(8,128)(2,1)S(1)}, bf16[80,2304]{1,0:T(8,128)(2,1)}, u32[]{:S(2)}, u32[]{:S(2)}) collective-permute-start(bf16[80,2304]{1,0:T(8,128)(2,1)S(1)} %bitcast.27), channel_id=1, source_target_pairs={{0,24},{8,0},{16,8},{24,16},{32,56},{40,32},{48,40},{56,48},{64,88... | collective-permute-start | bytes 1105928 | tf_op jit(solution)/shard_map/ppermute | solution.py:372
  128.6 18.1 %collective-permute-start.19 = (bf16[80,2304]{1,0:T(8,128)(2,1)}, bf16[80,2304]{1,0:T(8,128)(2,1)S(1)}, u32[]{:S(2)}, u32[]{:S(2)}) collective-permute-start(bf16[80,2304]{1,0:T(8,128)(2,1)} %get-tuple-element.71), channel_id=1, source_target_pairs={{0,32},{8,40},{16,48},{24,56},{32,64},{40,72},{48,80},{56,88},{64,... | collective-permute-start | bytes 1105928 | tf_op jit(solution)/shard_map/ppermute | solution.py:372
  128.7 28.8 %collective-permute-start.18 = (bf16[80,2304]{1,0:T(8,128)(2,1)}, bf16[80,2304]{1,0:T(8,128)(2,1)S(1)}, u32[]{:S(2)}, u32[]{:S(2)}) collective-permute-start(bf16[80,2304]{1,0:T(8,128)(2,1)} %get-tuple-element.69), channel_id=1, source_target_pairs={{0,96},{8,104},{16,112},{24,120},{32,0},{40,8},{48,16},{56,24},{64... | collective-permute-start | bytes 1105928 | tf_op jit(solution)/shard_map/ppermute | solution.py:372
  131.4 26.2 %collective-permute-start.21 = (bf16[80,2304]{1,0:T(8,128)(2,1)}, bf16[80,2304]{1,0:T(8,128)(2,1)S(1)}, u32[]{:S(2)}, u32[]{:S(2)}) collective-permute-start(bf16[80,2304]{1,0:T(8,128)(2,1)} %get-tuple-element.73), channel_id=1, source_target_pairs={{0,32},{8,40},{16,48},{24,56},{32,64},{40,72},{48,80},{56,88},{64,... | collective-permute-start | bytes 1105928 | tf_op jit(solution)/shard_map/ppermute | solution.py:372
  131.4 16.5 %collective-permute-start.22 = (bf16[80,2304]{1,0:T(8,128)(2,1)}, bf16[80,2304]{1,0:T(8,128)(2,1)S(1)}, u32[]{:S(2)}, u32[]{:S(2)}) collective-permute-start(bf16[80,2304]{1,0:T(8,128)(2,1)} %get-tuple-element.75), channel_id=1, source_target_pairs={{0,96},{8,104},{16,112},{24,120},{32,0},{40,8},{48,16},{56,24},{64... | collective-permute-start | bytes 1105928 | tf_op jit(solution)/shard_map/ppermute | solution.py:372
  134.1 30.1 %collective-permute-start.27 = (bf16[80,2304]{1,0:T(8,128)(2,1)}, bf16[80,2304]{1,0:T(8,128)(2,1)S(1)}, u32[]{:S(2)}, u32[]{:S(2)}) collective-permute-start(bf16[80,2304]{1,0:T(8,128)(2,1)} %get-tuple-element.81), channel_id=1, source_target_pairs={{0,24},{8,0},{16,8},{24,16},{32,56},{40,32},{48,40},{56,48},{64,88... | collective-permute-start | bytes 1105928 | tf_op jit(solution)/shard_map/ppermute | solution.py:372
  157.5 8.8 %collective-permute-start.30 = (bf16[80,2304]{1,0:T(8,128)(2,1)S(1)}, bf16[80,2304]{1,0:T(8,128)(2,1)S(1)}, u32[]{:S(2)}, u32[]{:S(2)}) collective-permute-start(bf16[80,2304]{1,0:T(8,128)(2,1)S(1)} %copy-done.14), channel_id=1, source_target_pairs={{0,8},{8,16},{16,24},{24,0},{32,40},{40,48},{48,56},{56,32},{64,72... | collective-permute-start | bytes 1105928 | tf_op jit(solution)/shard_map/ppermute | solution.py:372
  157.6 13.5 %collective-permute-start.29 = (bf16[80,2304]{1,0:T(8,128)(2,1)S(1)}, bf16[80,2304]{1,0:T(8,128)(2,1)S(1)}, u32[]{:S(2)}, u32[]{:S(2)}) collective-permute-start(bf16[80,2304]{1,0:T(8,128)(2,1)S(1)} %add_convert_fusion.1), channel_id=1, source_target_pairs={{0,8},{8,16},{16,24},{24,0},{32,40},{40,48},{48,56},{56,32},{64,72... | collective-permute-start | bytes 1105928 | tf_op jit(solution)/shard_map/ppermute | solution.py:372
  162.1 9.0 %collective-permute-start.32 = (bf16[80,2304]{1,0:T(8,128)(2,1)S(1)}, bf16[80,2304]{1,0:T(8,128)(2,1)S(1)}, u32[]{:S(2)}, u32[]{:S(2)}) collective-permute-start(bf16[80,2304]{1,0:T(8,128)(2,1)S(1)} %add_convert_fusion), channel_id=1, source_target_pairs={{0,24},{8,0},{16,8},{24,16},{32,56},{40,32},{48,40},{56,48},{64,88... | collective-permute-start | bytes 1105928 | tf_op jit(solution)/shard_map/ppermute | solution.py:372
  162.4 12.0 %collective-permute-start.24 = (bf16[40,2304]{1,0:T(8,128)(2,1)S(1)}, bf16[40,2304]{1,0:T(8,128)(2,1)S(1)}, u32[]{:S(2)}, u32[]{:S(2)}) collective-permute-start(bf16[40,2304]{1,0:T(8,128)(2,1)S(1)} %get-tuple-element.77), channel_id=1, source_target_pairs={{0,16},{8,24},{16,0},{24,8},{32,48},{40,56},{48,32},{56,40},{64,80... | collective-permute-start | bytes 552968 | tf_op jit(solution)/shard_map/ppermute | solution.py:372
  164.2 11.3 %collective-permute-start.25 = (bf16[40,2304]{1,0:T(8,128)(2,1)S(1)}, bf16[40,2304]{1,0:T(8,128)(2,1)S(1)}, u32[]{:S(2)}, u32[]{:S(2)}) collective-permute-start(bf16[40,2304]{1,0:T(8,128)(2,1)S(1)} %get-tuple-element.78), channel_id=1, source_target_pairs={{0,24},{8,0},{16,8},{24,16},{32,56},{40,32},{48,40},{56,48},{64,88... | collective-permute-start | bytes 552968 | tf_op jit(solution)/shard_map/ppermute | solution.py:372
  166.3 10.5 %collective-permute-start.26 = (bf16[40,2304]{1,0:T(8,128)(2,1)S(1)}, bf16[40,2304]{1,0:T(8,128)(2,1)S(1)}, u32[]{:S(2)}, u32[]{:S(2)}) collective-permute-start(bf16[40,2304]{1,0:T(8,128)(2,1)S(1)} %get-tuple-element.79), channel_id=1, source_target_pairs={{0,8},{8,16},{16,24},{24,0},{32,40},{40,48},{48,56},{56,32},{64,72... | collective-permute-start | bytes 552968 | tf_op jit(solution)/shard_map/ppermute | solution.py:372
  (30 other events, 455.8 us)

commit v2 on v1

--- a/solution.py
+++ b/solution.py
@@ -30,8 +30,8 @@
     return lax.dot_general(a, b, (((0,), (0,)), ((), ())), preferred_element_type=F32)
 
 
-def attend_kernel(table, length, place, q_ref, k_ref, v_ref, nk_ref, nv_ref, out_ref, top_sc, den_sc, *, share):
-    groups = out_ref.shape[0]
+def attend_kernel(table, length, place, q_ref, k_ref, v_ref, nk_ref, nv_ref, keep_ref, send_ref, sum_sc, top_sc, den_sc, *, share):
+    groups = 2 * keep_ref.shape[0]
     req, group = pl.program_id(0), pl.program_id(1)
     new_len = q_ref.shape[1]
     pages, page_len = k_ref.shape[1], k_ref.shape[3]
@@ -73,7 +73,8 @@
             index = (group * pairs + pair) * 4 + piece
             dest = index // (share // 32)
             offset = pl.multiple_of((index - dest * (share // 32)) * 32, 32)
-            out_ref[dest, pl.ds(offset, 32), pl.ds(lane_at, new_len)] = num[piece * 32 : piece * 32 + 32]
+            side = (dest + place[0]) % 2
+            sum_sc[side, dest // 2, pl.ds(offset, 32), pl.ds(lane_at, new_len)] = num[piece * 32 : piece * 32 + 32]
         head = (group * pairs + pair) * 2
         for half in range(2):
             lanes = slice(half * new_len, half * new_len + new_len)
@@ -82,10 +83,12 @@
 
     @pl.when((req == pl.num_programs(0) - 1) & (group == pl.num_programs(1) - 1))
     def _():
-        for dest in range(out_ref.shape[0]):
+        for dest in range(groups):
             first = dest * share // HD
             stats = jnp.concatenate([top_sc[first : first + 8, 0, :], den_sc[first : first + 8, 0, :]], axis=0)
-            out_ref[dest, share : share + STAT_ROWS, :] = stats.astype(BF16)
+            sum_sc[(dest + place[0]) % 2, dest // 2, share : share + STAT_ROWS, :] = stats.astype(BF16)
+        keep_ref[...] = sum_sc[0]
+        send_ref[...] = sum_sc[1]
 
 
 def attend(table, length, place, queries, cache_pool, new_kv, dests):
@@ -109,10 +112,11 @@
                 pl.BlockSpec((1, 1, local_new, block), lambda r, g, *_: (r, 0, 0, g)),
                 pl.BlockSpec((1, 1, local_new, block), lambda r, g, *_: (r, 1, 0, g)),
             ],
-            out_specs=pl.BlockSpec((dests, share + STAT_ROWS, req_here * new_len), lambda r, g, *_: (0, 0, 0)),
-            scratch_shapes=[pltpu.VMEM((heads + 12, 1, req_here * new_len), F32)] * 2,
-        ),
-        out_shape=jax.ShapeDtypeStruct((dests, share + STAT_ROWS, req_here * new_len), BF16),
+            out_specs=[pl.BlockSpec((dests // 2, share + STAT_ROWS, req_here * new_len), lambda r, g, *_: (0, 0, 0))] * 2,
+            scratch_shapes=[pltpu.VMEM((2, dests // 2, share + STAT_ROWS, req_here * new_len), BF16)]
+            + [pltpu.VMEM((heads + 12, 1, req_here * new_len), F32)] * 2,
+        ),
+        out_shape=[jax.ShapeDtypeStruct((dests // 2, share + STAT_ROWS, req_here * new_len), BF16)] * 2,
         cost_estimate=pl.CostEstimate(
             flops=4 * req_here * new_len * width * keys,
             bytes_accessed=cache_pool.size * 2 + queries.size * 2,
@@ -121,6 +125,44 @@
         compiler_params=pltpu.CompilerParams(vmem_limit_bytes=60 << 20),
         name="attend",
     )(table, length, place, queries, cache_pool, cache_pool, new_kv, new_kv)
+
+
+def merge_kernel(place, own_ref, other_ref, out_ref, spread_sc, *, share):
+    tokens = own_ref.shape[2]
+    offset = pl.multiple_of(place[0] % 2 * (HD // 2), HD // 2)
+    both = (own_ref, other_ref)
+    for dest in range(own_ref.shape[0]):
+        tops = [ref[dest, share : share + 8, :].astype(F32) for ref in both]
+        top = jnp.maximum(*tops)
+        scales = [jnp.exp(t - top) for t in tops]
+        den = functools.reduce(jnp.add, [s * ref[dest, share + 8 : share + 16, :].astype(F32) for s, ref in zip(scales, both)])
+        total = None
+        for side, ref in enumerate(both):
+            for head in range(5):
+                spread_sc[side, head * HD : head * HD + HD, :] = jnp.broadcast_to(scales[side][head : head + 1, :], (HD, tokens))
+            term = ref[dest, :share, :].astype(F32) * spread_sc[side, pl.ds(offset, share), :]
+            total = term if total is None else total + term
+        out_ref[dest, :share, :] = total.astype(BF16)
+        out_ref[dest, share:, :] = jnp.concatenate([top, den], axis=0).astype(BF16)
+
+
+def merge(place, own, other):
+    dests, rows, tokens = own.shape
+    whole = pl.BlockSpec((dests, rows, tokens), lambda i, *_: (0, 0, 0))
+    return pl.pallas_call(
+        functools.partial(merge_kernel, share=rows - STAT_ROWS),
+        grid_spec=pltpu.PrefetchScalarGridSpec(
+            num_scalar_prefetch=1,
+            grid=(1,),
+            in_specs=[whole, whole],
+            out_specs=whole,
+            scratch_shapes=[pltpu.VMEM((2, 5 * HD, tokens), F32)],
+        ),
+        out_shape=jax.ShapeDtypeStruct(own.shape, BF16),
+        cost_estimate=pl.CostEstimate(flops=4 * own.size, bytes_accessed=6 * own.size, transcendentals=0),
+        compiler_params=pltpu.CompilerParams(vmem_limit_bytes=10 << 20),
+        name="merge",
+    )(place, own, other)
 
 
 def join_kernel(place, recv_ref, res_ref, gain_ref, slot_ref, placed_ref, hidden_ref, spread_sc, *, share):
@@ -221,65 +263,57 @@
 
 def expert_kernel(*refs, count):
     blocks, gate_up_hbm, down_hbm = refs[:count], refs[count], refs[count + 1]
-    outs, (x_sc, gate_up_ref, down_ref, weight_sc, both_sc, y_sc, sems) = refs[count + 2 : 2 * count + 2], refs[2 * count + 2 :]
-    rows = blocks[0].shape[0]
-    groups, _, units = gate_up_ref.shape
-    share = x_sc.shape[1] // groups
-    half = weight_sc.shape[1] // 2
+    outs, (x_sc, gate_up_sc, down_sc, both_sc, y_sc, sems) = refs[count + 2 : -6], refs[-6:]
+    rows, out_rows, units = blocks[0].shape[0], outs[0].shape[0], down_sc.shape[1]
+    half = gate_up_sc.shape[1] // 2
     tile = 256
     loads = [pltpu.make_async_copy(b, x_sc.at[pl.ds(i * rows, rows)], sems.at[i]) for i, b in enumerate(blocks)]
-    stores = [pltpu.make_async_copy(y_sc.at[pl.ds(i * rows, rows)], o, sems.at[count + i]) for i, o in enumerate(outs)]
-    parts = [pltpu.make_async_copy(gate_up_hbm.at[g], gate_up_ref.at[g], sems.at[2 * count + g]) for g in range(groups)]
-    down_load = pltpu.make_async_copy(down_hbm, down_ref, sems.at[2 * count + groups])
-    for load in (*parts, *loads, down_load):
+    loads.append(pltpu.make_async_copy(gate_up_hbm, gate_up_sc, sems.at[count]))
+    down_load = pltpu.make_async_copy(down_hbm, down_sc, sems.at[count + 1])
+    for load in (*loads, down_load):
         load.start()
-    for g in range(groups):
-        parts[g].wait()
-        weight_sc[g * share : g * share + share, :units] = gate_up_ref[g, :share]
-        weight_sc[g * share : g * share + share, half : half + units] = gate_up_ref[g, share:]
     for load in loads:
         load.wait()
 
     @pl.loop(0, 2 * half // tile)
     def _(j):
         lanes = pl.ds(pl.multiple_of(j * tile, tile), tile)
-        both_sc[:, lanes] = jnp.dot(x_sc[...], weight_sc[:, lanes], preferred_element_type=F32)
+        both_sc[:, lanes] = jnp.dot(x_sc[...], gate_up_sc[:, lanes], preferred_element_type=F32)
 
     gate, up = both_sc[:, :units], both_sc[:, half : half + units]
     act = (gate / (1.0 + jnp.exp(-gate)) * up).astype(BF16)
     down_load.wait()
 
-    @pl.loop(0, down_ref.shape[0] // tile)
+    @pl.loop(0, down_sc.shape[0] // tile)
     def _(j):
         lanes = pl.ds(pl.multiple_of(j * tile, tile), tile)
-        y_sc[:, lanes] = nt_dot(act, down_ref[lanes, :]).astype(BF16)
-
-    for copy in stores:
-        copy.start()
-    for copy in stores:
-        copy.wait()
-
-
-def expert(blocks, gate_up, down):
+        y_sc[:, lanes] = nt_dot(act, down_sc[lanes, :]).astype(BF16)
+        for i, out in enumerate(outs):
+            at = pl.ds(i * out_rows, out_rows)
+            pltpu.make_async_copy(y_sc.at[at, lanes], out.at[:, lanes], sems.at[count + 2 + i]).start()
+
+    for i, out in enumerate(outs):
+        pltpu.make_async_copy(y_sc.at[pl.ds(i * out_rows, out_rows)], out, sems.at[count + 2 + i]).wait()
+
+
+def expert(blocks, gate_up, down, out_rows):
     rows, width = blocks[0].shape
     units = down.shape[1]
     count = len(blocks)
     total = count * rows
-    packed = 2 * (-(-units // 128) * 128)
     anywhere = pl.BlockSpec(memory_space=pltpu.HBM)
     return pl.pallas_call(
         functools.partial(expert_kernel, count=count),
         in_specs=[anywhere] * (count + 2),
-        out_specs=[anywhere] * count,
-        out_shape=[jax.ShapeDtypeStruct((rows, width), BF16)] * count,
+        out_specs=[anywhere] * (total // out_rows),
+        out_shape=[jax.ShapeDtypeStruct((out_rows, width), BF16)] * (total // out_rows),
         scratch_shapes=[
             pltpu.VMEM((total, width), BF16),
             pltpu.VMEM(gate_up.shape, BF16),
             pltpu.VMEM(down.shape, BF16),
-            pltpu.VMEM((width, packed), BF16),
-            pltpu.VMEM((total, packed), F32),
+            pltpu.VMEM((total, gate_up.shape[1]), F32),
             pltpu.VMEM((total, width), BF16),
-            pltpu.SemaphoreType.DMA((2 * count + gate_up.shape[0] + 1,)),
+            pltpu.SemaphoreType.DMA((count + 2 + total // out_rows,)),
         ],
         cost_estimate=pl.CostEstimate(
             flops=6 * total * width * units,
@@ -300,8 +334,10 @@
     rows = outs[0].shape[0]
     for i, out in enumerate(outs):
         at = slice(i % 2 * rows, i % 2 * rows + rows)
-        some = refs[:3] if i < 2 else refs[3:6]
-        out[...] = functools.reduce(jnp.add, [ref[at, :].astype(F32) for ref in some]).astype(BF16)
+        lower = slice((i % 2 + 2) * rows, (i % 2 + 3) * rows)
+        first, second, third = refs[:3] if i < 2 else refs[3:6]
+        total = first[at, :].astype(F32) + second[at, :].astype(F32) + third[lower, :].astype(F32)
+        out[...] = total.astype(BF16)
 
 
 def add_blocks(low, high):
@@ -398,10 +434,15 @@
 
     down_all = exchange(jnp.transpose(w_down, (0, 2, 1)))
     place = narrow_pos.reshape(1)
-    sums = attend(page_table, cached_len, place, queries, cache_pool, new_kv, narrow_count)
-    sums, down_all, w_gate_up = lax.optimization_barrier((sums, down_all, w_gate_up))
-    later = jnp.concatenate([w_gate_up[:, :, 0], w_gate_up[:, :, 1]], axis=1)
-    sums = exchange(sums)
+    own, other = attend(page_table, cached_len, place, queries, cache_pool, new_kv, narrow_count)
+    own, w_gate_up = lax.optimization_barrier((own, w_gate_up))
+    padding = ((0, 0), (0, 0), (0, -units % 128))
+    later = jnp.concatenate([jnp.pad(w_gate_up[:, :, 0], padding), jnp.pad(w_gate_up[:, :, 1], padding)], axis=2)
+    other = lax.ppermute(other, "narrow", [(i, i ^ 1) for i in range(narrow_count)])
+    sums = merge(place, own, other)
+    sums, down_all = lax.optimization_barrier((sums, down_all))
+    chips = [[2 * x + core for x in range(narrow_count // 2)] for core in range(2)]
+    sums = lax.all_to_all(sums, "narrow", 0, 0, axis_index_groups=chips, tiled=True)
 
     flat_ids = expert_ids.reshape(token_rows * 2)
     onehot = (flat_ids[:, None] == jnp.arange(expert_count, dtype=jnp.int32)[None, :]).astype(BF16)
@@ -416,7 +457,7 @@
     placed = exchange(placed)
     later, placed = lax.optimization_barrier((later, placed))
     later = exchange(later)
-    down_all = down_all.reshape(width, units)
+    later, down_all = later.reshape(width, -1), down_all.reshape(width, units)
     rows = norm_rows(placed, share)
 
     half = CAP // 2
@@ -430,11 +471,11 @@
         before_low, after_high = shift(low, second, 1), shift(high, second, -1)
         before_high, after_low = shift(high, second, 1), shift(low, second, -1)
         far_low, far_high = shift(before_low, second, 1), shift(after_high, second, -1)
-        early += [before_low, after_high, far_low, far_high]
+        early += [far_low, after_high, far_high, before_low]
         late += [low, high, after_low, before_high]
-    early = list(expert(early, later, down_all))
+    early = list(expert(early, later, down_all, 2 * CAP))
     early[0], *late = lax.optimization_barrier((early[0], *late))
-    late = expert(late, later, down_all)
+    late = expert(late, later, down_all, CAP)
 
     def back(blocks, axis):
         return [blocks[0], *(shift(block, axis, -step) for block, step in zip(blocks[1:], STEPS))]
@@ -444,13 +485,15 @@
 
     four = []
     for color, second in enumerate(("y", "z")):
-        before_low, after_high, far_low, far_high = early[4 * color : 4 * color + 4]
         low, high, after_low, before_high = late[4 * color : 4 * color + 4]
         got = []
-        for block, step in zip((far_low, far_high, before_low, after_high), (1, -1, -1, 1)):
+        for block, step in zip(early[2 * color : 2 * color + 2], (1, -1)):
             got.append(shift(block, second, step))
-        more_low, more_high = shift(joined(after_low, got[0]), second, 1), shift(joined(before_high, got[1]), second, -1)
-        four.append(add_blocks([low, got[2], more_low], [high, got[3], more_high]))
+        more_low, more_high = (
+            shift(joined(after_low, got[0][:CAP]), second, 1),
+            shift(joined(before_high, got[1][:CAP]), second, -1),
+        )
+        four.append(add_blocks([low, more_low, got[1]], [high, more_high, got[0]]))
     out_rows = finish([*back(four[0], "z"), *back(four[1], "y")], narrow_count)
     out_rows = exchange(out_rows)
     return mix(out_rows.reshape(expert_count * CAP, share), slots.T, route_weight.T, hidden).T

time: 208 us -> 185 us (0.89)
  waiting for transfers between devices: 50.4 us -> 30.4 us
  blocking collectives: 25.3 us -> 20.7 us
    all_to_all x4 -> x3, waiting for transfers between devices: 20 us -> 4.65 us  [exchange(): return lax.all_to_all(x, 'narrow', 0, 0, tiled=True)]
    ppermute x36 -> x32, waiting for transfers between devices: 30.4 us -> 19.7 us  [shift(): return lax.ppermute(x, 'wide', ring_pairs(axis, step))]
    all_to_all x1, blocking collectives: 25.3 us -> 20.7 us  [exchange(): return lax.all_to_all(x, 'narrow', 0, 0, tiled=True)]
    all_to_all x0 -> x1, waiting for transfers between devices: none -> 4.36 us  [local(): lax.all_to_all(sums, 'narrow', 0, 0, axis_index_groups=chips, tiled=True)]
    all_to_all x0 -> x1, starting transfers between devices: none -> 4.15 us  [local(): lax.all_to_all(sums, 'narrow', 0, 0, axis_index_groups=chips, tiled=True)]
    all_to_all x4 -> x3, starting transfers between devices: 20.1 us -> 16.2 us  [exchange(): return lax.all_to_all(x, 'narrow', 0, 0, tiled=True)]
    ppermute x36 -> x32, starting transfers between devices: 51.9 us -> 51.7 us  [shift(): return lax.ppermute(x, 'wide', ring_pairs(axis, step))]
  transfers between devices with their start and end apart: 40 -> 37, of which waited for: 16 -> 13; matrix products, arithmetic and copies ran while one was open for 6% -> 8% of each run, Pallas kernels for 20% -> 23%
where the time goes in v2:
time: 185 us
  starting transfers between devices  72 us (39%)
  Pallas kernels  45.2 us (24%)
  waiting for transfers between devices  30.4 us (16%)
  blocking collectives  20.7 us (11%)
  local copies, waits for them, and re-layouts  10.1 us (5%)
  other arithmetic  5.58 us (3%)
    ppermute x32, starting transfers between devices, shift(): return lax.ppermute(x, 'wide', ring_pairs(axis, step))  51.7 us
    all_to_all x1, blocking collectives, exchange(): return lax.all_to_all(x, 'narrow', 0, 0, tiled=True)  20.7 us
    pallas_call x2, Pallas kernels, expert(): pl.pallas_call(functools.partial(expert_kernel, count=count), in_specs=[a...  20.6 us
    ppermute x32, waiting for transfers between devices, shift(): return lax.ppermute(x, 'wide', ring_pairs(axis, step))  19.7 us
    pallas_call x1, Pallas kernels, attend(): pl.pallas_call(functools.partial(attend_kernel, share=share), grid_spec=p...  18.3 us
    all_to_all x3, starting transfers between devices, exchange(): return lax.all_to_all(x, 'narrow', 0, 0, tiled=True)  16.2 us
    all_to_all x3, waiting for transfers between devices, exchange(): return lax.all_to_all(x, 'narrow', 0, 0, tiled=True)  4.65 us
    all_to_all x1, waiting for transfers between devices, local(): lax.all_to_all(sums, 'narrow', 0, 0, axis_index_groups=chips, tiled=True)  4.36 us
  transfers between devices with their start and end apart: 37, of which 13 were waited for; matrix products, arithmetic and copies ran while one was open for 8% of the time, Pallas kernels for 23%

profile of v2, /device:TPU:1, one launch (start us, length us, event | category | flops | bytes accessed | tf_op | source)
XLA Modules:
  0.0 184.6 jit_solution(16833162955104817843)
XLA Ops:
  0.0 5.9 %all-to-all-start = ((bf16[8,288,360]{2,1,0:T(8,128)(2,1)}), bf16[8,288,360]{2,1,0:T(8,128)(2,1)}, u32[]{:S(2)}, u32[]{:S(2)}) async-start(bf16[8,288,360]{2,1,0:T(8,128)(2,1)} %bitcast.33), calls=%async_computation | async-start | bytes 3538944 | tf_op jit(solution)/shard_map/all_to_all | solution.py:433
  5.9 18.3 %attend.1 = (bf16[4,304,256]{2,1,0:T(8,128)(2,1)}, bf16[4,304,256]{2,1,0:T(8,128)(2,1)}) custom-call(s32[2,32]{1,0:T(2,128)} %table.1, s32[2]{0:T(128)} %length.1, s32[1]{0:T(128)} %bitcast.place, bf16[2,128,2304]{2,1,0:T(8,128)(2,1)} %q_ref.1, bf16[2,4,2,128,2304]{4,3,2,1,0:T(8,128)(2,1)} %v_ref.1, bf16[2,4,2,128,2304]{4,3,2,1,0:T(8,128)(2,1)} %v_ref.1, ...), custom_call_target="tpu_custom_call" | custom-call | flops 1245708288 | bytes 10616832 | tf_op jit(solution)/shard_map/attend/pallas_call | solution.py:103
  28.9 4.1 %all-to-all-start.1 = ((bf16[4,304,256]{2,1,0:T(8,128)(2,1)}), bf16[4,304,256]{2,1,0:T(8,128)(2,1)S(1)}, u32[]{:S(2)}, u32[]{:S(2)}) async-start(bf16[4,304,256]{2,1,0:T(8,128)(2,1)} %merge.1), calls=%async_computation.1 | async-start | bytes 1245184 | tf_op jit(solution)/shard_map/all_to_all | solution.py:445
  34.5 4.2 %copy.14 = bf16[8,288,2,360]{3,1,0,2:T(8,128)(2,1)} copy(bf16[8,288,2,360]{3,2,1,0:T(2,128)(2,1)} %param.20) | data formatting | bytes 6635520 | tf_op jit(solution)/shard_map/optimization_barrier | solution.py:438
  38.7 4.4 %all-to-all-done.1.recv_ref = bf16[4,304,256]{2,1,0:T(8,128)(2,1)S(1)} async-done(((bf16[4,304,256]{2,1,0:T(8,128)(2,1)}), bf16[4,304,256]{2,1,0:T(8,128)(2,1)S(1)}, u32[]{:S(2)}, u32[]{:S(2)}) %all-to-all-start.1) | async-done | bytes 622624 | tf_op jit(solution)/shard_map/all_to_all | solution.py:445
  45.2 4.9 %all-to-all-start.2 = ((bf16[8,80,384]{2,1,0:T(8,128)(2,1)}), bf16[8,80,384]{2,1,0:T(8,128)(2,1)S(1)}, u32[]{:S(2)}, u32[]{:S(2)}) async-start(bf16[8,80,384]{2,1,0:T(8,128)(2,1)} %get-tuple-element.53), calls=%async_computation.2 | async-start | bytes 983040 | tf_op jit(solution)/shard_map/all_to_all | solution.py:433
  50.1 2.4 %slice_bitcast_fusion.1 = (bf16[8,288,360]{2,1,0:T(8,128)(2,1)S(1)}, bf16[8,288,360]{2,1,0:T(8,128)(2,1)S(1)}) fusion(bf16[8,288,2,360]{3,1,0,2:T(8,128)(2,1)} %copy.14), kind=kLoop, calls=%fused_computation.6 | loop fusion | bytes 6635520 | tf_op jit(solution)/shard_map/squeeze | solution.py:440
  52.4 2.0 %fusion.2 = bf16[8,288,768]{2,1,0:T(8,128)(2,1)} fusion(bf16[8,288,360]{2,1,0:T(8,128)(2,1)S(1)} %get-tuple-element.92, bf16[8,288,360]{2,1,0:T(8,128)(2,1)S(1)} %get-tuple-element.91), kind=kLoop, calls=%fused_computation.4 | loop fusion | flops 14155776 | bytes 6856704 | tf_op jit(solution)/shard_map/concatenate | solution.py:440
  54.4 4.6 %all-to-all-done.2.recv_ref = bf16[8,80,384]{2,1,0:T(8,128)(2,1)S(1)} async-done(((bf16[8,80,384]{2,1,0:T(8,128)(2,1)}), bf16[8,80,384]{2,1,0:T(8,128)(2,1)S(1)}, u32[]{:S(2)}, u32[]{:S(2)}) %all-to-all-start.2) | async-done | bytes 491552 | tf_op jit(solution)/shard_map/all_to_all | solution.py:433
  59.1 5.3 %all-to-all-start.3 = ((bf16[8,288,768]{2,1,0:T(8,128)(2,1)}), bf16[8,288,768]{2,1,0:T(8,128)(2,1)}, u32[]{:S(2)}, u32[]{:S(2)}) async-start(bf16[8,288,768]{2,1,0:T(8,128)(2,1)} %fusion.2), calls=%async_computation.3 | async-start | bytes 7077888 | tf_op jit(solution)/shard_map/all_to_all | solution.py:433
  64.8 3.8 %collective-permute-start.3 = (bf16[40,2304]{1,0:T(8,128)(2,1)S(1)}, bf16[40,2304]{1,0:T(8,128)(2,1)S(1)}, u32[]{:S(2)}, u32[]{:S(2)}) collective-permute-start(bf16[40,2304]{1,0:T(8,128)(2,1)S(1)} %get-tuple-element.94.refs_0_), channel_id=1, source_target_pairs={{0,24},{8,0},{16,8},{24,16},{32,56},{40,32},{48,40},{56,48},{64,88... | collective-permute-start | bytes 552968 | tf_op jit(solution)/shard_map/ppermute | solution.py:408
  70.0 2.7 %collective-permute-start.10 = (bf16[40,2304]{1,0:T(8,128)(2,1)S(1)}, bf16[40,2304]{1,0:T(8,128)(2,1)S(1)}, u32[]{:S(2)}, u32[]{:S(2)}) collective-permute-start(bf16[40,2304]{1,0:T(8,128)(2,1)S(1)} %get-tuple-element.93.refs_0_), channel_id=1, source_target_pairs={{0,96},{8,104},{16,112},{24,120},{32,0},{40,8},{48,16},{56,24},{64... | collective-permute-start | bytes 552968 | tf_op jit(solution)/shard_map/ppermute | solution.py:408
  72.7 2.6 %collective-permute-start.8 = (bf16[40,2304]{1,0:T(8,128)(2,1)S(1)}, bf16[40,2304]{1,0:T(8,128)(2,1)S(1)}, u32[]{:S(2)}, u32[]{:S(2)}) collective-permute-start(bf16[40,2304]{1,0:T(8,128)(2,1)S(1)} %get-tuple-element.93.refs_0_), channel_id=1, source_target_pairs={{0,64},{8,72},{16,80},{24,88},{32,96},{40,104},{48,112},{56,120},{... | collective-permute-start | bytes 552968 | tf_op jit(solution)/shard_map/ppermute | solution.py:408
  75.3 4.3 %collective-permute-done.2.refs_2_ = bf16[40,2304]{1,0:T(8,128)(2,1)S(1)} collective-permute-done((bf16[40,2304]{1,0:T(8,128)(2,1)S(1)}, bf16[40,2304]{1,0:T(8,128)(2,1)S(1)}, u32[]{:S(2)}, u32[]{:S(2)}) %collective-permute-start.2) | collective-permute-done | bytes 184352 | tf_op jit(solution)/shard_map/ppermute | solution.py:408
  79.7 2.8 %collective-permute-start.6 = (bf16[80,2304]{1,0:T(8,128)(2,1)S(1)}, bf16[80,2304]{1,0:T(8,128)(2,1)S(1)}, u32[]{:S(2)}, u32[]{:S(2)}) collective-permute-start(bf16[80,2304]{1,0:T(8,128)(2,1)S(1)} %bitcast.24), channel_id=1, source_target_pairs={{0,96},{8,104},{16,112},{24,120},{32,0},{40,8},{48,16},{56,24},{64... | collective-permute-start | bytes 1105928 | tf_op jit(solution)/shard_map/ppermute | solution.py:408
  82.6 4.4 %collective-permute-start.13 = (bf16[80,2304]{1,0:T(8,128)(2,1)S(1)}, bf16[80,2304]{1,0:T(8,128)(2,1)S(1)}, u32[]{:S(2)}, u32[]{:S(2)}) collective-permute-start(bf16[80,2304]{1,0:T(8,128)(2,1)S(1)} %bitcast.30), channel_id=1, source_target_pairs={{0,24},{8,0},{16,8},{24,16},{32,56},{40,32},{48,40},{56,48},{64,88... | collective-permute-start | bytes 1105928 | tf_op jit(solution)/shard_map/ppermute | solution.py:408
  86.9 4.3 %collective-permute-done.6.refs_1_ = bf16[80,2304]{1,0:T(8,128)(2,1)S(1)} collective-permute-done((bf16[80,2304]{1,0:T(8,128)(2,1)S(1)}, bf16[80,2304]{1,0:T(8,128)(2,1)S(1)}, u32[]{:S(2)}, u32[]{:S(2)}) %collective-permute-start.6) | collective-permute-done | bytes 368672 | tf_op jit(solution)/shard_map/ppermute | solution.py:408
  91.2 3.5 %collective-permute-start.7 = (bf16[80,2304]{1,0:T(8,128)(2,1)S(1)}, bf16[80,2304]{1,0:T(8,128)(2,1)S(1)}, u32[]{:S(2)}, u32[]{:S(2)}) collective-permute-start(bf16[80,2304]{1,0:T(8,128)(2,1)S(1)} %collective-permute-done.6.refs_1_), channel_id=1, source_target_pairs={{0,96},{8,104},{16,112},{24,120},{32,0},{40,8},{48,16},{56,24},{64... | collective-permute-start | bytes 1105928 | tf_op jit(solution)/shard_map/ppermute | solution.py:408
  94.8 4.1 %collective-permute-start.14 = (bf16[80,2304]{1,0:T(8,128)(2,1)S(1)}, bf16[80,2304]{1,0:T(8,128)(2,1)S(1)}, u32[]{:S(2)}, u32[]{:S(2)}) collective-permute-start(bf16[80,2304]{1,0:T(8,128)(2,1)S(1)} %collective-permute-done.13.refs_5_), channel_id=1, source_target_pairs={{0,24},{8,0},{16,8},{24,16},{32,56},{40,32},{48,40},{56,48},{64,88... | collective-permute-start | bytes 1105928 | tf_op jit(solution)/shard_map/ppermute | solution.py:408
  99.2 2.4 %collective-permute-done.7.refs_2_ = bf16[80,2304]{1,0:T(8,128)(2,1)S(1)} collective-permute-done((bf16[80,2304]{1,0:T(8,128)(2,1)S(1)}, bf16[80,2304]{1,0:T(8,128)(2,1)S(1)}, u32[]{:S(2)}, u32[]{:S(2)}) %collective-permute-start.7) | collective-permute-done | bytes 368672 | tf_op jit(solution)/shard_map/ppermute | solution.py:408
  101.6 3.5 %collective-permute-start.15 = (bf16[80,2304]{1,0:T(8,128)(2,1)S(1)}, bf16[80,2304]{1,0:T(8,128)(2,1)}, u32[]{:S(2)}, u32[]{:S(2)}) collective-permute-start(bf16[80,2304]{1,0:T(8,128)(2,1)S(1)} %bitcast.22), channel_id=1, source_target_pairs={{0,96},{8,104},{16,112},{24,120},{32,0},{40,8},{48,16},{56,24},{64... | collective-permute-start | bytes 1105928 | tf_op jit(solution)/shard_map/ppermute | solution.py:408
  106.2 3.8 %collective-permute-start.17 = (bf16[80,2304]{1,0:T(8,128)(2,1)S(1)}, bf16[80,2304]{1,0:T(8,128)(2,1)}, u32[]{:S(2)}, u32[]{:S(2)}) collective-permute-start(bf16[80,2304]{1,0:T(8,128)(2,1)S(1)} %bitcast.28), channel_id=1, source_target_pairs={{0,24},{8,0},{16,8},{24,16},{32,56},{40,32},{48,40},{56,48},{64,88... | collective-permute-start | bytes 1105928 | tf_op jit(solution)/shard_map/ppermute | solution.py:408
  110.0 10.3 %expert.2 = (bf16[160,2304]{1,0:T(8,128)(2,1)}, bf16[160,2304]{1,0:T(8,128)(2,1)}, bf16[160,2304]{1,0:T(8,128)(2,1)}, bf16[160,2304]{1,0:T(8,128)(2,1)}) custom-call(bf16[80,2304]{1,0:T(8,128)(2,1)} %copy-done.20, bf16[80,2304]{1,0:T(8,128)(2,1)} %copy-done.15, bf16[80,2304]{1,0:T(8,128)(2,1)} %copy-done.19, bf16[80,2304]{1,0:T(8,128)(2,1)} %copy-done.16, ...), custom_call_target="tpu_custom_call" | custom-call | flops 3185049600 | bytes 10874880 | tf_op jit(solution)/shard_map/expert/pallas_call | solution.py:305
  120.5 2.7 %collective-permute-start.21 = (bf16[160,2304]{1,0:T(8,128)(2,1)}, bf16[160,2304]{1,0:T(8,128)(2,1)}, u32[]{:S(2)}, u32[]{:S(2)}) collective-permute-start(bf16[160,2304]{1,0:T(8,128)(2,1)} %get-tuple-element.73), channel_id=1, source_target_pairs={{0,96},{8,104},{16,112},{24,120},{32,0},{40,8},{48,16},{56,24},{64... | collective-permute-start | bytes 2211848 | tf_op jit(solution)/shard_map/ppermute | solution.py:408
  123.2 2.7 %collective-permute-start.28 = (bf16[160,2304]{1,0:T(8,128)(2,1)}, bf16[160,2304]{1,0:T(8,128)(2,1)S(1)}, u32[]{:S(2)}, u32[]{:S(2)}) collective-permute-start(bf16[160,2304]{1,0:T(8,128)(2,1)} %get-tuple-element.83), channel_id=1, source_target_pairs={{0,24},{8,0},{16,8},{24,16},{32,56},{40,32},{48,40},{56,48},{64,88... | collective-permute-start | bytes 2211848 | tf_op jit(solution)/shard_map/ppermute | solution.py:408
  125.9 10.3 %expert.3 = (bf16[80,2304]{1,0:T(8,128)(2,1)}, bf16[80,2304]{1,0:T(8,128)(2,1)}, bf16[80,2304]{1,0:T(8,128)(2,1)}, bf16[80,2304]{1,0:T(8,128)(2,1)}, bf16[80,230...) custom-call(bf16[80,2304]{1,0:T(8,128)(2,1)} %bitcast.23, ...), custom_call_target="tpu_custom_call" | custom-call | flops 3185049600 | bytes 10874880 | tf_op jit(solution)/shard_map/expert/pallas_call | solution.py:305
  139.9 2.7 %collective-permute-start.22 = (bf16[80,2304]{1,0:T(8,128)(2,1)S(1)}, bf16[80,2304]{1,0:T(8,128)(2,1)S(1)}, u32[]{:S(2)}, u32[]{:S(2)}) collective-permute-start(bf16[80,2304]{1,0:T(8,128)(2,1)S(1)} %add_convert_fusion.2), channel_id=1, source_target_pairs={{0,96},{8,104},{16,112},{24,120},{32,0},{40,8},{48,16},{56,24},{64... | collective-permute-start | bytes 1105928 | tf_op jit(solution)/shard_map/ppermute | solution.py:408
  143.9 2.7 %collective-permute-start.29 = (bf16[80,2304]{1,0:T(8,128)(2,1)S(1)}, bf16[80,2304]{1,0:T(8,128)(2,1)S(1)}, u32[]{:S(2)}, u32[]{:S(2)}) collective-permute-start(bf16[80,2304]{1,0:T(8,128)(2,1)S(1)} %add_convert_fusion), channel_id=1, source_target_pairs={{0,24},{8,0},{16,8},{24,16},{32,56},{40,32},{48,40},{56,48},{64,88... | collective-permute-start | bytes 1105928 | tf_op jit(solution)/shard_map/ppermute | solution.py:408
  152.1 2.1 %collective-permute-start.30 = (bf16[40,2304]{1,0:T(8,128)(2,1)S(1)}, bf16[40,2304]{1,0:T(8,128)(2,1)S(1)}, u32[]{:S(2)}, u32[]{:S(2)}) collective-permute-start(bf16[40,2304]{1,0:T(8,128)(2,1)S(1)} %get-tuple-element.87), channel_id=1, source_target_pairs={{0,64},{8,72},{16,80},{24,88},{32,96},{40,104},{48,112},{56,120},{... | collective-permute-start | bytes 552968 | tf_op jit(solution)/shard_map/ppermute | solution.py:408
  154.2 2.4 %collective-permute-start.31 = (bf16[40,2304]{1,0:T(8,128)(2,1)S(1)}, bf16[40,2304]{1,0:T(8,128)(2,1)S(1)}, u32[]{:S(2)}, u32[]{:S(2)}) collective-permute-start(bf16[40,2304]{1,0:T(8,128)(2,1)S(1)} %get-tuple-element.88), channel_id=1, source_target_pairs={{0,96},{8,104},{16,112},{24,120},{32,0},{40,8},{48,16},{56,24},{64... | collective-permute-start | bytes 552968 | tf_op jit(solution)/shard_map/ppermute | solution.py:408
  156.7 2.8 %collective-permute-done.24.refs_2_ = bf16[40,2304]{1,0:T(8,128)(2,1)S(1)} collective-permute-done((bf16[40,2304]{1,0:T(8,128)(2,1)S(1)}, bf16[40,2304]{1,0:T(8,128)(2,1)S(1)}, u32[]{:S(2)}, u32[]{:S(2)}) %collective-permute-start.24) | collective-permute-done | bytes 184352 | tf_op jit(solution)/shard_map/ppermute | solution.py:408
  162.8 20.7 %all_to_all.25 = bf16[8,80,288]{2,1,0:T(8,128)(2,1)S(1)} all-to-all(bf16[8,80,288]{2,1,0:T(8,128)(2,1)S(1)} %finish.1), channel_id=1, replica_groups=mesh['wide'=16,'narrow'=8] {'narrow'}, dimensions={0} | all-to-all | bytes 737280 | tf_op jit(solution)/shard_map/all_to_all | solution.py:433
  (119 shorter events, 26.3 us)
Async XLA Ops:
  0.0 28.9 %all-to-all-start = ((bf16[8,288,360]{2,1,0:T(8,128)(2,1)}), bf16[8,288,360]{2,1,0:T(8,128)(2,1)}, u32[]{:S(2)}, u32[]{:S(2)}) async-start(bf16[8,288,360]{2,1,0:T(8,128)(2,1)} %bitcast.33), calls=%async_computation | async-start | bytes 3538944 | tf_op jit(solution)/shard_map/all_to_all | solution.py:433
  28.9 14.1 %all-to-all-start.1 = ((bf16[4,304,256]{2,1,0:T(8,128)(2,1)}), bf16[4,304,256]{2,1,0:T(8,128)(2,1)S(1)}, u32[]{:S(2)}, u32[]{:S(2)}) async-start(bf16[4,304,256]{2,1,0:T(8,128)(2,1)} %merge.1), calls=%async_computation.1 | async-start | bytes 1245184 | tf_op jit(solution)/shard_map/all_to_all | solution.py:445
  45.2 13.9 %all-to-all-start.2 = ((bf16[8,80,384]{2,1,0:T(8,128)(2,1)}), bf16[8,80,384]{2,1,0:T(8,128)(2,1)S(1)}, u32[]{:S(2)}, u32[]{:S(2)}) async-start(bf16[8,80,384]{2,1,0:T(8,128)(2,1)} %get-tuple-element.53), calls=%async_computation.2 | async-start | bytes 983040 | tf_op jit(solution)/shard_map/all_to_all | solution.py:433
  59.1 50.9 %all-to-all-start.3 = ((bf16[8,288,768]{2,1,0:T(8,128)(2,1)}), bf16[8,288,768]{2,1,0:T(8,128)(2,1)}, u32[]{:S(2)}, u32[]{:S(2)}) async-start(bf16[8,288,768]{2,1,0:T(8,128)(2,1)} %fusion.2), calls=%async_computation.3 | async-start | bytes 7077888 | tf_op jit(solution)/shard_map/all_to_all | solution.py:433
  64.8 7.9 %collective-permute-start.3 = (bf16[40,2304]{1,0:T(8,128)(2,1)S(1)}, bf16[40,2304]{1,0:T(8,128)(2,1)S(1)}, u32[]{:S(2)}, u32[]{:S(2)}) collective-permute-start(bf16[40,2304]{1,0:T(8,128)(2,1)S(1)} %get-tuple-element.94.refs_0_), channel_id=1, source_target_pairs={{0,24},{8,0},{16,8},{24,16},{32,56},{40,32},{48,40},{56,48},{64,88... | collective-permute-start | bytes 552968 | tf_op jit(solution)/shard_map/ppermute | solution.py:408
  68.6 10.9 %collective-permute-start.2 = (bf16[40,2304]{1,0:T(8,128)(2,1)S(1)}, bf16[40,2304]{1,0:T(8,128)(2,1)S(1)}, u32[]{:S(2)}, u32[]{:S(2)}) collective-permute-start(bf16[40,2304]{1,0:T(8,128)(2,1)S(1)} %get-tuple-element.94.refs_0_), channel_id=1, source_target_pairs={{0,8},{8,16},{16,24},{24,0},{32,40},{40,48},{48,56},{56,32},{64,72... | collective-permute-start | bytes 552968 | tf_op jit(solution)/shard_map/ppermute | solution.py:408
  68.6 10.9 %collective-permute-start.1 = (bf16[40,2304]{1,0:T(8,128)(2,1)S(1)}, bf16[40,2304]{1,0:T(8,128)(2,1)S(1)}, u32[]{:S(2)}, u32[]{:S(2)}) collective-permute-start(bf16[40,2304]{1,0:T(8,128)(2,1)S(1)} %get-tuple-element.94.refs_0_), channel_id=1, source_target_pairs={{0,16},{8,24},{16,0},{24,8},{32,48},{40,56},{48,32},{56,40},{64,80... | collective-permute-start | bytes 552968 | tf_op jit(solution)/shard_map/ppermute | solution.py:408
  70.0 12.5 %collective-permute-start.10 = (bf16[40,2304]{1,0:T(8,128)(2,1)S(1)}, bf16[40,2304]{1,0:T(8,128)(2,1)S(1)}, u32[]{:S(2)}, u32[]{:S(2)}) collective-permute-start(bf16[40,2304]{1,0:T(8,128)(2,1)S(1)} %get-tuple-element.93.refs_0_), channel_id=1, source_target_pairs={{0,96},{8,104},{16,112},{24,120},{32,0},{40,8},{48,16},{56,24},{64... | collective-permute-start | bytes 552968 | tf_op jit(solution)/shard_map/ppermute | solution.py:408
  72.7 9.8 %collective-permute-start.9 = (bf16[40,2304]{1,0:T(8,128)(2,1)S(1)}, bf16[40,2304]{1,0:T(8,128)(2,1)S(1)}, u32[]{:S(2)}, u32[]{:S(2)}) collective-permute-start(bf16[40,2304]{1,0:T(8,128)(2,1)S(1)} %get-tuple-element.93.refs_0_), channel_id=1, source_target_pairs={{0,32},{8,40},{16,48},{24,56},{32,64},{40,72},{48,80},{56,88},{64,... | collective-permute-start | bytes 552968 | tf_op jit(solution)/shard_map/ppermute | solution.py:408
  72.7 9.8 %collective-permute-start.8 = (bf16[40,2304]{1,0:T(8,128)(2,1)S(1)}, bf16[40,2304]{1,0:T(8,128)(2,1)S(1)}, u32[]{:S(2)}, u32[]{:S(2)}) collective-permute-start(bf16[40,2304]{1,0:T(8,128)(2,1)S(1)} %get-tuple-element.93.refs_0_), channel_id=1, source_target_pairs={{0,64},{8,72},{16,80},{24,88},{32,96},{40,104},{48,112},{56,120},{... | collective-permute-start | bytes 552968 | tf_op jit(solution)/shard_map/ppermute | solution.py:408
  79.7 11.6 %collective-permute-start.6 = (bf16[80,2304]{1,0:T(8,128)(2,1)S(1)}, bf16[80,2304]{1,0:T(8,128)(2,1)S(1)}, u32[]{:S(2)}, u32[]{:S(2)}) collective-permute-start(bf16[80,2304]{1,0:T(8,128)(2,1)S(1)} %bitcast.24), channel_id=1, source_target_pairs={{0,96},{8,104},{16,112},{24,120},{32,0},{40,8},{48,16},{56,24},{64... | collective-permute-start | bytes 1105928 | tf_op jit(solution)/shard_map/ppermute | solution.py:408
  82.5 12.3 %collective-permute-start.4 = (bf16[80,2304]{1,0:T(8,128)(2,1)S(1)}, bf16[80,2304]{1,0:T(8,128)(2,1)S(1)}, u32[]{:S(2)}, u32[]{:S(2)}) collective-permute-start(bf16[80,2304]{1,0:T(8,128)(2,1)S(1)} %bitcast.21), channel_id=1, source_target_pairs={{0,32},{8,40},{16,48},{24,56},{32,64},{40,72},{48,80},{56,88},{64,... | collective-permute-start | bytes 1105928 | tf_op jit(solution)/shard_map/ppermute | solution.py:408
  82.6 12.2 %collective-permute-start.13 = (bf16[80,2304]{1,0:T(8,128)(2,1)S(1)}, bf16[80,2304]{1,0:T(8,128)(2,1)S(1)}, u32[]{:S(2)}, u32[]{:S(2)}) collective-permute-start(bf16[80,2304]{1,0:T(8,128)(2,1)S(1)} %bitcast.30), channel_id=1, source_target_pairs={{0,24},{8,0},{16,8},{24,16},{32,56},{40,32},{48,40},{56,48},{64,88... | collective-permute-start | bytes 1105928 | tf_op jit(solution)/shard_map/ppermute | solution.py:408
  86.9 12.0 %collective-permute-start.11 = (bf16[80,2304]{1,0:T(8,128)(2,1)S(1)}, bf16[80,2304]{1,0:T(8,128)(2,1)S(1)}, u32[]{:S(2)}, u32[]{:S(2)}) collective-permute-start(bf16[80,2304]{1,0:T(8,128)(2,1)S(1)} %bitcast.27), channel_id=1, source_target_pairs={{0,8},{8,16},{16,24},{24,0},{32,40},{40,48},{48,56},{56,32},{64,72... | collective-permute-start | bytes 1105928 | tf_op jit(solution)/shard_map/ppermute | solution.py:408
  91.2 10.3 %collective-permute-start.7 = (bf16[80,2304]{1,0:T(8,128)(2,1)S(1)}, bf16[80,2304]{1,0:T(8,128)(2,1)S(1)}, u32[]{:S(2)}, u32[]{:S(2)}) collective-permute-start(bf16[80,2304]{1,0:T(8,128)(2,1)S(1)} %collective-permute-done.6.refs_1_), channel_id=1, source_target_pairs={{0,96},{8,104},{16,112},{24,120},{32,0},{40,8},{48,16},{56,24},{64... | collective-permute-start | bytes 1105928 | tf_op jit(solution)/shard_map/ppermute | solution.py:408
  94.8 10.3 %collective-permute-start.5 = (bf16[80,2304]{1,0:T(8,128)(2,1)S(1)}, bf16[80,2304]{1,0:T(8,128)(2,1)S(1)}, u32[]{:S(2)}, u32[]{:S(2)}) collective-permute-start(bf16[80,2304]{1,0:T(8,128)(2,1)S(1)} %collective-permute-done.4.refs_3_), channel_id=1, source_target_pairs={{0,32},{8,40},{16,48},{24,56},{32,64},{40,72},{48,80},{56,88},{64,... | collective-permute-start | bytes 1105928 | tf_op jit(solution)/shard_map/ppermute | solution.py:408
  94.8 11.4 %collective-permute-start.14 = (bf16[80,2304]{1,0:T(8,128)(2,1)S(1)}, bf16[80,2304]{1,0:T(8,128)(2,1)S(1)}, u32[]{:S(2)}, u32[]{:S(2)}) collective-permute-start(bf16[80,2304]{1,0:T(8,128)(2,1)S(1)} %collective-permute-done.13.refs_5_), channel_id=1, source_target_pairs={{0,24},{8,0},{16,8},{24,16},{32,56},{40,32},{48,40},{56,48},{64,88... | collective-permute-start | bytes 1105928 | tf_op jit(solution)/shard_map/ppermute | solution.py:408
  98.9 11.1 %collective-permute-start.12 = (bf16[80,2304]{1,0:T(8,128)(2,1)S(1)}, bf16[80,2304]{1,0:T(8,128)(2,1)}, u32[]{:S(2)}, u32[]{:S(2)}) collective-permute-start(bf16[80,2304]{1,0:T(8,128)(2,1)S(1)} %collective-permute-done.11.refs_7_), channel_id=1, source_target_pairs={{0,8},{8,16},{16,24},{24,0},{32,40},{40,48},{48,56},{56,32},{64,72... | collective-permute-start | bytes 1105928 | tf_op jit(solution)/shard_map/ppermute | solution.py:408
  98.9 21.5 %collective-permute-start.16 = (bf16[80,2304]{1,0:T(8,128)(2,1)S(1)}, bf16[80,2304]{1,0:T(8,128)(2,1)}, u32[]{:S(2)}, u32[]{:S(2)}) collective-permute-start(bf16[80,2304]{1,0:T(8,128)(2,1)S(1)} %bitcast.25), channel_id=1, source_target_pairs={{0,32},{8,40},{16,48},{24,56},{32,64},{40,72},{48,80},{56,88},{64,... | collective-permute-start | bytes 1105928 | tf_op jit(solution)/shard_map/ppermute | solution.py:408
  101.6 18.9 %collective-permute-start.15 = (bf16[80,2304]{1,0:T(8,128)(2,1)S(1)}, bf16[80,2304]{1,0:T(8,128)(2,1)}, u32[]{:S(2)}, u32[]{:S(2)}) collective-permute-start(bf16[80,2304]{1,0:T(8,128)(2,1)S(1)} %bitcast.22), channel_id=1, source_target_pairs={{0,96},{8,104},{16,112},{24,120},{32,0},{40,8},{48,16},{56,24},{64... | collective-permute-start | bytes 1105928 | tf_op jit(solution)/shard_map/ppermute | solution.py:408
  105.1 15.3 %collective-permute-start.18 = (bf16[80,2304]{1,0:T(8,128)(2,1)S(1)}, bf16[80,2304]{1,0:T(8,128)(2,1)}, u32[]{:S(2)}, u32[]{:S(2)}) collective-permute-start(bf16[80,2304]{1,0:T(8,128)(2,1)S(1)} %bitcast.31), channel_id=1, source_target_pairs={{0,8},{8,16},{16,24},{24,0},{32,40},{40,48},{48,56},{56,32},{64,72... | collective-permute-start | bytes 1105928 | tf_op jit(solution)/shard_map/ppermute | solution.py:408
  106.2 14.3 %collective-permute-start.17 = (bf16[80,2304]{1,0:T(8,128)(2,1)S(1)}, bf16[80,2304]{1,0:T(8,128)(2,1)}, u32[]{:S(2)}, u32[]{:S(2)}) collective-permute-start(bf16[80,2304]{1,0:T(8,128)(2,1)S(1)} %bitcast.28), channel_id=1, source_target_pairs={{0,24},{8,0},{16,8},{24,16},{32,56},{40,32},{48,40},{56,48},{64,88... | collective-permute-start | bytes 1105928 | tf_op jit(solution)/shard_map/ppermute | solution.py:408
  120.4 17.0 %collective-permute-start.19 = (bf16[160,2304]{1,0:T(8,128)(2,1)}, bf16[160,2304]{1,0:T(8,128)(2,1)S(1)}, u32[]{:S(2)}, u32[]{:S(2)}) collective-permute-start(bf16[160,2304]{1,0:T(8,128)(2,1)} %get-tuple-element.72), channel_id=1, source_target_pairs={{0,32},{8,40},{16,48},{24,56},{32,64},{40,72},{48,80},{56,88},{64,... | collective-permute-start | bytes 2211848 | tf_op jit(solution)/shard_map/ppermute | solution.py:408
  120.5 18.2 %collective-permute-start.21 = (bf16[160,2304]{1,0:T(8,128)(2,1)}, bf16[160,2304]{1,0:T(8,128)(2,1)}, u32[]{:S(2)}, u32[]{:S(2)}) collective-permute-start(bf16[160,2304]{1,0:T(8,128)(2,1)} %get-tuple-element.73), channel_id=1, source_target_pairs={{0,96},{8,104},{16,112},{24,120},{32,0},{40,8},{48,16},{56,24},{64... | collective-permute-start | bytes 2211848 | tf_op jit(solution)/shard_map/ppermute | solution.py:408
  123.2 19.4 %collective-permute-start.26 = (bf16[160,2304]{1,0:T(8,128)(2,1)}, bf16[160,2304]{1,0:T(8,128)(2,1)S(1)}, u32[]{:S(2)}, u32[]{:S(2)}) collective-permute-start(bf16[160,2304]{1,0:T(8,128)(2,1)} %get-tuple-element.82), channel_id=1, source_target_pairs={{0,8},{8,16},{16,24},{24,0},{32,40},{40,48},{48,56},{56,32},{64,72... | collective-permute-start | bytes 2211848 | tf_op jit(solution)/shard_map/ppermute | solution.py:408
  123.2 20.6 %collective-permute-start.28 = (bf16[160,2304]{1,0:T(8,128)(2,1)}, bf16[160,2304]{1,0:T(8,128)(2,1)S(1)}, u32[]{:S(2)}, u32[]{:S(2)}) collective-permute-start(bf16[160,2304]{1,0:T(8,128)(2,1)} %get-tuple-element.83), channel_id=1, source_target_pairs={{0,24},{8,0},{16,8},{24,16},{32,56},{40,32},{48,40},{56,48},{64,88... | collective-permute-start | bytes 2211848 | tf_op jit(solution)/shard_map/ppermute | solution.py:408
  138.6 8.0 %collective-permute-start.20 = (bf16[80,2304]{1,0:T(8,128)(2,1)S(1)}, bf16[80,2304]{1,0:T(8,128)(2,1)S(1)}, u32[]{:S(2)}, u32[]{:S(2)}) collective-permute-start(bf16[80,2304]{1,0:T(8,128)(2,1)S(1)} %add_convert_fusion.3), channel_id=1, source_target_pairs={{0,32},{8,40},{16,48},{24,56},{32,64},{40,72},{48,80},{56,88},{64,... | collective-permute-start | bytes 1105928 | tf_op jit(solution)/shard_map/ppermute | solution.py:408
  143.7 8.1 %collective-permute-start.27 = (bf16[80,2304]{1,0:T(8,128)(2,1)S(1)}, bf16[80,2304]{1,0:T(8,128)(2,1)S(1)}, u32[]{:S(2)}, u32[]{:S(2)}) collective-permute-start(bf16[80,2304]{1,0:T(8,128)(2,1)S(1)} %add_convert_fusion.1), channel_id=1, source_target_pairs={{0,8},{8,16},{16,24},{24,0},{32,40},{40,48},{48,56},{56,32},{64,72... | collective-permute-start | bytes 1105928 | tf_op jit(solution)/shard_map/ppermute | solution.py:408
  143.9 7.9 %collective-permute-start.29 = (bf16[80,2304]{1,0:T(8,128)(2,1)S(1)}, bf16[80,2304]{1,0:T(8,128)(2,1)S(1)}, u32[]{:S(2)}, u32[]{:S(2)}) collective-permute-start(bf16[80,2304]{1,0:T(8,128)(2,1)S(1)} %add_convert_fusion), channel_id=1, source_target_pairs={{0,24},{8,0},{16,8},{24,16},{32,56},{40,32},{48,40},{56,48},{64,88... | collective-permute-start | bytes 1105928 | tf_op jit(solution)/shard_map/ppermute | solution.py:408
  148.5 8.2 %collective-permute-start.23 = (bf16[40,2304]{1,0:T(8,128)(2,1)S(1)}, bf16[40,2304]{1,0:T(8,128)(2,1)S(1)}, u32[]{:S(2)}, u32[]{:S(2)}) collective-permute-start(bf16[40,2304]{1,0:T(8,128)(2,1)S(1)} %get-tuple-element.77), channel_id=1, source_target_pairs={{0,16},{8,24},{16,0},{24,8},{32,48},{40,56},{48,32},{56,40},{64,80... | collective-permute-start | bytes 552968 | tf_op jit(solution)/shard_map/ppermute | solution.py:408
  150.3 9.2 %collective-permute-start.24 = (bf16[40,2304]{1,0:T(8,128)(2,1)S(1)}, bf16[40,2304]{1,0:T(8,128)(2,1)S(1)}, u32[]{:S(2)}, u32[]{:S(2)}) collective-permute-start(bf16[40,2304]{1,0:T(8,128)(2,1)S(1)} %get-tuple-element.78), channel_id=1, source_target_pairs={{0,24},{8,0},{16,8},{24,16},{32,56},{40,32},{48,40},{56,48},{64,88... | collective-permute-start | bytes 552968 | tf_op jit(solution)/shard_map/ppermute | solution.py:408
  150.3 9.4 %collective-permute-start.25 = (bf16[40,2304]{1,0:T(8,128)(2,1)S(1)}, bf16[40,2304]{1,0:T(8,128)(2,1)S(1)}, u32[]{:S(2)}, u32[]{:S(2)}) collective-permute-start(bf16[40,2304]{1,0:T(8,128)(2,1)S(1)} %get-tuple-element.79), channel_id=1, source_target_pairs={{0,8},{8,16},{16,24},{24,0},{32,40},{40,48},{48,56},{56,32},{64,72... | collective-permute-start | bytes 552968 | tf_op jit(solution)/shard_map/ppermute | solution.py:408
  (27 other events, 437.0 us)

commit v3 on v2

--- a/solution.py
+++ b/solution.py
@@ -127,11 +127,13 @@
     )(table, length, place, queries, cache_pool, cache_pool, new_kv, new_kv)
 
 
-def merge_kernel(place, own_ref, other_ref, out_ref, spread_sc, *, share):
+def merge_kernel(place, own_ref, other_ref, *refs, share):
+    outs, spread_sc = refs[:-1], refs[-1]
     tokens = own_ref.shape[2]
     offset = pl.multiple_of(place[0] % 2 * (HD // 2), HD // 2)
     both = (own_ref, other_ref)
-    for dest in range(own_ref.shape[0]):
+    for step, out_ref in enumerate(outs):
+        dest = (place[0] // 2 + step) % len(outs)
         tops = [ref[dest, share : share + 8, :].astype(F32) for ref in both]
         top = jnp.maximum(*tops)
         scales = [jnp.exp(t - top) for t in tops]
@@ -142,8 +144,8 @@
                 spread_sc[side, head * HD : head * HD + HD, :] = jnp.broadcast_to(scales[side][head : head + 1, :], (HD, tokens))
             term = ref[dest, :share, :].astype(F32) * spread_sc[side, pl.ds(offset, share), :]
             total = term if total is None else total + term
-        out_ref[dest, :share, :] = total.astype(BF16)
-        out_ref[dest, share:, :] = jnp.concatenate([top, den], axis=0).astype(BF16)
+        out_ref[:share, :] = total.astype(BF16)
+        out_ref[share:, :] = jnp.concatenate([top, den], axis=0).astype(BF16)
 
 
 def merge(place, own, other):
@@ -155,92 +157,87 @@
             num_scalar_prefetch=1,
             grid=(1,),
             in_specs=[whole, whole],
-            out_specs=whole,
+            out_specs=[pl.BlockSpec((rows, tokens), lambda i, *_: (0, 0))] * dests,
             scratch_shapes=[pltpu.VMEM((2, 5 * HD, tokens), F32)],
         ),
-        out_shape=jax.ShapeDtypeStruct(own.shape, BF16),
+        out_shape=[jax.ShapeDtypeStruct((rows, tokens), BF16)] * dests,
         cost_estimate=pl.CostEstimate(flops=4 * own.size, bytes_accessed=6 * own.size, transcendentals=0),
         compiler_params=pltpu.CompilerParams(vmem_limit_bytes=10 << 20),
         name="merge",
     )(place, own, other)
 
 
-def join_kernel(place, recv_ref, res_ref, gain_ref, slot_ref, placed_ref, hidden_ref, spread_sc, *, share):
-    groups = recv_ref.shape[0]
-    tokens = recv_ref.shape[2]
-    slots = placed_ref.shape[0] * placed_ref.shape[1]
-    padded = placed_ref.shape[2]
-    tops = [recv_ref[g, share : share + 8, :].astype(F32) for g in range(groups)]
+def join_kernel(place, *refs, share, groups):
+    recv_refs, (res_ref, gain_ref, slot_ref) = refs[:groups], refs[groups : groups + 3]
+    outs, (hidden_ref, spread_sc) = refs[groups + 3 : -2], refs[-2:]
+    tokens = hidden_ref.shape[1]
+    rows, padded = outs[0].shape
+    slots = len(outs) * rows
+    tops = [ref[share : share + 8, :].astype(F32) for ref in recv_refs]
     top = functools.reduce(jnp.maximum, tops)
     scales = [jnp.exp(t - top) for t in tops]
-    den = functools.reduce(jnp.add, [s * recv_ref[g, share + 8 : share + 16, :].astype(F32) for g, s in enumerate(scales)])
+    den = functools.reduce(jnp.add, [s * ref[share + 8 : share + 16, :].astype(F32) for s, ref in zip(scales, recv_refs)])
     offset = pl.multiple_of(place[0] % 2 * (HD // 2), HD // 2)
     total = res_ref[...]
-    for g in range(groups):
+    for g, ref in enumerate(recv_refs):
         factor = scales[g] / den
         for head in range(5):
             spread_sc[g, head * HD : head * HD + HD, :] = jnp.broadcast_to(factor[head : head + 1, :], (HD, tokens))
-        total = total + recv_ref[g, :share, :].astype(F32) * spread_sc[g, pl.ds(offset, share), :]
+        total = total + ref[:share, :].astype(F32) * spread_sc[g, pl.ds(offset, share), :]
     hidden_ref[...] = total
     square = jnp.sum(total * total, axis=0, keepdims=True)
     high = square.astype(BF16).astype(F32)
     row = lax.broadcasted_iota(jnp.int32, (padded - share, tokens), 0)
     tail = jnp.where(row == 0, high, jnp.where(row == 1, square - high, 0.0)).astype(BF16)
-    rows = jnp.concatenate([(total * gain_ref[...]).astype(BF16), tail], axis=0)
-    at = lax.broadcasted_iota(jnp.int32, (slots, tokens), 0)
+    filled = jnp.concatenate([(total * gain_ref[...]).astype(BF16), tail], axis=0)
+    at = lax.broadcasted_iota(jnp.int32, (slots, tokens), 0) + place[0] * rows
+    at = jnp.where(at < slots, at, at - slots)
     picks = (at == slot_ref[0:1, :]) | (at == slot_ref[1:2, :])
-    placed = nt_dot(jnp.where(picks, 1.0, 0.0).astype(BF16), rows)
-    placed_ref[...] = placed.astype(BF16).reshape(placed_ref.shape)
+    placed = nt_dot(jnp.where(picks, 1.0, 0.0).astype(BF16), filled).astype(BF16)
+    for i, out in enumerate(outs):
+        out[...] = placed[i * rows : i * rows + rows]
 
 
 def join(place, recv, residual, gain, slots, experts):
-    groups, rows, tokens = recv.shape
+    rows, tokens = recv[0].shape
     share = rows - STAT_ROWS
     padded = -(-(share + 2) // 128) * 128
     whole = lambda *shape: pl.BlockSpec(shape, lambda i, *_: (0,) * len(shape))
     return pl.pallas_call(
-        functools.partial(join_kernel, share=share),
+        functools.partial(join_kernel, share=share, groups=len(recv)),
         grid_spec=pltpu.PrefetchScalarGridSpec(
             num_scalar_prefetch=1,
             grid=(1,),
-            in_specs=[
-                whole(groups, rows, tokens),
-                whole(share, tokens),
-                whole(share, 1),
-                whole(2, tokens),
-            ],
-            out_specs=[whole(experts, CAP, padded), whole(share, tokens)],
-            scratch_shapes=[pltpu.VMEM((groups, 5 * HD, tokens), F32)],
-        ),
-        out_shape=[
-            jax.ShapeDtypeStruct((experts, CAP, padded), BF16),
-            jax.ShapeDtypeStruct((share, tokens), F32),
-        ],
+            in_specs=[whole(rows, tokens)] * len(recv) + [whole(share, tokens), whole(share, 1), whole(2, tokens)],
+            out_specs=[whole(CAP, padded)] * experts + [whole(share, tokens)],
+            scratch_shapes=[pltpu.VMEM((len(recv), 5 * HD, tokens), F32)],
+        ),
+        out_shape=[jax.ShapeDtypeStruct((CAP, padded), BF16)] * experts + [jax.ShapeDtypeStruct((share, tokens), F32)],
         cost_estimate=pl.CostEstimate(
-            flops=2 * experts * CAP * padded * tokens, bytes_accessed=recv.size * 2 + experts * CAP * padded * 2, transcendentals=0
+            flops=2 * experts * CAP * padded * tokens, bytes_accessed=8 * rows * tokens + experts * CAP * padded * 2, transcendentals=0
         ),
         compiler_params=pltpu.CompilerParams(vmem_limit_bytes=10 << 20),
         name="join",
-    )(place, recv, residual, gain, slots)
-
-
-def norm_kernel(recv_ref, out_ref, *, share):
-    groups, _, _ = recv_ref.shape
-    blocks = [recv_ref[g].astype(F32) for g in range(groups)]
+    )(place, *recv, residual, gain, slots)
+
+
+def norm_kernel(*refs, share):
+    recv_refs, out_ref = refs[:-1], refs[-1]
+    blocks = [ref[...].astype(F32) for ref in recv_refs]
     square = functools.reduce(jnp.add, [b[:, share : share + 1] + b[:, share + 1 : share + 2] for b in blocks])
-    scale = lax.rsqrt(square / (groups * share) + EPSILON)
+    scale = lax.rsqrt(square / (len(blocks) * share) + EPSILON)
     out_ref[...] = jnp.concatenate([b[:, :share] * scale for b in blocks], axis=1).astype(BF16)
 
 
 def norm_rows(recv, share):
-    groups, rows, _ = recv.shape
+    rows, padded = recv[0].shape
     return pl.pallas_call(
         functools.partial(norm_kernel, share=share),
-        out_shape=jax.ShapeDtypeStruct((rows, groups * share), BF16),
-        cost_estimate=pl.CostEstimate(flops=0, bytes_accessed=recv.size * 4, transcendentals=0),
+        out_shape=jax.ShapeDtypeStruct((rows, len(recv) * share), BF16),
+        cost_estimate=pl.CostEstimate(flops=0, bytes_accessed=len(recv) * rows * padded * 4, transcendentals=0),
         compiler_params=pltpu.CompilerParams(vmem_limit_bytes=4 << 20),
         name="norm_rows",
-    )(recv)
+    )(*recv)
 
 
 def stack_kernel(*refs):
@@ -261,14 +258,17 @@
     return [pair.reshape(2 * rows, width) for pair in pairs]
 
 
-def expert_kernel(*refs, count):
+def expert_kernel(place, *refs, count):
     blocks, gate_up_hbm, down_hbm = refs[:count], refs[count], refs[count + 1]
     outs, (x_sc, gate_up_sc, down_sc, both_sc, y_sc, sems) = refs[count + 2 : -6], refs[-6:]
     rows, out_rows, units = blocks[0].shape[0], outs[0].shape[0], down_sc.shape[1]
     half = gate_up_sc.shape[1] // 2
     tile = 256
     loads = [pltpu.make_async_copy(b, x_sc.at[pl.ds(i * rows, rows)], sems.at[i]) for i, b in enumerate(blocks)]
-    loads.append(pltpu.make_async_copy(gate_up_hbm, gate_up_sc, sems.at[count]))
+    groups, share = gate_up_hbm.shape[:2]
+    for g in range(groups):
+        source = (place[0] + groups - g) % groups
+        loads.append(pltpu.make_async_copy(gate_up_hbm.at[source], gate_up_sc.at[pl.ds(g * share, share)], sems.at[count + 2 + len(outs) + g]))
     down_load = pltpu.make_async_copy(down_hbm, down_sc, sems.at[count + 1])
     for load in (*loads, down_load):
         load.start()
@@ -296,7 +296,7 @@
         pltpu.make_async_copy(y_sc.at[pl.ds(i * out_rows, out_rows)], out, sems.at[count + 2 + i]).wait()
 
 
-def expert(blocks, gate_up, down, out_rows):
+def expert(place, blocks, gate_up, down, out_rows):
     rows, width = blocks[0].shape
     units = down.shape[1]
     count = len(blocks)
@@ -304,16 +304,16 @@
     anywhere = pl.BlockSpec(memory_space=pltpu.HBM)
     return pl.pallas_call(
         functools.partial(expert_kernel, count=count),
-        in_specs=[anywhere] * (count + 2),
+        in_specs=[pl.BlockSpec(memory_space=pltpu.SMEM)] + [anywhere] * (count + 2),
         out_specs=[anywhere] * (total // out_rows),
         out_shape=[jax.ShapeDtypeStruct((out_rows, width), BF16)] * (total // out_rows),
         scratch_shapes=[
             pltpu.VMEM((total, width), BF16),
-            pltpu.VMEM(gate_up.shape, BF16),
+            pltpu.VMEM((width, gate_up.shape[2]), BF16),
             pltpu.VMEM(down.shape, BF16),
-            pltpu.VMEM((total, gate_up.shape[1]), F32),
+            pltpu.VMEM((total, gate_up.shape[2]), F32),
             pltpu.VMEM((total, width), BF16),
-            pltpu.SemaphoreType.DMA((count + 2 + total // out_rows,)),
+            pltpu.SemaphoreType.DMA((count + 2 + total // out_rows + gate_up.shape[0],)),
         ],
         cost_estimate=pl.CostEstimate(
             flops=6 * total * width * units,
@@ -322,7 +322,7 @@
         ),
         compiler_params=pltpu.CompilerParams(vmem_limit_bytes=60 << 20),
         name="expert",
-    )(*blocks, gate_up, down)
+    )(place, *blocks, gate_up, down)
 
 
 def total_of(refs):
@@ -435,14 +435,17 @@
     down_all = exchange(jnp.transpose(w_down, (0, 2, 1)))
     place = narrow_pos.reshape(1)
     own, other = attend(page_table, cached_len, place, queries, cache_pool, new_kv, narrow_count)
-    own, w_gate_up = lax.optimization_barrier((own, w_gate_up))
-    padding = ((0, 0), (0, 0), (0, -units % 128))
-    later = jnp.concatenate([jnp.pad(w_gate_up[:, :, 0], padding), jnp.pad(w_gate_up[:, :, 1], padding)], axis=2)
     other = lax.ppermute(other, "narrow", [(i, i ^ 1) for i in range(narrow_count)])
-    sums = merge(place, own, other)
-    sums, down_all = lax.optimization_barrier((sums, down_all))
-    chips = [[2 * x + core for x in range(narrow_count // 2)] for core in range(2)]
-    sums = lax.all_to_all(sums, "narrow", 0, 0, axis_index_groups=chips, tiled=True)
+
+    def along(x, step):
+        return lax.ppermute(x, "narrow", [(i, (i + step) % narrow_count) for i in range(narrow_count)])
+
+    merged = list(merge(place, own, other))
+    w_gate_up, down_all, merged[0] = lax.optimization_barrier((w_gate_up, down_all, merged[0]))
+    sums = merged[:1]
+    for step in range(1, len(merged)):
+        sums.append(along(merged[step], 2 * step))
+    gate_up_all = exchange(w_gate_up)
 
     flat_ids = expert_ids.reshape(token_rows * 2)
     onehot = (flat_ids[:, None] == jnp.arange(expert_count, dtype=jnp.int32)[None, :]).astype(BF16)
@@ -453,12 +456,11 @@
 
     res_share = lax.dynamic_slice_in_dim(residual, narrow_pos * share, share, 1).astype(F32).T
     gain_share = lax.dynamic_slice_in_dim(norm_gain, narrow_pos * share, share, 0)[:, None]
-    placed, hidden = join(place, sums, res_share, gain_share, slots.T, expert_count)
-    placed = exchange(placed)
-    later, placed = lax.optimization_barrier((later, placed))
-    later = exchange(later)
-    later, down_all = later.reshape(width, -1), down_all.reshape(width, units)
-    rows = norm_rows(placed, share)
+    *placed, hidden = join(place, sums, res_share, gain_share, slots.T, expert_count)
+    rows = norm_rows([along(x, i) if i else x for i, x in enumerate(placed)], share)
+    gate_up_all = jnp.pad(gate_up_all.reshape(width, 2, units), ((0, 0), (0, 0), (0, -units % 128)))
+    gate_up_all = gate_up_all.reshape(width, -1).reshape(narrow_count, share, -1)
+    down_all = down_all.reshape(width, units)
 
     half = CAP // 2
 
@@ -473,9 +475,9 @@
         far_low, far_high = shift(before_low, second, 1), shift(after_high, second, -1)
         early += [far_low, after_high, far_high, before_low]
         late += [low, high, after_low, before_high]
-    early = list(expert(early, later, down_all, 2 * CAP))
+    early = list(expert(place, early, gate_up_all, down_all, 2 * CAP))
     early[0], *late = lax.optimization_barrier((early[0], *late))
-    late = expert(late, later, down_all, CAP)
+    late = expert(place, late, gate_up_all, down_all, CAP)
 
     def back(blocks, axis):
         return [blocks[0], *(shift(block, axis, -step) for block, step in zip(blocks[1:], STEPS))]

time: 185 us -> 236 us (1.28)
  waiting for transfers between devices: 30.4 us -> 73.2 us
  local copies, waits for them, and re-layouts: 10.1 us -> 20.5 us
  blocking collectives: 20.7 us -> 23.1 us
    ppermute x0 -> x10, waiting for transfers between devices: none -> 45.1 us  [along(): lax.ppermute(x, 'narrow', [(i, (i + step) % narrow_count) for i in range(...]
    ppermute x0 -> x10, starting transfers between devices: none -> 12.8 us  [along(): lax.ppermute(x, 'narrow', [(i, (i + step) % narrow_count) for i in range(...]
    another operation x0 -> x1, local copies, waits for them, and re-layouts: none -> 8.9 us  [local(): gate_up_all.reshape(width, -1).reshape(narrow_count, share, -1)]
    pad x0 -> x1, local copies, waits for them, and re-layouts: none -> 7.36 us  [local(): jnp.pad(gate_up_all.reshape(width, 2, units), ((0, 0), (0, 0), (0, -units...]
    ppermute x32, starting transfers between devices: 51.7 us -> 46.2 us  [shift(): return lax.ppermute(x, 'wide', ring_pairs(axis, step))]
    ppermute x32, waiting for transfers between devices: 19.7 us -> 25 us  [shift(): return lax.ppermute(x, 'wide', ring_pairs(axis, step))]
    all_to_all x3 -> x2, starting transfers between devices: 16.2 us -> 11.4 us  [exchange(): return lax.all_to_all(x, 'narrow', 0, 0, tiled=True)]
    all_to_all x1 -> x0, waiting for transfers between devices: 4.36 us -> none  [local(): lax.all_to_all(sums, 'narrow', 0, 0, axis_index_groups=chips, tiled=True)]
  transfers between devices with their start and end apart: 37 -> 45, of which waited for: 13 -> 23; matrix products, arithmetic and copies ran while one was open for 8% -> 9% of each run, Pallas kernels for 23% -> 18%
where the time goes in v3:
time: 236 us; the launch traced here: 235 us
  waiting for transfers between devices  73.2 us (31%)
  starting transfers between devices  70.4 us (30%)
  Pallas kernels  43.4 us (18%)
  blocking collectives  23.1 us (10%)
  local copies, waits for them, and re-layouts  20.5 us (9%)
  other arithmetic  3.56 us (2%)
    ppermute x32, starting transfers between devices, shift(): return lax.ppermute(x, 'wide', ring_pairs(axis, step))  46.2 us
    ppermute x10, waiting for transfers between devices, along(): lax.ppermute(x, 'narrow', [(i, (i + step) % narrow_count) for i in range(...  45.1 us
    ppermute x32, waiting for transfers between devices, shift(): return lax.ppermute(x, 'wide', ring_pairs(axis, step))  25 us
    all_to_all x1, blocking collectives, exchange(): return lax.all_to_all(x, 'narrow', 0, 0, tiled=True)  23.1 us
    pallas_call x2, Pallas kernels, expert(): pl.pallas_call(functools.partial(expert_kernel, count=count), in_specs=[p...  20.5 us
    pallas_call x1, Pallas kernels, attend(): pl.pallas_call(functools.partial(attend_kernel, share=share), grid_spec=p...  18.1 us
    ppermute x10, starting transfers between devices, along(): lax.ppermute(x, 'narrow', [(i, (i + step) % narrow_count) for i in range(...  12.8 us
    all_to_all x2, starting transfers between devices, exchange(): return lax.all_to_all(x, 'narrow', 0, 0, tiled=True)  11.4 us
  transfers between devices with their start and end apart: 45, of which 23 were waited for; matrix products, arithmetic and copies ran while one was open for 9% of the time, Pallas kernels for 18%

profile of v3, /device:TPU:1, one launch (start us, length us, event | category | flops | bytes accessed | tf_op | source)
XLA Modules:
  0.0 234.8 jit_solution(14380157576832612737)
XLA Ops:
  0.0 5.9 %all-to-all-start = ((bf16[8,288,360]{2,1,0:T(8,128)(2,1)}), bf16[8,288,360]{2,1,0:T(8,128)(2,1)}, u32[]{:S(2)}, u32[]{:S(2)}) async-start(bf16[8,288,360]{2,1,0:T(8,128)(2,1)} %bitcast.29), calls=%async_computation | async-start | bytes 3538944 | tf_op jit(solution)/shard_map/all_to_all | solution.py:433
  5.9 18.1 %attend.1 = (bf16[4,304,256]{2,1,0:T(8,128)(2,1)}, bf16[4,304,256]{2,1,0:T(8,128)(2,1)}) custom-call(s32[2,32]{1,0:T(2,128)} %table.1, s32[2]{0:T(128)} %length.1, s32[1]{0:T(128)} %bitcast.place, bf16[2,128,2304]{2,1,0:T(8,128)(2,1)} %q_ref.1, bf16[2,4,2,128,2304]{4,3,2,1,0:T(8,128)(2,1)} %v_ref.1, bf16[2,4,2,128,2304]{4,3,2,1,0:T(8,128)(2,1)} %v_ref.1, ...), custom_call_target="tpu_custom_call" | custom-call | flops 1245708288 | bytes 10616832 | tf_op jit(solution)/shard_map/attend/pallas_call | solution.py:103
  24.1 2.3 collective-permute-done.other_ref
  28.7 5.5 %all-to-all-start.1 = ((bf16[8,288,2,360]{3,2,1,0:T(2,128)(2,1)}), bf16[8,288,2,360]{3,2,1,0:T(2,128)(2,1)}, u32[]{:S(2)}, u32[]{:S(2)}) async-start(bf16[8,288,2,360]{3,2,1,0:T(2,128)(2,1)} %param.20), calls=%async_computation.1 | async-start | bytes 7077888 | tf_op jit(solution)/shard_map/all_to_all | solution.py:433
  37.6 2.4 %collective-permute-start.2 = (bf16[304,256]{1,0:T(8,128)(2,1)S(1)}, bf16[304,256]{1,0:T(8,128)(2,1)S(1)}, u32[]{:S(2)}, u32[]{:S(2)}) collective-permute-start(bf16[304,256]{1,0:T(8,128)(2,1)S(1)} %get-tuple-element.61), channel_id=1, source_target_pairs={{0,4},{1,5},{2,6},{3,7},{4,0},{5,1},{6,2},{7,3},{8,12},{9,13},{10,... | collective-permute-start | bytes 466952 | tf_op jit(solution)/shard_map/ppermute | solution.py:441
  41.2 37.9 %collective-permute-done.1.refs_1_ = bf16[304,256]{1,0:T(8,128)(2,1)S(1)} collective-permute-done((bf16[304,256]{1,0:T(8,128)(2,1)S(1)}, bf16[304,256]{1,0:T(8,128)(2,1)S(1)}, u32[]{:S(2)}, u32[]{:S(2)}) %collective-permute-start.1) | collective-permute-done | bytes 155680 | tf_op jit(solution)/shard_map/ppermute | solution.py:441
  79.1 3.5 %collective-permute-done.2.refs_2_ = bf16[304,256]{1,0:T(8,128)(2,1)S(1)} collective-permute-done((bf16[304,256]{1,0:T(8,128)(2,1)S(1)}, bf16[304,256]{1,0:T(8,128)(2,1)S(1)}, u32[]{:S(2)}, u32[]{:S(2)}) %collective-permute-start.2) | collective-permute-done | bytes 155680 | tf_op jit(solution)/shard_map/ppermute | solution.py:441
  86.0 2.7 %collective-permute-start.7 = (bf16[80,384]{1,0:T(8,128)(2,1)S(1)}, bf16[80,384]{1,0:T(8,128)(2,1)S(1)}, u32[]{:S(2)}, u32[]{:S(2)}) collective-permute-start(bf16[80,384]{1,0:T(8,128)(2,1)S(1)} %get-tuple-element.67), channel_id=1, source_target_pairs={{0,4},{1,5},{2,6},{3,7},{4,0},{5,1},{6,2},{7,3},{8,12},{9,13},{10,... | collective-permute-start | bytes 184328 | tf_op jit(solution)/shard_map/ppermute | solution.py:441
  88.7 2.6 %collective-permute-start.8 = (bf16[80,384]{1,0:T(8,128)(2,1)S(1)}, bf16[80,384]{1,0:T(8,128)(2,1)S(1)}, u32[]{:S(2)}, u32[]{:S(2)}) collective-permute-start(bf16[80,384]{1,0:T(8,128)(2,1)S(1)} %get-tuple-element.68), channel_id=1, source_target_pairs={{0,5},{1,6},{2,7},{3,0},{4,1},{5,2},{6,3},{7,4},{8,13},{9,14},{10,... | collective-permute-start | bytes 184328 | tf_op jit(solution)/shard_map/ppermute | solution.py:441
  95.9 3.8 %collective-permute-start.13 = (bf16[40,2304]{1,0:T(8,128)(2,1)S(1)}, bf16[40,2304]{1,0:T(8,128)(2,1)S(1)}, u32[]{:S(2)}, u32[]{:S(2)}) collective-permute-start(bf16[40,2304]{1,0:T(8,128)(2,1)S(1)} %get-tuple-element.108.refs_0_), channel_id=1, source_target_pairs={{0,24},{8,0},{16,8},{24,16},{32,56},{40,32},{48,40},{56,48},{64,88... | collective-permute-start | bytes 552968 | tf_op jit(solution)/shard_map/ppermute | solution.py:408
  101.0 2.7 %collective-permute-start.20 = (bf16[40,2304]{1,0:T(8,128)(2,1)S(1)}, bf16[40,2304]{1,0:T(8,128)(2,1)S(1)}, u32[]{:S(2)}, u32[]{:S(2)}) collective-permute-start(bf16[40,2304]{1,0:T(8,128)(2,1)S(1)} %get-tuple-element.107.refs_0_), channel_id=1, source_target_pairs={{0,96},{8,104},{16,112},{24,120},{32,0},{40,8},{48,16},{56,24},{64... | collective-permute-start | bytes 552968 | tf_op jit(solution)/shard_map/ppermute | solution.py:408
  103.7 3.7 %collective-permute-done.13.refs_3_ = bf16[40,2304]{1,0:T(8,128)(2,1)S(1)} collective-permute-done((bf16[40,2304]{1,0:T(8,128)(2,1)S(1)}, bf16[40,2304]{1,0:T(8,128)(2,1)S(1)}, u32[]{:S(2)}, u32[]{:S(2)}) %collective-permute-start.13) | collective-permute-done | bytes 184352 | tf_op jit(solution)/shard_map/ppermute | solution.py:408
  107.5 2.9 %collective-permute-start.18 = (bf16[40,2304]{1,0:T(8,128)(2,1)S(1)}, bf16[40,2304]{1,0:T(8,128)(2,1)S(1)}, u32[]{:S(2)}, u32[]{:S(2)}) collective-permute-start(bf16[40,2304]{1,0:T(8,128)(2,1)S(1)} %get-tuple-element.107.refs_0_), channel_id=1, source_target_pairs={{0,64},{8,72},{16,80},{24,88},{32,96},{40,104},{48,112},{56,120},{... | collective-permute-start | bytes 552968 | tf_op jit(solution)/shard_map/ppermute | solution.py:408
  110.8 2.8 %collective-permute-start.16 = (bf16[80,2304]{1,0:T(8,128)(2,1)S(1)}, bf16[80,2304]{1,0:T(8,128)(2,1)S(1)}, u32[]{:S(2)}, u32[]{:S(2)}) collective-permute-start(bf16[80,2304]{1,0:T(8,128)(2,1)S(1)} %bitcast.20), channel_id=1, source_target_pairs={{0,96},{8,104},{16,112},{24,120},{32,0},{40,8},{48,16},{56,24},{64... | collective-permute-start | bytes 1105928 | tf_op jit(solution)/shard_map/ppermute | solution.py:408
  114.2 3.8 %collective-permute-start.23 = (bf16[80,2304]{1,0:T(8,128)(2,1)S(1)}, bf16[80,2304]{1,0:T(8,128)(2,1)S(1)}, u32[]{:S(2)}, u32[]{:S(2)}) collective-permute-start(bf16[80,2304]{1,0:T(8,128)(2,1)S(1)} %bitcast.26), channel_id=1, source_target_pairs={{0,24},{8,0},{16,8},{24,16},{32,56},{40,32},{48,40},{56,48},{64,88... | collective-permute-start | bytes 1105928 | tf_op jit(solution)/shard_map/ppermute | solution.py:408
  118.0 4.4 %collective-permute-done.16.refs_1_ = bf16[80,2304]{1,0:T(8,128)(2,1)S(1)} collective-permute-done((bf16[80,2304]{1,0:T(8,128)(2,1)S(1)}, bf16[80,2304]{1,0:T(8,128)(2,1)S(1)}, u32[]{:S(2)}, u32[]{:S(2)}) %collective-permute-start.16) | collective-permute-done | bytes 368672 | tf_op jit(solution)/shard_map/ppermute | solution.py:408
  122.4 3.4 %collective-permute-start.17 = (bf16[80,2304]{1,0:T(8,128)(2,1)S(1)}, bf16[80,2304]{1,0:T(8,128)(2,1)S(1)}, u32[]{:S(2)}, u32[]{:S(2)}) collective-permute-start(bf16[80,2304]{1,0:T(8,128)(2,1)S(1)} %collective-permute-done.16.refs_1_), channel_id=1, source_target_pairs={{0,96},{8,104},{16,112},{24,120},{32,0},{40,8},{48,16},{56,24},{64... | collective-permute-start | bytes 1105928 | tf_op jit(solution)/shard_map/ppermute | solution.py:408
  125.8 4.0 %collective-permute-start.24 = (bf16[80,2304]{1,0:T(8,128)(2,1)S(1)}, bf16[80,2304]{1,0:T(8,128)(2,1)S(1)}, u32[]{:S(2)}, u32[]{:S(2)}) collective-permute-start(bf16[80,2304]{1,0:T(8,128)(2,1)S(1)} %collective-permute-done.23.refs_5_), channel_id=1, source_target_pairs={{0,24},{8,0},{16,8},{24,16},{32,56},{40,32},{48,40},{56,48},{64,88... | collective-permute-start | bytes 1105928 | tf_op jit(solution)/shard_map/ppermute | solution.py:408
  129.9 2.7 %collective-permute-done.17.refs_2_ = bf16[80,2304]{1,0:T(8,128)(2,1)S(1)} collective-permute-done((bf16[80,2304]{1,0:T(8,128)(2,1)S(1)}, bf16[80,2304]{1,0:T(8,128)(2,1)S(1)}, u32[]{:S(2)}, u32[]{:S(2)}) %collective-permute-start.17) | collective-permute-done | bytes 368672 | tf_op jit(solution)/shard_map/ppermute | solution.py:408
  132.5 3.4 %collective-permute-start.25 = (bf16[80,2304]{1,0:T(8,128)(2,1)S(1)}, bf16[80,2304]{1,0:T(8,128)(2,1)}, u32[]{:S(2)}, u32[]{:S(2)}) collective-permute-start(bf16[80,2304]{1,0:T(8,128)(2,1)S(1)} %bitcast.18), channel_id=1, source_target_pairs={{0,96},{8,104},{16,112},{24,120},{32,0},{40,8},{48,16},{56,24},{64... | collective-permute-start | bytes 1105928 | tf_op jit(solution)/shard_map/ppermute | solution.py:408
  137.8 4.3 %collective-permute-start.27 = (bf16[80,2304]{1,0:T(8,128)(2,1)S(1)}, bf16[80,2304]{1,0:T(8,128)(2,1)}, u32[]{:S(2)}, u32[]{:S(2)}) collective-permute-start(bf16[80,2304]{1,0:T(8,128)(2,1)S(1)} %bitcast.24), channel_id=1, source_target_pairs={{0,24},{8,0},{16,8},{24,16},{32,56},{40,32},{48,40},{56,48},{64,88... | collective-permute-start | bytes 1105928 | tf_op jit(solution)/shard_map/ppermute | solution.py:408
  142.1 7.4 %pad.4 = bf16[2304,2,384]{2,1,0:T(2,128)(2,1)} pad(bf16[2304,2,360]{2,1,0:T(2,128)(2,1)} %bitcast.8, bf16[]{:T(256)} %constant.15.clone.1), padding=0_0x0_0x0_24 | pad | bytes 6856706 | tf_op jit(solution)/shard_map/jit(_pad)/pad | solution.py:461
  149.5 8.9 %reshape_reshape.3.refs_8_ = bf16[8,288,768]{2,1,0:T(8,128)(2,1)} reshape(bf16[2304,2,384]{2,1,0:T(2,128)(2,1)} %pad.4) | data formatting | bytes 7077888 | tf_op jit(solution)/shard_map/reshape;reshape | solution.py:462
  158.4 10.3 %expert.2 = (bf16[160,2304]{1,0:T(8,128)(2,1)}, bf16[160,2304]{1,0:T(8,128)(2,1)}, bf16[160,2304]{1,0:T(8,128)(2,1)}, bf16[160,2304]{1,0:T(8,128)(2,1)}) custom-call(s32[1]{0:T(128)} %bitcast.place, bf16[80,2304]{1,0:T(8,128)(2,1)} %copy-done.19, bf16[80,2304]{1,0:T(8,128)(2,1)} %copy-done.15, bf16[80,2304]{1,0:T(8,128)(2,1)} %copy-done.18, ...), custom_call_target="tpu_custom_call" | custom-call | flops 3185049600 | bytes 10874880 | tf_op jit(solution)/shard_map/expert/pallas_call | solution.py:305
  168.8 2.7 %collective-permute-start.31 = (bf16[160,2304]{1,0:T(8,128)(2,1)}, bf16[160,2304]{1,0:T(8,128)(2,1)}, u32[]{:S(2)}, u32[]{:S(2)}) collective-permute-start(bf16[160,2304]{1,0:T(8,128)(2,1)} %get-tuple-element.89), channel_id=1, source_target_pairs={{0,96},{8,104},{16,112},{24,120},{32,0},{40,8},{48,16},{56,24},{64... | collective-permute-start | bytes 2211848 | tf_op jit(solution)/shard_map/ppermute | solution.py:408
  171.5 2.7 %collective-permute-start.38 = (bf16[160,2304]{1,0:T(8,128)(2,1)}, bf16[160,2304]{1,0:T(8,128)(2,1)S(1)}, u32[]{:S(2)}, u32[]{:S(2)}) collective-permute-start(bf16[160,2304]{1,0:T(8,128)(2,1)} %get-tuple-element.99), channel_id=1, source_target_pairs={{0,24},{8,0},{16,8},{24,16},{32,56},{40,32},{48,40},{56,48},{64,88... | collective-permute-start | bytes 2211848 | tf_op jit(solution)/shard_map/ppermute | solution.py:408
  174.2 10.3 %expert.3 = (bf16[80,2304]{1,0:T(8,128)(2,1)}, bf16[80,2304]{1,0:T(8,128)(2,1)}, bf16[80,2304]{1,0:T(8,128)(2,1)}, bf16[80,2304]{1,0:T(8,128)(2,1)}, bf16[80,230...) custom-call(s32[1]{0:T(128)} %bitcast.place, ...), custom_call_target="tpu_custom_call" | custom-call | flops 3185049600 | bytes 10874880 | tf_op jit(solution)/shard_map/expert/pallas_call | solution.py:305
  187.9 2.7 %collective-permute-start.32 = (bf16[80,2304]{1,0:T(8,128)(2,1)S(1)}, bf16[80,2304]{1,0:T(8,128)(2,1)S(1)}, u32[]{:S(2)}, u32[]{:S(2)}) collective-permute-start(bf16[80,2304]{1,0:T(8,128)(2,1)S(1)} %add_convert_fusion.2), channel_id=1, source_target_pairs={{0,96},{8,104},{16,112},{24,120},{32,0},{40,8},{48,16},{56,24},{64... | collective-permute-start | bytes 1105928 | tf_op jit(solution)/shard_map/ppermute | solution.py:408
  191.9 2.7 %collective-permute-start.39 = (bf16[80,2304]{1,0:T(8,128)(2,1)S(1)}, bf16[80,2304]{1,0:T(8,128)(2,1)S(1)}, u32[]{:S(2)}, u32[]{:S(2)}) collective-permute-start(bf16[80,2304]{1,0:T(8,128)(2,1)S(1)} %add_convert_fusion), channel_id=1, source_target_pairs={{0,24},{8,0},{16,8},{24,16},{32,56},{40,32},{48,40},{56,48},{64,88... | collective-permute-start | bytes 1105928 | tf_op jit(solution)/shard_map/ppermute | solution.py:408
  202.1 2.3 collective-permute-done.33.refs_1_
  207.8 2.5 %collective-permute-done.42.refs_7_ = bf16[40,2304]{1,0:T(8,128)(2,1)S(1)} collective-permute-done((bf16[40,2304]{1,0:T(8,128)(2,1)S(1)}, bf16[40,2304]{1,0:T(8,128)(2,1)S(1)}, u32[]{:S(2)}, u32[]{:S(2)}) %collective-permute-start.42) | collective-permute-done | bytes 184352 | tf_op jit(solution)/shard_map/ppermute | solution.py:408
  210.6 23.1 %all_to_all.15 = bf16[8,80,288]{2,1,0:T(8,128)(2,1)S(1)} all-to-all(bf16[8,80,288]{2,1,0:T(8,128)(2,1)S(1)} %finish.1), channel_id=1, replica_groups=mesh['wide'=16,'narrow'=8] {'narrow'}, dimensions={0} | all-to-all | bytes 737280 | tf_op jit(solution)/shard_map/all_to_all | solution.py:433
  (132 shorter events, 36.0 us)
Async XLA Ops:
  0.0 28.7 %all-to-all-start = ((bf16[8,288,360]{2,1,0:T(8,128)(2,1)}), bf16[8,288,360]{2,1,0:T(8,128)(2,1)}, u32[]{:S(2)}, u32[]{:S(2)}) async-start(bf16[8,288,360]{2,1,0:T(8,128)(2,1)} %bitcast.29), calls=%async_computation | async-start | bytes 3538944 | tf_op jit(solution)/shard_map/all_to_all | solution.py:433
  28.7 113.4 %all-to-all-start.1 = ((bf16[8,288,2,360]{3,2,1,0:T(2,128)(2,1)}), bf16[8,288,2,360]{3,2,1,0:T(2,128)(2,1)}, u32[]{:S(2)}, u32[]{:S(2)}) async-start(bf16[8,288,2,360]{3,2,1,0:T(2,128)(2,1)} %param.20), calls=%async_computation.1 | async-start | bytes 7077888 | tf_op jit(solution)/shard_map/all_to_all | solution.py:433
  36.2 42.9 %collective-permute-start.1 = (bf16[304,256]{1,0:T(8,128)(2,1)S(1)}, bf16[304,256]{1,0:T(8,128)(2,1)S(1)}, u32[]{:S(2)}, u32[]{:S(2)}) collective-permute-start(bf16[304,256]{1,0:T(8,128)(2,1)S(1)} %get-tuple-element.60), channel_id=1, source_target_pairs={{0,2},{1,3},{2,4},{3,5},{4,6},{5,7},{6,0},{7,1},{8,10},{9,11},{10,... | collective-permute-start | bytes 466952 | tf_op jit(solution)/shard_map/ppermute | solution.py:441
  37.6 45.0 %collective-permute-start.2 = (bf16[304,256]{1,0:T(8,128)(2,1)S(1)}, bf16[304,256]{1,0:T(8,128)(2,1)S(1)}, u32[]{:S(2)}, u32[]{:S(2)}) collective-permute-start(bf16[304,256]{1,0:T(8,128)(2,1)S(1)} %get-tuple-element.61), channel_id=1, source_target_pairs={{0,4},{1,5},{2,6},{3,7},{4,0},{5,1},{6,2},{7,3},{8,12},{9,13},{10,... | collective-permute-start | bytes 466952 | tf_op jit(solution)/shard_map/ppermute | solution.py:441
  40.0 42.6 %collective-permute-start.3 = (bf16[304,256]{1,0:T(8,128)(2,1)S(1)}, bf16[304,256]{1,0:T(8,128)(2,1)S(1)}, u32[]{:S(2)}, u32[]{:S(2)}) collective-permute-start(bf16[304,256]{1,0:T(8,128)(2,1)S(1)} %get-tuple-element.62), channel_id=1, source_target_pairs={{0,6},{1,7},{2,0},{3,1},{4,2},{5,3},{6,4},{7,5},{8,14},{9,15},{10,... | collective-permute-start | bytes 466952 | tf_op jit(solution)/shard_map/ppermute | solution.py:441
  85.4 7.8 %collective-permute-start.6 = (bf16[80,384]{1,0:T(8,128)(2,1)S(1)}, bf16[80,384]{1,0:T(8,128)(2,1)S(1)}, u32[]{:S(2)}, u32[]{:S(2)}) collective-permute-start(bf16[80,384]{1,0:T(8,128)(2,1)S(1)} %get-tuple-element.66), channel_id=1, source_target_pairs={{0,3},{1,4},{2,5},{3,6},{4,7},{5,0},{6,1},{7,2},{8,11},{9,12},{10,... | collective-permute-start | bytes 184328 | tf_op jit(solution)/shard_map/ppermute | solution.py:441
  95.9 11.6 %collective-permute-start.13 = (bf16[40,2304]{1,0:T(8,128)(2,1)S(1)}, bf16[40,2304]{1,0:T(8,128)(2,1)S(1)}, u32[]{:S(2)}, u32[]{:S(2)}) collective-permute-start(bf16[40,2304]{1,0:T(8,128)(2,1)S(1)} %get-tuple-element.108.refs_0_), channel_id=1, source_target_pairs={{0,24},{8,0},{16,8},{24,16},{32,56},{40,32},{48,40},{56,48},{64,88... | collective-permute-start | bytes 552968 | tf_op jit(solution)/shard_map/ppermute | solution.py:408
  99.7 11.1 %collective-permute-start.12 = (bf16[40,2304]{1,0:T(8,128)(2,1)S(1)}, bf16[40,2304]{1,0:T(8,128)(2,1)S(1)}, u32[]{:S(2)}, u32[]{:S(2)}) collective-permute-start(bf16[40,2304]{1,0:T(8,128)(2,1)S(1)} %get-tuple-element.108.refs_0_), channel_id=1, source_target_pairs={{0,8},{8,16},{16,24},{24,0},{32,40},{40,48},{48,56},{56,32},{64,72... | collective-permute-start | bytes 552968 | tf_op jit(solution)/shard_map/ppermute | solution.py:408
  99.7 11.1 %collective-permute-start.11 = (bf16[40,2304]{1,0:T(8,128)(2,1)S(1)}, bf16[40,2304]{1,0:T(8,128)(2,1)S(1)}, u32[]{:S(2)}, u32[]{:S(2)}) collective-permute-start(bf16[40,2304]{1,0:T(8,128)(2,1)S(1)} %get-tuple-element.108.refs_0_), channel_id=1, source_target_pairs={{0,16},{8,24},{16,0},{24,8},{32,48},{40,56},{48,32},{56,40},{64,80... | collective-permute-start | bytes 552968 | tf_op jit(solution)/shard_map/ppermute | solution.py:408
  101.0 12.6 %collective-permute-start.20 = (bf16[40,2304]{1,0:T(8,128)(2,1)S(1)}, bf16[40,2304]{1,0:T(8,128)(2,1)S(1)}, u32[]{:S(2)}, u32[]{:S(2)}) collective-permute-start(bf16[40,2304]{1,0:T(8,128)(2,1)S(1)} %get-tuple-element.107.refs_0_), channel_id=1, source_target_pairs={{0,96},{8,104},{16,112},{24,120},{32,0},{40,8},{48,16},{56,24},{64... | collective-permute-start | bytes 552968 | tf_op jit(solution)/shard_map/ppermute | solution.py:408
  103.7 9.9 %collective-permute-start.19 = (bf16[40,2304]{1,0:T(8,128)(2,1)S(1)}, bf16[40,2304]{1,0:T(8,128)(2,1)S(1)}, u32[]{:S(2)}, u32[]{:S(2)}) collective-permute-start(bf16[40,2304]{1,0:T(8,128)(2,1)S(1)} %get-tuple-element.107.refs_0_), channel_id=1, source_target_pairs={{0,32},{8,40},{16,48},{24,56},{32,64},{40,72},{48,80},{56,88},{64,... | collective-permute-start | bytes 552968 | tf_op jit(solution)/shard_map/ppermute | solution.py:408
  110.8 11.6 %collective-permute-start.16 = (bf16[80,2304]{1,0:T(8,128)(2,1)S(1)}, bf16[80,2304]{1,0:T(8,128)(2,1)S(1)}, u32[]{:S(2)}, u32[]{:S(2)}) collective-permute-start(bf16[80,2304]{1,0:T(8,128)(2,1)S(1)} %bitcast.20), channel_id=1, source_target_pairs={{0,96},{8,104},{16,112},{24,120},{32,0},{40,8},{48,16},{56,24},{64... | collective-permute-start | bytes 1105928 | tf_op jit(solution)/shard_map/ppermute | solution.py:408
  113.6 12.2 %collective-permute-start.14 = (bf16[80,2304]{1,0:T(8,128)(2,1)S(1)}, bf16[80,2304]{1,0:T(8,128)(2,1)S(1)}, u32[]{:S(2)}, u32[]{:S(2)}) collective-permute-start(bf16[80,2304]{1,0:T(8,128)(2,1)S(1)} %bitcast.17), channel_id=1, source_target_pairs={{0,32},{8,40},{16,48},{24,56},{32,64},{40,72},{48,80},{56,88},{64,... | collective-permute-start | bytes 1105928 | tf_op jit(solution)/shard_map/ppermute | solution.py:408
  114.2 11.6 %collective-permute-start.23 = (bf16[80,2304]{1,0:T(8,128)(2,1)S(1)}, bf16[80,2304]{1,0:T(8,128)(2,1)S(1)}, u32[]{:S(2)}, u32[]{:S(2)}) collective-permute-start(bf16[80,2304]{1,0:T(8,128)(2,1)S(1)} %bitcast.26), channel_id=1, source_target_pairs={{0,24},{8,0},{16,8},{24,16},{32,56},{40,32},{48,40},{56,48},{64,88... | collective-permute-start | bytes 1105928 | tf_op jit(solution)/shard_map/ppermute | solution.py:408
  118.0 11.8 %collective-permute-start.21 = (bf16[80,2304]{1,0:T(8,128)(2,1)S(1)}, bf16[80,2304]{1,0:T(8,128)(2,1)}, u32[]{:S(2)}, u32[]{:S(2)}) collective-permute-start(bf16[80,2304]{1,0:T(8,128)(2,1)S(1)} %bitcast.23), channel_id=1, source_target_pairs={{0,8},{8,16},{16,24},{24,0},{32,40},{40,48},{48,56},{56,32},{64,72... | collective-permute-start | bytes 1105928 | tf_op jit(solution)/shard_map/ppermute | solution.py:408
  122.4 10.2 %collective-permute-start.17 = (bf16[80,2304]{1,0:T(8,128)(2,1)S(1)}, bf16[80,2304]{1,0:T(8,128)(2,1)S(1)}, u32[]{:S(2)}, u32[]{:S(2)}) collective-permute-start(bf16[80,2304]{1,0:T(8,128)(2,1)S(1)} %collective-permute-done.16.refs_1_), channel_id=1, source_target_pairs={{0,96},{8,104},{16,112},{24,120},{32,0},{40,8},{48,16},{56,24},{64... | collective-permute-start | bytes 1105928 | tf_op jit(solution)/shard_map/ppermute | solution.py:408
  125.8 10.2 %collective-permute-start.15 = (bf16[80,2304]{1,0:T(8,128)(2,1)S(1)}, bf16[80,2304]{1,0:T(8,128)(2,1)S(1)}, u32[]{:S(2)}, u32[]{:S(2)}) collective-permute-start(bf16[80,2304]{1,0:T(8,128)(2,1)S(1)} %collective-permute-done.14.refs_3_), channel_id=1, source_target_pairs={{0,32},{8,40},{16,48},{24,56},{32,64},{40,72},{48,80},{56,88},{64,... | collective-permute-start | bytes 1105928 | tf_op jit(solution)/shard_map/ppermute | solution.py:408
  125.8 11.2 %collective-permute-start.24 = (bf16[80,2304]{1,0:T(8,128)(2,1)S(1)}, bf16[80,2304]{1,0:T(8,128)(2,1)S(1)}, u32[]{:S(2)}, u32[]{:S(2)}) collective-permute-start(bf16[80,2304]{1,0:T(8,128)(2,1)S(1)} %collective-permute-done.23.refs_5_), channel_id=1, source_target_pairs={{0,24},{8,0},{16,8},{24,16},{32,56},{40,32},{48,40},{56,48},{64,88... | collective-permute-start | bytes 1105928 | tf_op jit(solution)/shard_map/ppermute | solution.py:408
  129.8 28.6 %collective-permute-start.22 = (bf16[80,2304]{1,0:T(8,128)(2,1)}, bf16[80,2304]{1,0:T(8,128)(2,1)}, u32[]{:S(2)}, u32[]{:S(2)}) collective-permute-start(bf16[80,2304]{1,0:T(8,128)(2,1)} %collective-permute-done.21.refs_7_), channel_id=1, source_target_pairs={{0,8},{8,16},{16,24},{24,0},{32,40},{40,48},{48,56},{56,32},{64,72... | collective-permute-start | bytes 1105928 | tf_op jit(solution)/shard_map/ppermute | solution.py:408
  129.8 38.9 %collective-permute-start.26 = (bf16[80,2304]{1,0:T(8,128)(2,1)S(1)}, bf16[80,2304]{1,0:T(8,128)(2,1)}, u32[]{:S(2)}, u32[]{:S(2)}) collective-permute-start(bf16[80,2304]{1,0:T(8,128)(2,1)S(1)} %bitcast.21), channel_id=1, source_target_pairs={{0,32},{8,40},{16,48},{24,56},{32,64},{40,72},{48,80},{56,88},{64,... | collective-permute-start | bytes 1105928 | tf_op jit(solution)/shard_map/ppermute | solution.py:408
  132.5 36.2 %collective-permute-start.25 = (bf16[80,2304]{1,0:T(8,128)(2,1)S(1)}, bf16[80,2304]{1,0:T(8,128)(2,1)}, u32[]{:S(2)}, u32[]{:S(2)}) collective-permute-start(bf16[80,2304]{1,0:T(8,128)(2,1)S(1)} %bitcast.18), channel_id=1, source_target_pairs={{0,96},{8,104},{16,112},{24,120},{32,0},{40,8},{48,16},{56,24},{64... | collective-permute-start | bytes 1105928 | tf_op jit(solution)/shard_map/ppermute | solution.py:408
  136.0 32.8 %collective-permute-start.28 = (bf16[80,2304]{1,0:T(8,128)(2,1)S(1)}, bf16[80,2304]{1,0:T(8,128)(2,1)}, u32[]{:S(2)}, u32[]{:S(2)}) collective-permute-start(bf16[80,2304]{1,0:T(8,128)(2,1)S(1)} %bitcast.27), channel_id=1, source_target_pairs={{0,8},{8,16},{16,24},{24,0},{32,40},{40,48},{48,56},{56,32},{64,72... | collective-permute-start | bytes 1105928 | tf_op jit(solution)/shard_map/ppermute | solution.py:408
  137.8 31.0 %collective-permute-start.27 = (bf16[80,2304]{1,0:T(8,128)(2,1)S(1)}, bf16[80,2304]{1,0:T(8,128)(2,1)}, u32[]{:S(2)}, u32[]{:S(2)}) collective-permute-start(bf16[80,2304]{1,0:T(8,128)(2,1)S(1)} %bitcast.24), channel_id=1, source_target_pairs={{0,24},{8,0},{16,8},{24,16},{32,56},{40,32},{48,40},{56,48},{64,88... | collective-permute-start | bytes 1105928 | tf_op jit(solution)/shard_map/ppermute | solution.py:408
  168.7 16.7 %collective-permute-start.29 = (bf16[160,2304]{1,0:T(8,128)(2,1)}, bf16[160,2304]{1,0:T(8,128)(2,1)S(1)}, u32[]{:S(2)}, u32[]{:S(2)}) collective-permute-start(bf16[160,2304]{1,0:T(8,128)(2,1)} %get-tuple-element.88), channel_id=1, source_target_pairs={{0,32},{8,40},{16,48},{24,56},{32,64},{40,72},{48,80},{56,88},{64,... | collective-permute-start | bytes 2211848 | tf_op jit(solution)/shard_map/ppermute | solution.py:408
  168.8 17.8 %collective-permute-start.31 = (bf16[160,2304]{1,0:T(8,128)(2,1)}, bf16[160,2304]{1,0:T(8,128)(2,1)}, u32[]{:S(2)}, u32[]{:S(2)}) collective-permute-start(bf16[160,2304]{1,0:T(8,128)(2,1)} %get-tuple-element.89), channel_id=1, source_target_pairs={{0,96},{8,104},{16,112},{24,120},{32,0},{40,8},{48,16},{56,24},{64... | collective-permute-start | bytes 2211848 | tf_op jit(solution)/shard_map/ppermute | solution.py:408
  171.5 19.1 %collective-permute-start.36 = (bf16[160,2304]{1,0:T(8,128)(2,1)}, bf16[160,2304]{1,0:T(8,128)(2,1)S(1)}, u32[]{:S(2)}, u32[]{:S(2)}) collective-permute-start(bf16[160,2304]{1,0:T(8,128)(2,1)} %get-tuple-element.98), channel_id=1, source_target_pairs={{0,8},{8,16},{16,24},{24,0},{32,40},{40,48},{48,56},{56,32},{64,72... | collective-permute-start | bytes 2211848 | tf_op jit(solution)/shard_map/ppermute | solution.py:408
  171.5 20.3 %collective-permute-start.38 = (bf16[160,2304]{1,0:T(8,128)(2,1)}, bf16[160,2304]{1,0:T(8,128)(2,1)S(1)}, u32[]{:S(2)}, u32[]{:S(2)}) collective-permute-start(bf16[160,2304]{1,0:T(8,128)(2,1)} %get-tuple-element.99), channel_id=1, source_target_pairs={{0,24},{8,0},{16,8},{24,16},{32,56},{40,32},{48,40},{56,48},{64,88... | collective-permute-start | bytes 2211848 | tf_op jit(solution)/shard_map/ppermute | solution.py:408
  186.6 8.0 %collective-permute-start.30 = (bf16[80,2304]{1,0:T(8,128)(2,1)S(1)}, bf16[80,2304]{1,0:T(8,128)(2,1)S(1)}, u32[]{:S(2)}, u32[]{:S(2)}) collective-permute-start(bf16[80,2304]{1,0:T(8,128)(2,1)S(1)} %add_convert_fusion.3), channel_id=1, source_target_pairs={{0,32},{8,40},{16,48},{24,56},{32,64},{40,72},{48,80},{56,88},{64,... | collective-permute-start | bytes 1105928 | tf_op jit(solution)/shard_map/ppermute | solution.py:408
  191.9 9.3 %collective-permute-start.39 = (bf16[80,2304]{1,0:T(8,128)(2,1)S(1)}, bf16[80,2304]{1,0:T(8,128)(2,1)S(1)}, u32[]{:S(2)}, u32[]{:S(2)}) collective-permute-start(bf16[80,2304]{1,0:T(8,128)(2,1)S(1)} %add_convert_fusion), channel_id=1, source_target_pairs={{0,24},{8,0},{16,8},{24,16},{32,56},{40,32},{48,40},{56,48},{64,88... | collective-permute-start | bytes 1105928 | tf_op jit(solution)/shard_map/ppermute | solution.py:408
  196.5 7.9 %collective-permute-start.33 = (bf16[40,2304]{1,0:T(8,128)(2,1)S(1)}, bf16[40,2304]{1,0:T(8,128)(2,1)S(1)}, u32[]{:S(2)}, u32[]{:S(2)}) collective-permute-start(bf16[40,2304]{1,0:T(8,128)(2,1)S(1)} %get-tuple-element.93), channel_id=1, source_target_pairs={{0,16},{8,24},{16,0},{24,8},{32,48},{40,56},{48,32},{56,40},{64,80... | collective-permute-start | bytes 552968 | tf_op jit(solution)/shard_map/ppermute | solution.py:408
  197.0 9.1 %collective-permute-start.34 = (bf16[40,2304]{1,0:T(8,128)(2,1)S(1)}, bf16[40,2304]{1,0:T(8,128)(2,1)S(1)}, u32[]{:S(2)}, u32[]{:S(2)}) collective-permute-start(bf16[40,2304]{1,0:T(8,128)(2,1)S(1)} %get-tuple-element.94), channel_id=1, source_target_pairs={{0,24},{8,0},{16,8},{24,16},{32,56},{40,32},{48,40},{56,48},{64,88... | collective-permute-start | bytes 552968 | tf_op jit(solution)/shard_map/ppermute | solution.py:408
  197.3 10.0 %collective-permute-start.35 = (bf16[40,2304]{1,0:T(8,128)(2,1)S(1)}, bf16[40,2304]{1,0:T(8,128)(2,1)S(1)}, u32[]{:S(2)}, u32[]{:S(2)}) collective-permute-start(bf16[40,2304]{1,0:T(8,128)(2,1)S(1)} %get-tuple-element.95), channel_id=1, source_target_pairs={{0,8},{8,16},{16,24},{24,0},{32,40},{40,48},{48,56},{56,32},{64,72... | collective-permute-start | bytes 552968 | tf_op jit(solution)/shard_map/ppermute | solution.py:408
  (34 other events, 469.4 us)

commit v4 on v3

--- a/solution.py
+++ b/solution.py
@@ -260,18 +260,24 @@
 
 def expert_kernel(place, *refs, count):
     blocks, gate_up_hbm, down_hbm = refs[:count], refs[count], refs[count + 1]
-    outs, (x_sc, gate_up_sc, down_sc, both_sc, y_sc, sems) = refs[count + 2 : -6], refs[-6:]
+    outs, (x_sc, part_sc, gate_up_sc, down_sc, both_sc, y_sc, sems) = refs[count + 2 : -7], refs[-7:]
     rows, out_rows, units = blocks[0].shape[0], outs[0].shape[0], down_sc.shape[1]
     half = gate_up_sc.shape[1] // 2
     tile = 256
     loads = [pltpu.make_async_copy(b, x_sc.at[pl.ds(i * rows, rows)], sems.at[i]) for i, b in enumerate(blocks)]
-    groups, share = gate_up_hbm.shape[:2]
+    groups, _, share, _ = gate_up_hbm.shape
+    parts = []
     for g in range(groups):
         source = (place[0] + groups - g) % groups
-        loads.append(pltpu.make_async_copy(gate_up_hbm.at[source], gate_up_sc.at[pl.ds(g * share, share)], sems.at[count + 2 + len(outs) + g]))
+        parts.append(pltpu.make_async_copy(gate_up_hbm.at[source], part_sc.at[g], sems.at[count + 2 + len(outs) + g]))
     down_load = pltpu.make_async_copy(down_hbm, down_sc, sems.at[count + 1])
-    for load in (*loads, down_load):
+    for load in (*parts, *loads, down_load):
         load.start()
+    for g in range(groups):
+        parts[g].wait()
+        at = slice(g * share, g * share + share)
+        gate_up_sc[at, :units] = part_sc[g, 0]
+        gate_up_sc[at, half : half + units] = part_sc[g, 1]
     for load in loads:
         load.wait()
 
@@ -301,6 +307,7 @@
     units = down.shape[1]
     count = len(blocks)
     total = count * rows
+    packed = 2 * (-(-units // 128) * 128)
     anywhere = pl.BlockSpec(memory_space=pltpu.HBM)
     return pl.pallas_call(
         functools.partial(expert_kernel, count=count),
@@ -309,9 +316,10 @@
         out_shape=[jax.ShapeDtypeStruct((out_rows, width), BF16)] * (total // out_rows),
         scratch_shapes=[
             pltpu.VMEM((total, width), BF16),
-            pltpu.VMEM((width, gate_up.shape[2]), BF16),
+            pltpu.VMEM(gate_up.shape, BF16),
+            pltpu.VMEM((width, packed), BF16),
             pltpu.VMEM(down.shape, BF16),
-            pltpu.VMEM((total, gate_up.shape[2]), F32),
+            pltpu.VMEM((total, packed), F32),
             pltpu.VMEM((total, width), BF16),
             pltpu.SemaphoreType.DMA((count + 2 + total // out_rows + gate_up.shape[0],)),
         ],
@@ -445,6 +453,7 @@
     sums = merged[:1]
     for step in range(1, len(merged)):
         sums.append(along(merged[step], 2 * step))
+    w_gate_up, sums[1] = lax.optimization_barrier((jnp.transpose(w_gate_up, (0, 2, 1, 3)), sums[1]))
     gate_up_all = exchange(w_gate_up)
 
     flat_ids = expert_ids.reshape(token_rows * 2)
@@ -457,9 +466,9 @@
     res_share = lax.dynamic_slice_in_dim(residual, narrow_pos * share, share, 1).astype(F32).T
     gain_share = lax.dynamic_slice_in_dim(norm_gain, narrow_pos * share, share, 0)[:, None]
     *placed, hidden = join(place, sums, res_share, gain_share, slots.T, expert_count)
-    rows = norm_rows([along(x, i) if i else x for i, x in enumerate(placed)], share)
-    gate_up_all = jnp.pad(gate_up_all.reshape(width, 2, units), ((0, 0), (0, 0), (0, -units % 128)))
-    gate_up_all = gate_up_all.reshape(width, -1).reshape(narrow_count, share, -1)
+    for step in range(1, narrow_count):
+        placed[step] = along(placed[step], step)
+    rows = norm_rows(placed, share)
     down_all = down_all.reshape(width, units)
 
     half = CAP // 2

time: 236 us -> 220 us (0.932)
  local copies, waits for them, and re-layouts: 20.5 us -> 7.82 us
  starting transfers between devices: 70.4 us -> 75.5 us
  waiting for transfers between devices: 73.2 us -> 69.1 us
  blocking collectives: 23.1 us -> 20.7 us
    another operation x1 -> x0, local copies, waits for them, and re-layouts: 8.9 us -> none  [local(): gate_up_all.reshape(width, -1).reshape(narrow_count, share, -1)]
    pad x1 -> x0, local copies, waits for them, and re-layouts: 7.36 us -> none  [local(): jnp.pad(gate_up_all.reshape(width, 2, units), ((0, 0), (0, 0), (0, -units...]
    optimization_barrier x0 -> x1, local copies, waits for them, and re-layouts: none -> 4.29 us  [local(): lax.optimization_barrier((w_gate_up, down_all, merged[0]))]
    ppermute x32, starting transfers between devices: 46.2 us -> 49.6 us  [shift(): return lax.ppermute(x, 'wide', ring_pairs(axis, step))]
    ppermute x32, waiting for transfers between devices: 25 us -> 21.9 us  [shift(): return lax.ppermute(x, 'wide', ring_pairs(axis, step))]
    all_to_all x1, blocking collectives: 23.1 us -> 20.7 us  [exchange(): return lax.all_to_all(x, 'narrow', 0, 0, tiled=True)]
  transfers between devices with their start and end apart: 45 -> 45, of which waited for: 23 -> 20; matrix products, arithmetic and copies ran while one was open for 9% -> 4% of each run, Pallas kernels for 18% -> 19%
where the time goes in v4:
time: 220 us
  starting transfers between devices  75.5 us (34%)
  waiting for transfers between devices  69.1 us (31%)
  Pallas kernels  43.2 us (20%)
  blocking collectives  20.7 us (9%)
  local copies, waits for them, and re-layouts  7.82 us (4%)
  other arithmetic  2.53 us (1%)
    ppermute x32, starting transfers between devices, shift(): return lax.ppermute(x, 'wide', ring_pairs(axis, step))  49.6 us
    ppermute x10, waiting for transfers between devices, along(): lax.ppermute(x, 'narrow', [(i, (i + step) % narrow_count) for i in range(...  44.9 us
    ppermute x32, waiting for transfers between devices, shift(): return lax.ppermute(x, 'wide', ring_pairs(axis, step))  21.9 us
    all_to_all x1, blocking collectives, exchange(): return lax.all_to_all(x, 'narrow', 0, 0, tiled=True)  20.7 us
    pallas_call x2, Pallas kernels, expert(): pl.pallas_call(functools.partial(expert_kernel, count=count), in_specs=[p...  20.4 us
    pallas_call x1, Pallas kernels, attend(): pl.pallas_call(functools.partial(attend_kernel, share=share), grid_spec=p...  18 us
    ppermute x10, starting transfers between devices, along(): lax.ppermute(x, 'narrow', [(i, (i + step) % narrow_count) for i in range(...  14.5 us
    all_to_all x2, starting transfers between devices, exchange(): return lax.all_to_all(x, 'narrow', 0, 0, tiled=True)  11.4 us
  transfers between devices with their start and end apart: 45, of which 20 were waited for; matrix products, arithmetic and copies ran while one was open for 4% of the time, Pallas kernels for 19%

profile of v4, /device:TPU:1, one launch (start us, length us, event | category | flops | bytes accessed | tf_op | source)
XLA Modules:
  0.0 219.6 jit_solution(2979767148323623899)
XLA Ops:
  0.0 5.9 %all-to-all-start = ((bf16[8,288,360]{2,1,0:T(8,128)(2,1)}), bf16[8,288,360]{2,1,0:T(8,128)(2,1)}, u32[]{:S(2)}, u32[]{:S(2)}) async-start(bf16[8,288,360]{2,1,0:T(8,128)(2,1)} %bitcast.32), calls=%async_computation | async-start | bytes 3538944 | tf_op jit(solution)/shard_map/all_to_all | solution.py:441
  5.9 18.0 %attend.1 = (bf16[4,304,256]{2,1,0:T(8,128)(2,1)}, bf16[4,304,256]{2,1,0:T(8,128)(2,1)}) custom-call(s32[2,32]{1,0:T(2,128)} %table.1, s32[2]{0:T(128)} %length.1, s32[1]{0:T(128)} %bitcast.place, bf16[2,128,2304]{2,1,0:T(8,128)(2,1)} %q_ref.1, bf16[2,4,2,128,2304]{4,3,2,1,0:T(8,128)(2,1)} %v_ref.1, bf16[2,4,2,128,2304]{4,3,2,1,0:T(8,128)(2,1)} %v_ref.1, ...), custom_call_target="tpu_custom_call" | custom-call | flops 1245708288 | bytes 10616832 | tf_op jit(solution)/shard_map/attend/pallas_call | solution.py:103
  24.0 2.3 %collective-permute-done.other_ref = bf16[4,304,256]{2,1,0:T(8,128)(2,1)S(1)} collective-permute-done((bf16[4,304,256]{2,1,0:T(8,128)(2,1)}, bf16[4,304,256]{2,1,0:T(8,128)(2,1)S(1)}, u32[]{:S(2)}, u32[]{:S(2)}) %collective-permute-start) | collective-permute-done | bytes 622624 | tf_op jit(solution)/shard_map/ppermute | solution.py:446
  29.3 4.3 %copy.21 = bf16[8,288,2,360]{3,1,2,0:T(8,128)(2,1)} copy(bf16[8,288,2,360]{3,2,1,0:T(2,128)(2,1)} %param.20) | data formatting | bytes 6635520 | tf_op jit(solution)/shard_map/optimization_barrier | solution.py:452
  34.6 5.5 %all-to-all-start.1 = ((bf16[8,2,288,360]{3,2,1,0:T(8,128)(2,1)}), bf16[8,2,288,360]{3,2,1,0:T(8,128)(2,1)}, u32[]{:S(2)}, u32[]{:S(2)}) async-start(bf16[8,2,288,360]{3,2,1,0:T(8,128)(2,1)} %bitcast.31), calls=%async_computation.1 | async-start | bytes 7077888 | tf_op jit(solution)/shard_map/all_to_all | solution.py:441
  42.1 3.0 %collective-permute-start.2 = (bf16[304,256]{1,0:T(8,128)(2,1)S(1)}, bf16[304,256]{1,0:T(8,128)(2,1)S(1)}, u32[]{:S(2)}, u32[]{:S(2)}) collective-permute-start(bf16[304,256]{1,0:T(8,128)(2,1)S(1)} %get-tuple-element.65), channel_id=1, source_target_pairs={{0,4},{1,5},{2,6},{3,7},{4,0},{5,1},{6,2},{7,3},{8,12},{9,13},{10,... | collective-permute-start | bytes 466952 | tf_op jit(solution)/shard_map/ppermute | solution.py:449
  45.9 39.2 %collective-permute-done.2.refs_2_ = bf16[304,256]{1,0:T(8,128)(2,1)S(1)} collective-permute-done((bf16[304,256]{1,0:T(8,128)(2,1)S(1)}, bf16[304,256]{1,0:T(8,128)(2,1)S(1)}, u32[]{:S(2)}, u32[]{:S(2)}) %collective-permute-start.2) | collective-permute-done | bytes 155680 | tf_op jit(solution)/shard_map/ppermute | solution.py:449
  88.3 2.0 collective-permute-start.4
  93.6 2.1 collective-permute-start.8
  95.7 1.9 collective-permute-start.10
  100.8 3.8 %collective-permute-start.13 = (bf16[40,2304]{1,0:T(8,128)(2,1)S(1)}, bf16[40,2304]{1,0:T(8,128)(2,1)S(1)}, u32[]{:S(2)}, u32[]{:S(2)}) collective-permute-start(bf16[40,2304]{1,0:T(8,128)(2,1)S(1)} %get-tuple-element.112.refs_0_), channel_id=1, source_target_pairs={{0,24},{8,0},{16,8},{24,16},{32,56},{40,32},{48,40},{56,48},{64,88... | collective-permute-start | bytes 552968 | tf_op jit(solution)/shard_map/ppermute | solution.py:416
  106.0 2.7 %collective-permute-start.20 = (bf16[40,2304]{1,0:T(8,128)(2,1)S(1)}, bf16[40,2304]{1,0:T(8,128)(2,1)S(1)}, u32[]{:S(2)}, u32[]{:S(2)}) collective-permute-start(bf16[40,2304]{1,0:T(8,128)(2,1)S(1)} %get-tuple-element.111.refs_0_), channel_id=1, source_target_pairs={{0,96},{8,104},{16,112},{24,120},{32,0},{40,8},{48,16},{56,24},{64... | collective-permute-start | bytes 552968 | tf_op jit(solution)/shard_map/ppermute | solution.py:416
  108.7 3.7 %collective-permute-done.13.refs_3_ = bf16[40,2304]{1,0:T(8,128)(2,1)S(1)} collective-permute-done((bf16[40,2304]{1,0:T(8,128)(2,1)S(1)}, bf16[40,2304]{1,0:T(8,128)(2,1)S(1)}, u32[]{:S(2)}, u32[]{:S(2)}) %collective-permute-start.13) | collective-permute-done | bytes 184352 | tf_op jit(solution)/shard_map/ppermute | solution.py:416
  112.4 2.9 %collective-permute-start.18 = (bf16[40,2304]{1,0:T(8,128)(2,1)S(1)}, bf16[40,2304]{1,0:T(8,128)(2,1)S(1)}, u32[]{:S(2)}, u32[]{:S(2)}) collective-permute-start(bf16[40,2304]{1,0:T(8,128)(2,1)S(1)} %get-tuple-element.111.refs_0_), channel_id=1, source_target_pairs={{0,64},{8,72},{16,80},{24,88},{32,96},{40,104},{48,112},{56,120},{... | collective-permute-start | bytes 552968 | tf_op jit(solution)/shard_map/ppermute | solution.py:416
  115.8 2.8 %collective-permute-start.16 = (bf16[80,2304]{1,0:T(8,128)(2,1)S(1)}, bf16[80,2304]{1,0:T(8,128)(2,1)S(1)}, u32[]{:S(2)}, u32[]{:S(2)}) collective-permute-start(bf16[80,2304]{1,0:T(8,128)(2,1)S(1)} %bitcast.22), channel_id=1, source_target_pairs={{0,96},{8,104},{16,112},{24,120},{32,0},{40,8},{48,16},{56,24},{64... | collective-permute-start | bytes 1105928 | tf_op jit(solution)/shard_map/ppermute | solution.py:416
  119.1 3.8 %collective-permute-start.23 = (bf16[80,2304]{1,0:T(8,128)(2,1)S(1)}, bf16[80,2304]{1,0:T(8,128)(2,1)S(1)}, u32[]{:S(2)}, u32[]{:S(2)}) collective-permute-start(bf16[80,2304]{1,0:T(8,128)(2,1)S(1)} %bitcast.28), channel_id=1, source_target_pairs={{0,24},{8,0},{16,8},{24,16},{32,56},{40,32},{48,40},{56,48},{64,88... | collective-permute-start | bytes 1105928 | tf_op jit(solution)/shard_map/ppermute | solution.py:416
  122.9 4.4 %collective-permute-done.16.refs_1_ = bf16[80,2304]{1,0:T(8,128)(2,1)S(1)} collective-permute-done((bf16[80,2304]{1,0:T(8,128)(2,1)S(1)}, bf16[80,2304]{1,0:T(8,128)(2,1)S(1)}, u32[]{:S(2)}, u32[]{:S(2)}) %collective-permute-start.16) | collective-permute-done | bytes 368672 | tf_op jit(solution)/shard_map/ppermute | solution.py:416
  127.4 3.4 %collective-permute-start.17 = (bf16[80,2304]{1,0:T(8,128)(2,1)S(1)}, bf16[80,2304]{1,0:T(8,128)(2,1)S(1)}, u32[]{:S(2)}, u32[]{:S(2)}) collective-permute-start(bf16[80,2304]{1,0:T(8,128)(2,1)S(1)} %collective-permute-done.16.refs_1_), channel_id=1, source_target_pairs={{0,96},{8,104},{16,112},{24,120},{32,0},{40,8},{48,16},{56,24},{64... | collective-permute-start | bytes 1105928 | tf_op jit(solution)/shard_map/ppermute | solution.py:416
  130.8 4.0 %collective-permute-start.24 = (bf16[80,2304]{1,0:T(8,128)(2,1)S(1)}, bf16[80,2304]{1,0:T(8,128)(2,1)S(1)}, u32[]{:S(2)}, u32[]{:S(2)}) collective-permute-start(bf16[80,2304]{1,0:T(8,128)(2,1)S(1)} %collective-permute-done.23.refs_5_), channel_id=1, source_target_pairs={{0,24},{8,0},{16,8},{24,16},{32,56},{40,32},{48,40},{56,48},{64,88... | collective-permute-start | bytes 1105928 | tf_op jit(solution)/shard_map/ppermute | solution.py:416
  134.9 2.6 %collective-permute-done.17.refs_2_ = bf16[80,2304]{1,0:T(8,128)(2,1)S(1)} collective-permute-done((bf16[80,2304]{1,0:T(8,128)(2,1)S(1)}, bf16[80,2304]{1,0:T(8,128)(2,1)S(1)}, u32[]{:S(2)}, u32[]{:S(2)}) %collective-permute-start.17) | collective-permute-done | bytes 368672 | tf_op jit(solution)/shard_map/ppermute | solution.py:416
  137.5 3.4 %collective-permute-start.25 = (bf16[80,2304]{1,0:T(8,128)(2,1)S(1)}, bf16[80,2304]{1,0:T(8,128)(2,1)}, u32[]{:S(2)}, u32[]{:S(2)}) collective-permute-start(bf16[80,2304]{1,0:T(8,128)(2,1)S(1)} %bitcast.20), channel_id=1, source_target_pairs={{0,96},{8,104},{16,112},{24,120},{32,0},{40,8},{48,16},{56,24},{64... | collective-permute-start | bytes 1105928 | tf_op jit(solution)/shard_map/ppermute | solution.py:416
  142.0 3.7 %collective-permute-start.27 = (bf16[80,2304]{1,0:T(8,128)(2,1)S(1)}, bf16[80,2304]{1,0:T(8,128)(2,1)}, u32[]{:S(2)}, u32[]{:S(2)}) collective-permute-start(bf16[80,2304]{1,0:T(8,128)(2,1)S(1)} %bitcast.26), channel_id=1, source_target_pairs={{0,24},{8,0},{16,8},{24,16},{32,56},{40,32},{48,40},{56,48},{64,88... | collective-permute-start | bytes 1105928 | tf_op jit(solution)/shard_map/ppermute | solution.py:416
  145.7 10.2 %expert.2 = (bf16[160,2304]{1,0:T(8,128)(2,1)}, bf16[160,2304]{1,0:T(8,128)(2,1)}, bf16[160,2304]{1,0:T(8,128)(2,1)}, bf16[160,2304]{1,0:T(8,128)(2,1)}) custom-call(s32[1]{0:T(128)} %bitcast.place, bf16[80,2304]{1,0:T(8,128)(2,1)} %copy-done.21, bf16[80,2304]{1,0:T(8,128)(2,1)} %copy-done.16, bf16[80,2304]{1,0:T(8,128)(2,1)} %copy-done.20, ...), custom_call_target="tpu_custom_call" | custom-call | flops 3185049600 | bytes 10874880 | tf_op jit(solution)/shard_map/expert/pallas_call | solution.py:312
  156.1 2.7 %collective-permute-start.31 = (bf16[160,2304]{1,0:T(8,128)(2,1)}, bf16[160,2304]{1,0:T(8,128)(2,1)}, u32[]{:S(2)}, u32[]{:S(2)}) collective-permute-start(bf16[160,2304]{1,0:T(8,128)(2,1)} %get-tuple-element.93), channel_id=1, source_target_pairs={{0,96},{8,104},{16,112},{24,120},{32,0},{40,8},{48,16},{56,24},{64... | collective-permute-start | bytes 2211848 | tf_op jit(solution)/shard_map/ppermute | solution.py:416
  158.7 2.7 %collective-permute-start.38 = (bf16[160,2304]{1,0:T(8,128)(2,1)}, bf16[160,2304]{1,0:T(8,128)(2,1)S(1)}, u32[]{:S(2)}, u32[]{:S(2)}) collective-permute-start(bf16[160,2304]{1,0:T(8,128)(2,1)} %get-tuple-element.103), channel_id=1, source_target_pairs={{0,24},{8,0},{16,8},{24,16},{32,56},{40,32},{48,40},{56,48},{64,88... | collective-permute-start | bytes 2211848 | tf_op jit(solution)/shard_map/ppermute | solution.py:416
  161.4 10.3 %expert.3 = (bf16[80,2304]{1,0:T(8,128)(2,1)}, bf16[80,2304]{1,0:T(8,128)(2,1)}, bf16[80,2304]{1,0:T(8,128)(2,1)}, bf16[80,2304]{1,0:T(8,128)(2,1)}, bf16[80,230...) custom-call(s32[1]{0:T(128)} %bitcast.place, ...), custom_call_target="tpu_custom_call" | custom-call | flops 3185049600 | bytes 10874880 | tf_op jit(solution)/shard_map/expert/pallas_call | solution.py:312
  175.1 2.7 %collective-permute-start.32 = (bf16[80,2304]{1,0:T(8,128)(2,1)S(1)}, bf16[80,2304]{1,0:T(8,128)(2,1)S(1)}, u32[]{:S(2)}, u32[]{:S(2)}) collective-permute-start(bf16[80,2304]{1,0:T(8,128)(2,1)S(1)} %add_convert_fusion.2), channel_id=1, source_target_pairs={{0,96},{8,104},{16,112},{24,120},{32,0},{40,8},{48,16},{56,24},{64... | collective-permute-start | bytes 1105928 | tf_op jit(solution)/shard_map/ppermute | solution.py:416
  178.1 2.7 %collective-permute-start.39 = (bf16[80,2304]{1,0:T(8,128)(2,1)S(1)}, bf16[80,2304]{1,0:T(8,128)(2,1)S(1)}, u32[]{:S(2)}, u32[]{:S(2)}) collective-permute-start(bf16[80,2304]{1,0:T(8,128)(2,1)S(1)} %add_convert_fusion), channel_id=1, source_target_pairs={{0,24},{8,0},{16,8},{24,16},{32,56},{40,32},{48,40},{56,48},{64,88... | collective-permute-start | bytes 1105928 | tf_op jit(solution)/shard_map/ppermute | solution.py:416
  187.3 2.0 collective-permute-start.40
  191.6 3.0 %collective-permute-done.34.refs_2_ = bf16[40,2304]{1,0:T(8,128)(2,1)S(1)} collective-permute-done((bf16[40,2304]{1,0:T(8,128)(2,1)S(1)}, bf16[40,2304]{1,0:T(8,128)(2,1)S(1)}, u32[]{:S(2)}, u32[]{:S(2)}) %collective-permute-start.34) | collective-permute-done | bytes 184352 | tf_op jit(solution)/shard_map/ppermute | solution.py:416
  194.6 2.0 collective-permute-done.35.refs_3_
  197.8 20.7 %all_to_all.15 = bf16[8,80,288]{2,1,0:T(8,128)(2,1)S(1)} all-to-all(bf16[8,80,288]{2,1,0:T(8,128)(2,1)S(1)} %finish.1), channel_id=1, replica_groups=mesh['wide'=16,'narrow'=8] {'narrow'}, dimensions={0} | all-to-all | bytes 737280 | tf_op jit(solution)/shard_map/all_to_all | solution.py:441
  (135 shorter events, 34.7 us)
Async XLA Ops:
  0.0 29.3 %all-to-all-start = ((bf16[8,288,360]{2,1,0:T(8,128)(2,1)}), bf16[8,288,360]{2,1,0:T(8,128)(2,1)}, u32[]{:S(2)}, u32[]{:S(2)}) async-start(bf16[8,288,360]{2,1,0:T(8,128)(2,1)} %bitcast.32), calls=%async_computation | async-start | bytes 3538944 | tf_op jit(solution)/shard_map/all_to_all | solution.py:441
  34.6 111.1 %all-to-all-start.1 = ((bf16[8,2,288,360]{3,2,1,0:T(8,128)(2,1)}), bf16[8,2,288,360]{3,2,1,0:T(8,128)(2,1)}, u32[]{:S(2)}, u32[]{:S(2)}) async-start(bf16[8,2,288,360]{3,2,1,0:T(8,128)(2,1)} %bitcast.31), calls=%async_computation.1 | async-start | bytes 7077888 | tf_op jit(solution)/shard_map/all_to_all | solution.py:441
  42.1 43.0 %collective-permute-start.2 = (bf16[304,256]{1,0:T(8,128)(2,1)S(1)}, bf16[304,256]{1,0:T(8,128)(2,1)S(1)}, u32[]{:S(2)}, u32[]{:S(2)}) collective-permute-start(bf16[304,256]{1,0:T(8,128)(2,1)S(1)} %get-tuple-element.65), channel_id=1, source_target_pairs={{0,4},{1,5},{2,6},{3,7},{4,0},{5,1},{6,2},{7,3},{8,12},{9,13},{10,... | collective-permute-start | bytes 466952 | tf_op jit(solution)/shard_map/ppermute | solution.py:449
  45.0 41.9 %collective-permute-start.3 = (bf16[304,256]{1,0:T(8,128)(2,1)S(1)}, bf16[304,256]{1,0:T(8,128)(2,1)S(1)}, u32[]{:S(2)}, u32[]{:S(2)}) collective-permute-start(bf16[304,256]{1,0:T(8,128)(2,1)S(1)} %get-tuple-element.66), channel_id=1, source_target_pairs={{0,6},{1,7},{2,0},{3,1},{4,2},{5,3},{6,4},{7,5},{8,14},{9,15},{10,... | collective-permute-start | bytes 466952 | tf_op jit(solution)/shard_map/ppermute | solution.py:449
  100.8 11.6 %collective-permute-start.13 = (bf16[40,2304]{1,0:T(8,128)(2,1)S(1)}, bf16[40,2304]{1,0:T(8,128)(2,1)S(1)}, u32[]{:S(2)}, u32[]{:S(2)}) collective-permute-start(bf16[40,2304]{1,0:T(8,128)(2,1)S(1)} %get-tuple-element.112.refs_0_), channel_id=1, source_target_pairs={{0,24},{8,0},{16,8},{24,16},{32,56},{40,32},{48,40},{56,48},{64,88... | collective-permute-start | bytes 552968 | tf_op jit(solution)/shard_map/ppermute | solution.py:416
  104.7 11.0 %collective-permute-start.12 = (bf16[40,2304]{1,0:T(8,128)(2,1)S(1)}, bf16[40,2304]{1,0:T(8,128)(2,1)S(1)}, u32[]{:S(2)}, u32[]{:S(2)}) collective-permute-start(bf16[40,2304]{1,0:T(8,128)(2,1)S(1)} %get-tuple-element.112.refs_0_), channel_id=1, source_target_pairs={{0,8},{8,16},{16,24},{24,0},{32,40},{40,48},{48,56},{56,32},{64,72... | collective-permute-start | bytes 552968 | tf_op jit(solution)/shard_map/ppermute | solution.py:416
  104.7 11.0 %collective-permute-start.11 = (bf16[40,2304]{1,0:T(8,128)(2,1)S(1)}, bf16[40,2304]{1,0:T(8,128)(2,1)S(1)}, u32[]{:S(2)}, u32[]{:S(2)}) collective-permute-start(bf16[40,2304]{1,0:T(8,128)(2,1)S(1)} %get-tuple-element.112.refs_0_), channel_id=1, source_target_pairs={{0,16},{8,24},{16,0},{24,8},{32,48},{40,56},{48,32},{56,40},{64,80... | collective-permute-start | bytes 552968 | tf_op jit(solution)/shard_map/ppermute | solution.py:416
  106.0 12.6 %collective-permute-start.20 = (bf16[40,2304]{1,0:T(8,128)(2,1)S(1)}, bf16[40,2304]{1,0:T(8,128)(2,1)S(1)}, u32[]{:S(2)}, u32[]{:S(2)}) collective-permute-start(bf16[40,2304]{1,0:T(8,128)(2,1)S(1)} %get-tuple-element.111.refs_0_), channel_id=1, source_target_pairs={{0,96},{8,104},{16,112},{24,120},{32,0},{40,8},{48,16},{56,24},{64... | collective-permute-start | bytes 552968 | tf_op jit(solution)/shard_map/ppermute | solution.py:416
  108.7 9.9 %collective-permute-start.19 = (bf16[40,2304]{1,0:T(8,128)(2,1)S(1)}, bf16[40,2304]{1,0:T(8,128)(2,1)S(1)}, u32[]{:S(2)}, u32[]{:S(2)}) collective-permute-start(bf16[40,2304]{1,0:T(8,128)(2,1)S(1)} %get-tuple-element.111.refs_0_), channel_id=1, source_target_pairs={{0,32},{8,40},{16,48},{24,56},{32,64},{40,72},{48,80},{56,88},{64,... | collective-permute-start | bytes 552968 | tf_op jit(solution)/shard_map/ppermute | solution.py:416
  115.8 11.6 %collective-permute-start.16 = (bf16[80,2304]{1,0:T(8,128)(2,1)S(1)}, bf16[80,2304]{1,0:T(8,128)(2,1)S(1)}, u32[]{:S(2)}, u32[]{:S(2)}) collective-permute-start(bf16[80,2304]{1,0:T(8,128)(2,1)S(1)} %bitcast.22), channel_id=1, source_target_pairs={{0,96},{8,104},{16,112},{24,120},{32,0},{40,8},{48,16},{56,24},{64... | collective-permute-start | bytes 1105928 | tf_op jit(solution)/shard_map/ppermute | solution.py:416
  118.6 12.2 %collective-permute-start.14 = (bf16[80,2304]{1,0:T(8,128)(2,1)S(1)}, bf16[80,2304]{1,0:T(8,128)(2,1)S(1)}, u32[]{:S(2)}, u32[]{:S(2)}) collective-permute-start(bf16[80,2304]{1,0:T(8,128)(2,1)S(1)} %bitcast.19), channel_id=1, source_target_pairs={{0,32},{8,40},{16,48},{24,56},{32,64},{40,72},{48,80},{56,88},{64,... | collective-permute-start | bytes 1105928 | tf_op jit(solution)/shard_map/ppermute | solution.py:416
  119.1 11.6 %collective-permute-start.23 = (bf16[80,2304]{1,0:T(8,128)(2,1)S(1)}, bf16[80,2304]{1,0:T(8,128)(2,1)S(1)}, u32[]{:S(2)}, u32[]{:S(2)}) collective-permute-start(bf16[80,2304]{1,0:T(8,128)(2,1)S(1)} %bitcast.28), channel_id=1, source_target_pairs={{0,24},{8,0},{16,8},{24,16},{32,56},{40,32},{48,40},{56,48},{64,88... | collective-permute-start | bytes 1105928 | tf_op jit(solution)/shard_map/ppermute | solution.py:416
  122.9 11.9 %collective-permute-start.21 = (bf16[80,2304]{1,0:T(8,128)(2,1)S(1)}, bf16[80,2304]{1,0:T(8,128)(2,1)S(1)}, u32[]{:S(2)}, u32[]{:S(2)}) collective-permute-start(bf16[80,2304]{1,0:T(8,128)(2,1)S(1)} %bitcast.25), channel_id=1, source_target_pairs={{0,8},{8,16},{16,24},{24,0},{32,40},{40,48},{48,56},{56,32},{64,72... | collective-permute-start | bytes 1105928 | tf_op jit(solution)/shard_map/ppermute | solution.py:416
  127.4 10.1 %collective-permute-start.17 = (bf16[80,2304]{1,0:T(8,128)(2,1)S(1)}, bf16[80,2304]{1,0:T(8,128)(2,1)S(1)}, u32[]{:S(2)}, u32[]{:S(2)}) collective-permute-start(bf16[80,2304]{1,0:T(8,128)(2,1)S(1)} %collective-permute-done.16.refs_1_), channel_id=1, source_target_pairs={{0,96},{8,104},{16,112},{24,120},{32,0},{40,8},{48,16},{56,24},{64... | collective-permute-start | bytes 1105928 | tf_op jit(solution)/shard_map/ppermute | solution.py:416
  130.8 10.1 %collective-permute-start.15 = (bf16[80,2304]{1,0:T(8,128)(2,1)S(1)}, bf16[80,2304]{1,0:T(8,128)(2,1)S(1)}, u32[]{:S(2)}, u32[]{:S(2)}) collective-permute-start(bf16[80,2304]{1,0:T(8,128)(2,1)S(1)} %collective-permute-done.14.refs_3_), channel_id=1, source_target_pairs={{0,32},{8,40},{16,48},{24,56},{32,64},{40,72},{48,80},{56,88},{64,... | collective-permute-start | bytes 1105928 | tf_op jit(solution)/shard_map/ppermute | solution.py:416
  130.8 11.2 %collective-permute-start.24 = (bf16[80,2304]{1,0:T(8,128)(2,1)S(1)}, bf16[80,2304]{1,0:T(8,128)(2,1)S(1)}, u32[]{:S(2)}, u32[]{:S(2)}) collective-permute-start(bf16[80,2304]{1,0:T(8,128)(2,1)S(1)} %collective-permute-done.23.refs_5_), channel_id=1, source_target_pairs={{0,24},{8,0},{16,8},{24,16},{32,56},{40,32},{48,40},{56,48},{64,88... | collective-permute-start | bytes 1105928 | tf_op jit(solution)/shard_map/ppermute | solution.py:416
  134.8 10.9 %collective-permute-start.22 = (bf16[80,2304]{1,0:T(8,128)(2,1)S(1)}, bf16[80,2304]{1,0:T(8,128)(2,1)}, u32[]{:S(2)}, u32[]{:S(2)}) collective-permute-start(bf16[80,2304]{1,0:T(8,128)(2,1)S(1)} %collective-permute-done.21.refs_7_), channel_id=1, source_target_pairs={{0,8},{8,16},{16,24},{24,0},{32,40},{40,48},{48,56},{56,32},{64,72... | collective-permute-start | bytes 1105928 | tf_op jit(solution)/shard_map/ppermute | solution.py:416
  134.8 21.2 %collective-permute-start.26 = (bf16[80,2304]{1,0:T(8,128)(2,1)S(1)}, bf16[80,2304]{1,0:T(8,128)(2,1)}, u32[]{:S(2)}, u32[]{:S(2)}) collective-permute-start(bf16[80,2304]{1,0:T(8,128)(2,1)S(1)} %bitcast.23), channel_id=1, source_target_pairs={{0,32},{8,40},{16,48},{24,56},{32,64},{40,72},{48,80},{56,88},{64,... | collective-permute-start | bytes 1105928 | tf_op jit(solution)/shard_map/ppermute | solution.py:416
  137.5 18.5 %collective-permute-start.25 = (bf16[80,2304]{1,0:T(8,128)(2,1)S(1)}, bf16[80,2304]{1,0:T(8,128)(2,1)}, u32[]{:S(2)}, u32[]{:S(2)}) collective-permute-start(bf16[80,2304]{1,0:T(8,128)(2,1)S(1)} %bitcast.20), channel_id=1, source_target_pairs={{0,96},{8,104},{16,112},{24,120},{32,0},{40,8},{48,16},{56,24},{64... | collective-permute-start | bytes 1105928 | tf_op jit(solution)/shard_map/ppermute | solution.py:416
  140.9 15.1 %collective-permute-start.28 = (bf16[80,2304]{1,0:T(8,128)(2,1)S(1)}, bf16[80,2304]{1,0:T(8,128)(2,1)}, u32[]{:S(2)}, u32[]{:S(2)}) collective-permute-start(bf16[80,2304]{1,0:T(8,128)(2,1)S(1)} %bitcast.29), channel_id=1, source_target_pairs={{0,8},{8,16},{16,24},{24,0},{32,40},{40,48},{48,56},{56,32},{64,72... | collective-permute-start | bytes 1105928 | tf_op jit(solution)/shard_map/ppermute | solution.py:416
  142.0 14.0 %collective-permute-start.27 = (bf16[80,2304]{1,0:T(8,128)(2,1)S(1)}, bf16[80,2304]{1,0:T(8,128)(2,1)}, u32[]{:S(2)}, u32[]{:S(2)}) collective-permute-start(bf16[80,2304]{1,0:T(8,128)(2,1)S(1)} %bitcast.26), channel_id=1, source_target_pairs={{0,24},{8,0},{16,8},{24,16},{32,56},{40,32},{48,40},{56,48},{64,88... | collective-permute-start | bytes 1105928 | tf_op jit(solution)/shard_map/ppermute | solution.py:416
  156.0 16.7 %collective-permute-start.29 = (bf16[160,2304]{1,0:T(8,128)(2,1)}, bf16[160,2304]{1,0:T(8,128)(2,1)S(1)}, u32[]{:S(2)}, u32[]{:S(2)}) collective-permute-start(bf16[160,2304]{1,0:T(8,128)(2,1)} %get-tuple-element.92), channel_id=1, source_target_pairs={{0,32},{8,40},{16,48},{24,56},{32,64},{40,72},{48,80},{56,88},{64,... | collective-permute-start | bytes 2211848 | tf_op jit(solution)/shard_map/ppermute | solution.py:416
  156.1 17.8 %collective-permute-start.31 = (bf16[160,2304]{1,0:T(8,128)(2,1)}, bf16[160,2304]{1,0:T(8,128)(2,1)}, u32[]{:S(2)}, u32[]{:S(2)}) collective-permute-start(bf16[160,2304]{1,0:T(8,128)(2,1)} %get-tuple-element.93), channel_id=1, source_target_pairs={{0,96},{8,104},{16,112},{24,120},{32,0},{40,8},{48,16},{56,24},{64... | collective-permute-start | bytes 2211848 | tf_op jit(solution)/shard_map/ppermute | solution.py:416
  158.7 19.1 %collective-permute-start.36 = (bf16[160,2304]{1,0:T(8,128)(2,1)}, bf16[160,2304]{1,0:T(8,128)(2,1)S(1)}, u32[]{:S(2)}, u32[]{:S(2)}) collective-permute-start(bf16[160,2304]{1,0:T(8,128)(2,1)} %get-tuple-element.102), channel_id=1, source_target_pairs={{0,8},{8,16},{16,24},{24,0},{32,40},{40,48},{48,56},{56,32},{64,72... | collective-permute-start | bytes 2211848 | tf_op jit(solution)/shard_map/ppermute | solution.py:416
  158.7 19.2 %collective-permute-start.38 = (bf16[160,2304]{1,0:T(8,128)(2,1)}, bf16[160,2304]{1,0:T(8,128)(2,1)S(1)}, u32[]{:S(2)}, u32[]{:S(2)}) collective-permute-start(bf16[160,2304]{1,0:T(8,128)(2,1)} %get-tuple-element.103), channel_id=1, source_target_pairs={{0,24},{8,0},{16,8},{24,16},{32,56},{40,32},{48,40},{56,48},{64,88... | collective-permute-start | bytes 2211848 | tf_op jit(solution)/shard_map/ppermute | solution.py:416
  173.8 7.6 %collective-permute-start.30 = (bf16[80,2304]{1,0:T(8,128)(2,1)S(1)}, bf16[80,2304]{1,0:T(8,128)(2,1)S(1)}, u32[]{:S(2)}, u32[]{:S(2)}) collective-permute-start(bf16[80,2304]{1,0:T(8,128)(2,1)S(1)} %add_convert_fusion.3), channel_id=1, source_target_pairs={{0,32},{8,40},{16,48},{24,56},{32,64},{40,72},{48,80},{56,88},{64,... | collective-permute-start | bytes 1105928 | tf_op jit(solution)/shard_map/ppermute | solution.py:416
  177.9 9.1 %collective-permute-start.37 = (bf16[80,2304]{1,0:T(8,128)(2,1)S(1)}, bf16[80,2304]{1,0:T(8,128)(2,1)S(1)}, u32[]{:S(2)}, u32[]{:S(2)}) collective-permute-start(bf16[80,2304]{1,0:T(8,128)(2,1)S(1)} %add_convert_fusion.1), channel_id=1, source_target_pairs={{0,8},{8,16},{16,24},{24,0},{32,40},{40,48},{48,56},{56,32},{64,72... | collective-permute-start | bytes 1105928 | tf_op jit(solution)/shard_map/ppermute | solution.py:416
  178.1 8.9 %collective-permute-start.39 = (bf16[80,2304]{1,0:T(8,128)(2,1)S(1)}, bf16[80,2304]{1,0:T(8,128)(2,1)S(1)}, u32[]{:S(2)}, u32[]{:S(2)}) collective-permute-start(bf16[80,2304]{1,0:T(8,128)(2,1)S(1)} %add_convert_fusion), channel_id=1, source_target_pairs={{0,24},{8,0},{16,8},{24,16},{32,56},{40,32},{48,40},{56,48},{64,88... | collective-permute-start | bytes 1105928 | tf_op jit(solution)/shard_map/ppermute | solution.py:416
  183.7 8.0 %collective-permute-start.33 = (bf16[40,2304]{1,0:T(8,128)(2,1)S(1)}, bf16[40,2304]{1,0:T(8,128)(2,1)S(1)}, u32[]{:S(2)}, u32[]{:S(2)}) collective-permute-start(bf16[40,2304]{1,0:T(8,128)(2,1)S(1)} %get-tuple-element.97), channel_id=1, source_target_pairs={{0,16},{8,24},{16,0},{24,8},{32,48},{40,56},{48,32},{56,40},{64,80... | collective-permute-start | bytes 552968 | tf_op jit(solution)/shard_map/ppermute | solution.py:416
  185.5 9.1 %collective-permute-start.34 = (bf16[40,2304]{1,0:T(8,128)(2,1)S(1)}, bf16[40,2304]{1,0:T(8,128)(2,1)S(1)}, u32[]{:S(2)}, u32[]{:S(2)}) collective-permute-start(bf16[40,2304]{1,0:T(8,128)(2,1)S(1)} %get-tuple-element.98), channel_id=1, source_target_pairs={{0,24},{8,0},{16,8},{24,16},{32,56},{40,32},{48,40},{56,48},{64,88... | collective-permute-start | bytes 552968 | tf_op jit(solution)/shard_map/ppermute | solution.py:416
  185.5 11.1 %collective-permute-start.35 = (bf16[40,2304]{1,0:T(8,128)(2,1)S(1)}, bf16[40,2304]{1,0:T(8,128)(2,1)S(1)}, u32[]{:S(2)}, u32[]{:S(2)}) collective-permute-start(bf16[40,2304]{1,0:T(8,128)(2,1)S(1)} %get-tuple-element.99), channel_id=1, source_target_pairs={{0,8},{8,16},{16,24},{24,0},{32,40},{40,48},{48,56},{56,32},{64,72... | collective-permute-start | bytes 552968 | tf_op jit(solution)/shard_map/ppermute | solution.py:416
  187.3 9.3 %collective-permute-start.40 = (bf16[40,2304]{1,0:T(8,128)(2,1)S(1)}, bf16[40,2304]{1,0:T(8,128)(2,1)S(1)}, u32[]{:S(2)}, u32[]{:S(2)}) collective-permute-start(bf16[40,2304]{1,0:T(8,128)(2,1)S(1)} %get-tuple-element.107), channel_id=1, source_target_pairs={{0,64},{8,72},{16,80},{24,88},{32,96},{40,104},{48,112},{56,120},{... | collective-permute-start | bytes 552968 | tf_op jit(solution)/shard_map/ppermute | solution.py:416
  (36 other events, 454.9 us)

commit v5 on v4

--- a/solution.py
+++ b/solution.py
@@ -30,7 +30,7 @@
     return lax.dot_general(a, b, (((0,), (0,)), ((), ())), preferred_element_type=F32)
 
 
-def attend_kernel(table, length, place, q_ref, k_ref, v_ref, nk_ref, nv_ref, keep_ref, send_ref, sum_sc, top_sc, den_sc, *, share):
+def attend_kernel(table, length, place, q_ref, k_ref, v_ref, nk_ref, nv_ref, keep_ref, send_ref, score_sc, sum_sc, top_sc, den_sc, *, share):
     groups = 2 * keep_ref.shape[0]
     req, group = pl.program_id(0), pl.program_id(1)
     new_len = q_ref.shape[1]
@@ -40,7 +40,6 @@
     lane_at = pl.multiple_of(req * new_len, new_len)
     col = lax.broadcasted_iota(jnp.int32, (new_len, 128), 1)
     row = lax.broadcasted_iota(jnp.int32, (128, new_len), 0)
-    page_row = lax.broadcasted_iota(jnp.int32, (page_len, 2 * new_len), 0)
     new_row = lax.broadcasted_iota(jnp.int32, (local_new, 2 * new_len), 0) + place[0] * local_new
     new_col = lax.broadcasted_iota(jnp.int32, (local_new, 2 * new_len), 1) % new_len
     new_valid = new_row <= new_col
@@ -53,17 +52,30 @@
         top_sc[...] = jnp.zeros_like(top_sc)
         den_sc[...] = jnp.zeros_like(den_sc)
 
-    for pair in range(pairs):
+    lane = lax.broadcasted_iota(jnp.int32, (page_len, 128), 1)
+    key = lax.broadcasted_iota(jnp.int32, (page_len, 128), 0)
+    biases = [jnp.where((lane == 0) & (key >= limits[i]), NEG_FILL, 0.0).astype(BF16) for i in range(pages)]
+    one = jnp.where(lax.broadcasted_iota(jnp.int32, (2 * new_len, 128), 1) == 0, 1.0, 0.0).astype(BF16)
+
+    def score(pair):
         at = slice(pair * 128, pair * 128 + 128)
         q = q_ref[0, :, at].astype(F32) * SCORE_SCALE
         both = jnp.concatenate([jnp.where(col < HD, q, 0.0), jnp.where(col < HD, 0.0, q)], axis=0).astype(BF16)
-        parts = [
-            jnp.where(page_row < limits[i], nt_dot(k_ref[0, places[i], 0, :, at], both), NEG_FILL) for i in range(pages)
-        ]
-        parts.append(jnp.where(new_valid, nt_dot(nk_ref[0, 0, :, at], both), NEG_FILL))
-        top = functools.reduce(jnp.maximum, [jnp.max(s, axis=0, keepdims=True) for s in parts])
-        top = top.astype(BF16).astype(F32)
-        weights = [jnp.exp(s - top) for s in parts]
+        wide = jnp.concatenate([both, one], axis=1)
+        for i in range(pages):
+            keys = jnp.concatenate([k_ref[0, places[i], 0, :, at], biases[i]], axis=1)
+            score_sc[pair % 2, i * page_len : (i + 1) * page_len, :] = nt_dot(keys, wide)
+        score_sc[pair % 2, pages * page_len :, :] = jnp.where(new_valid, nt_dot(nk_ref[0, 0, :, at], both), NEG_FILL)
+
+    score(0)
+    for pair in range(pairs):
+        at = slice(pair * 128, pair * 128 + 128)
+        if pair + 1 < pairs:
+            score(pair + 1)
+        cuts = [slice(i * page_len, (i + 1) * page_len) for i in range(pages)] + [slice(pages * page_len, None)]
+        tops = [jnp.max(score_sc[pair % 2, cut, :], axis=0, keepdims=True) for cut in cuts]
+        top = functools.reduce(jnp.maximum, tops).astype(BF16).astype(F32)
+        weights = [jnp.exp(score_sc[pair % 2, cut, :] - top) for cut in cuts]
         den = functools.reduce(jnp.add, [jnp.sum(w, axis=0, keepdims=True) for w in weights])
         low = jnp.concatenate([w.astype(BF16) for w in weights[:-1]], axis=0)
         values = jnp.concatenate([v_ref[0, places[i], 0, :, at] for i in range(pages)], axis=0)
@@ -113,7 +125,8 @@
                 pl.BlockSpec((1, 1, local_new, block), lambda r, g, *_: (r, 1, 0, g)),
             ],
             out_specs=[pl.BlockSpec((dests // 2, share + STAT_ROWS, req_here * new_len), lambda r, g, *_: (0, 0, 0))] * 2,
-            scratch_shapes=[pltpu.VMEM((2, dests // 2, share + STAT_ROWS, req_here * new_len), BF16)]
+            scratch_shapes=[pltpu.VMEM((2, keys, 2 * new_len), F32)]
+            + [pltpu.VMEM((2, dests // 2, share + STAT_ROWS, req_here * new_len), BF16)]
             + [pltpu.VMEM((heads + 12, 1, req_here * new_len), F32)] * 2,
         ),
         out_shape=[jax.ShapeDtypeStruct((dests // 2, share + STAT_ROWS, req_here * new_len), BF16)] * 2,

time: 220 us -> 219 us (level)
  Pallas kernels: 43.2 us -> 40.1 us
    pallas_call x1, Pallas kernels: 18 us -> 15 us  [attend(): pl.pallas_call(functools.partial(attend_kernel, share=share), grid_spec=p...]
    all_to_all x2, waiting for transfers between devices: 0.01 us -> 2.51 us  [exchange(): return lax.all_to_all(x, 'narrow', 0, 0, tiled=True)]
  transfers between devices with their start and end apart: 45 -> 45, of which waited for: 20 -> 20; matrix products, arithmetic and copies ran while one was open for 4% -> 4% of each run, Pallas kernels for 19% -> 18%
where the time goes in v5:
time: 219 us; the launch traced here: 218 us
  starting transfers between devices  75.5 us (34%)
  waiting for transfers between devices  70.6 us (32%)
  Pallas kernels  40.1 us (18%)
  blocking collectives  20.7 us (9%)
  local copies, waits for them, and re-layouts  7.82 us (4%)
  other arithmetic  2.53 us (1%)
    ppermute x32, starting transfers between devices, shift(): return lax.ppermute(x, 'wide', ring_pairs(axis, step))  49.6 us
    ppermute x10, waiting for transfers between devices, along(): lax.ppermute(x, 'narrow', [(i, (i + step) % narrow_count) for i in range(...  43.9 us
    ppermute x32, waiting for transfers between devices, shift(): return lax.ppermute(x, 'wide', ring_pairs(axis, step))  21.9 us
    all_to_all x1, blocking collectives, exchange(): return lax.all_to_all(x, 'narrow', 0, 0, tiled=True)  20.7 us
    pallas_call x2, Pallas kernels, expert(): pl.pallas_call(functools.partial(expert_kernel, count=count), in_specs=[p...  20.4 us
    pallas_call x1, Pallas kernels, attend(): pl.pallas_call(functools.partial(attend_kernel, share=share), grid_spec=p...  15 us
    ppermute x10, starting transfers between devices, along(): lax.ppermute(x, 'narrow', [(i, (i + step) % narrow_count) for i in range(...  14.5 us
    all_to_all x2, starting transfers between devices, exchange(): return lax.all_to_all(x, 'narrow', 0, 0, tiled=True)  11.4 us
  transfers between devices with their start and end apart: 45, of which 20 were waited for; matrix products, arithmetic and copies ran while one was open for 4% of the time, Pallas kernels for 18%

profile of v5, /device:TPU:1, one launch (start us, length us, event | category | flops | bytes accessed | tf_op | source)
XLA Modules:
  0.0 218.0 jit_solution(16461550266815840348)
XLA Ops:
  0.0 5.9 %all-to-all-start = ((bf16[8,288,360]{2,1,0:T(8,128)(2,1)}), bf16[8,288,360]{2,1,0:T(8,128)(2,1)}, u32[]{:S(2)}, u32[]{:S(2)}) async-start(bf16[8,288,360]{2,1,0:T(8,128)(2,1)} %bitcast.32), calls=%async_computation | async-start | bytes 3538944 | tf_op jit(solution)/shard_map/all_to_all | solution.py:454
  5.9 15.0 %attend.1 = (bf16[4,304,256]{2,1,0:T(8,128)(2,1)}, bf16[4,304,256]{2,1,0:T(8,128)(2,1)}) custom-call(s32[2,32]{1,0:T(2,128)} %table.1, s32[2]{0:T(128)} %length.1, s32[1]{0:T(128)} %bitcast.place, bf16[2,128,2304]{2,1,0:T(8,128)(2,1)} %q_ref.1, bf16[2,4,2,128,2304]{4,3,2,1,0:T(8,128)(2,1)} %v_ref.1, bf16[2,4,2,128,2304]{4,3,2,1,0:T(8,128)(2,1)} %v_ref.1, ...), custom_call_target="tpu_custom_call" | custom-call | flops 1245708288 | bytes 10616832 | tf_op jit(solution)/shard_map/attend/pallas_call | solution.py:115
  20.9 2.3 %collective-permute-done.other_ref = bf16[4,304,256]{2,1,0:T(8,128)(2,1)S(1)} collective-permute-done((bf16[4,304,256]{2,1,0:T(8,128)(2,1)}, bf16[4,304,256]{2,1,0:T(8,128)(2,1)S(1)}, u32[]{:S(2)}, u32[]{:S(2)}) %collective-permute-start) | collective-permute-done | bytes 622624 | tf_op jit(solution)/shard_map/ppermute | solution.py:459
  26.2 2.5 %all-to-all-done = bf16[8,288,360]{2,1,0:T(8,128)(2,1)} async-done(((bf16[8,288,360]{2,1,0:T(8,128)(2,1)}), bf16[8,288,360]{2,1,0:T(8,128)(2,1)}, u32[]{:S(2)}, u32[]{:S(2)}) %all-to-all-start) | async-done | bytes 1658912 | tf_op jit(solution)/shard_map/all_to_all | solution.py:454
  28.7 4.3 %copy.21 = bf16[8,288,2,360]{3,1,2,0:T(8,128)(2,1)} copy(bf16[8,288,2,360]{3,2,1,0:T(2,128)(2,1)} %param.20) | data formatting | bytes 6635520 | tf_op jit(solution)/shard_map/optimization_barrier | solution.py:465
  33.0 5.5 %all-to-all-start.1 = ((bf16[8,2,288,360]{3,2,1,0:T(8,128)(2,1)}), bf16[8,2,288,360]{3,2,1,0:T(8,128)(2,1)}, u32[]{:S(2)}, u32[]{:S(2)}) async-start(bf16[8,2,288,360]{3,2,1,0:T(8,128)(2,1)} %bitcast.31), calls=%async_computation.1 | async-start | bytes 7077888 | tf_op jit(solution)/shard_map/all_to_all | solution.py:454
  40.5 3.0 %collective-permute-start.2 = (bf16[304,256]{1,0:T(8,128)(2,1)S(1)}, bf16[304,256]{1,0:T(8,128)(2,1)S(1)}, u32[]{:S(2)}, u32[]{:S(2)}) collective-permute-start(bf16[304,256]{1,0:T(8,128)(2,1)S(1)} %get-tuple-element.65), channel_id=1, source_target_pairs={{0,4},{1,5},{2,6},{3,7},{4,0},{5,1},{6,2},{7,3},{8,12},{9,13},{10,... | collective-permute-start | bytes 466952 | tf_op jit(solution)/shard_map/ppermute | solution.py:462
  44.4 39.2 %collective-permute-done.2.refs_2_ = bf16[304,256]{1,0:T(8,128)(2,1)S(1)} collective-permute-done((bf16[304,256]{1,0:T(8,128)(2,1)S(1)}, bf16[304,256]{1,0:T(8,128)(2,1)S(1)}, u32[]{:S(2)}, u32[]{:S(2)}) %collective-permute-start.2) | collective-permute-done | bytes 155680 | tf_op jit(solution)/shard_map/ppermute | solution.py:462
  86.8 2.0 collective-permute-start.4
  92.0 2.1 collective-permute-start.8
  99.3 3.8 %collective-permute-start.13 = (bf16[40,2304]{1,0:T(8,128)(2,1)S(1)}, bf16[40,2304]{1,0:T(8,128)(2,1)S(1)}, u32[]{:S(2)}, u32[]{:S(2)}) collective-permute-start(bf16[40,2304]{1,0:T(8,128)(2,1)S(1)} %get-tuple-element.112.refs_0_), channel_id=1, source_target_pairs={{0,24},{8,0},{16,8},{24,16},{32,56},{40,32},{48,40},{56,48},{64,88... | collective-permute-start | bytes 552968 | tf_op jit(solution)/shard_map/ppermute | solution.py:429
  104.4 2.7 %collective-permute-start.20 = (bf16[40,2304]{1,0:T(8,128)(2,1)S(1)}, bf16[40,2304]{1,0:T(8,128)(2,1)S(1)}, u32[]{:S(2)}, u32[]{:S(2)}) collective-permute-start(bf16[40,2304]{1,0:T(8,128)(2,1)S(1)} %get-tuple-element.111.refs_0_), channel_id=1, source_target_pairs={{0,96},{8,104},{16,112},{24,120},{32,0},{40,8},{48,16},{56,24},{64... | collective-permute-start | bytes 552968 | tf_op jit(solution)/shard_map/ppermute | solution.py:429
  107.2 3.7 %collective-permute-done.13.refs_3_ = bf16[40,2304]{1,0:T(8,128)(2,1)S(1)} collective-permute-done((bf16[40,2304]{1,0:T(8,128)(2,1)S(1)}, bf16[40,2304]{1,0:T(8,128)(2,1)S(1)}, u32[]{:S(2)}, u32[]{:S(2)}) %collective-permute-start.13) | collective-permute-done | bytes 184352 | tf_op jit(solution)/shard_map/ppermute | solution.py:429
  110.9 2.9 %collective-permute-start.18 = (bf16[40,2304]{1,0:T(8,128)(2,1)S(1)}, bf16[40,2304]{1,0:T(8,128)(2,1)S(1)}, u32[]{:S(2)}, u32[]{:S(2)}) collective-permute-start(bf16[40,2304]{1,0:T(8,128)(2,1)S(1)} %get-tuple-element.111.refs_0_), channel_id=1, source_target_pairs={{0,64},{8,72},{16,80},{24,88},{32,96},{40,104},{48,112},{56,120},{... | collective-permute-start | bytes 552968 | tf_op jit(solution)/shard_map/ppermute | solution.py:429
  114.2 2.8 %collective-permute-start.16 = (bf16[80,2304]{1,0:T(8,128)(2,1)S(1)}, bf16[80,2304]{1,0:T(8,128)(2,1)S(1)}, u32[]{:S(2)}, u32[]{:S(2)}) collective-permute-start(bf16[80,2304]{1,0:T(8,128)(2,1)S(1)} %bitcast.22), channel_id=1, source_target_pairs={{0,96},{8,104},{16,112},{24,120},{32,0},{40,8},{48,16},{56,24},{64... | collective-permute-start | bytes 1105928 | tf_op jit(solution)/shard_map/ppermute | solution.py:429
  117.6 3.8 %collective-permute-start.23 = (bf16[80,2304]{1,0:T(8,128)(2,1)S(1)}, bf16[80,2304]{1,0:T(8,128)(2,1)S(1)}, u32[]{:S(2)}, u32[]{:S(2)}) collective-permute-start(bf16[80,2304]{1,0:T(8,128)(2,1)S(1)} %bitcast.28), channel_id=1, source_target_pairs={{0,24},{8,0},{16,8},{24,16},{32,56},{40,32},{48,40},{56,48},{64,88... | collective-permute-start | bytes 1105928 | tf_op jit(solution)/shard_map/ppermute | solution.py:429
  121.4 4.4 %collective-permute-done.16.refs_1_ = bf16[80,2304]{1,0:T(8,128)(2,1)S(1)} collective-permute-done((bf16[80,2304]{1,0:T(8,128)(2,1)S(1)}, bf16[80,2304]{1,0:T(8,128)(2,1)S(1)}, u32[]{:S(2)}, u32[]{:S(2)}) %collective-permute-start.16) | collective-permute-done | bytes 368672 | tf_op jit(solution)/shard_map/ppermute | solution.py:429
  125.8 3.4 %collective-permute-start.17 = (bf16[80,2304]{1,0:T(8,128)(2,1)S(1)}, bf16[80,2304]{1,0:T(8,128)(2,1)S(1)}, u32[]{:S(2)}, u32[]{:S(2)}) collective-permute-start(bf16[80,2304]{1,0:T(8,128)(2,1)S(1)} %collective-permute-done.16.refs_1_), channel_id=1, source_target_pairs={{0,96},{8,104},{16,112},{24,120},{32,0},{40,8},{48,16},{56,24},{64... | collective-permute-start | bytes 1105928 | tf_op jit(solution)/shard_map/ppermute | solution.py:429
  129.3 4.0 %collective-permute-start.24 = (bf16[80,2304]{1,0:T(8,128)(2,1)S(1)}, bf16[80,2304]{1,0:T(8,128)(2,1)S(1)}, u32[]{:S(2)}, u32[]{:S(2)}) collective-permute-start(bf16[80,2304]{1,0:T(8,128)(2,1)S(1)} %collective-permute-done.23.refs_5_), channel_id=1, source_target_pairs={{0,24},{8,0},{16,8},{24,16},{32,56},{40,32},{48,40},{56,48},{64,88... | collective-permute-start | bytes 1105928 | tf_op jit(solution)/shard_map/ppermute | solution.py:429
  133.3 2.6 %collective-permute-done.17.refs_2_ = bf16[80,2304]{1,0:T(8,128)(2,1)S(1)} collective-permute-done((bf16[80,2304]{1,0:T(8,128)(2,1)S(1)}, bf16[80,2304]{1,0:T(8,128)(2,1)S(1)}, u32[]{:S(2)}, u32[]{:S(2)}) %collective-permute-start.17) | collective-permute-done | bytes 368672 | tf_op jit(solution)/shard_map/ppermute | solution.py:429
  136.0 3.4 %collective-permute-start.25 = (bf16[80,2304]{1,0:T(8,128)(2,1)S(1)}, bf16[80,2304]{1,0:T(8,128)(2,1)}, u32[]{:S(2)}, u32[]{:S(2)}) collective-permute-start(bf16[80,2304]{1,0:T(8,128)(2,1)S(1)} %bitcast.20), channel_id=1, source_target_pairs={{0,96},{8,104},{16,112},{24,120},{32,0},{40,8},{48,16},{56,24},{64... | collective-permute-start | bytes 1105928 | tf_op jit(solution)/shard_map/ppermute | solution.py:429
  140.4 3.7 %collective-permute-start.27 = (bf16[80,2304]{1,0:T(8,128)(2,1)S(1)}, bf16[80,2304]{1,0:T(8,128)(2,1)}, u32[]{:S(2)}, u32[]{:S(2)}) collective-permute-start(bf16[80,2304]{1,0:T(8,128)(2,1)S(1)} %bitcast.26), channel_id=1, source_target_pairs={{0,24},{8,0},{16,8},{24,16},{32,56},{40,32},{48,40},{56,48},{64,88... | collective-permute-start | bytes 1105928 | tf_op jit(solution)/shard_map/ppermute | solution.py:429
  144.2 10.2 %expert.2 = (bf16[160,2304]{1,0:T(8,128)(2,1)}, bf16[160,2304]{1,0:T(8,128)(2,1)}, bf16[160,2304]{1,0:T(8,128)(2,1)}, bf16[160,2304]{1,0:T(8,128)(2,1)}) custom-call(s32[1]{0:T(128)} %bitcast.place, bf16[80,2304]{1,0:T(8,128)(2,1)} %copy-done.21, bf16[80,2304]{1,0:T(8,128)(2,1)} %copy-done.16, bf16[80,2304]{1,0:T(8,128)(2,1)} %copy-done.20, ...), custom_call_target="tpu_custom_call" | custom-call | flops 3185049600 | bytes 10874880 | tf_op jit(solution)/shard_map/expert/pallas_call | solution.py:325
  154.5 2.7 %collective-permute-start.31 = (bf16[160,2304]{1,0:T(8,128)(2,1)}, bf16[160,2304]{1,0:T(8,128)(2,1)}, u32[]{:S(2)}, u32[]{:S(2)}) collective-permute-start(bf16[160,2304]{1,0:T(8,128)(2,1)} %get-tuple-element.93), channel_id=1, source_target_pairs={{0,96},{8,104},{16,112},{24,120},{32,0},{40,8},{48,16},{56,24},{64... | collective-permute-start | bytes 2211848 | tf_op jit(solution)/shard_map/ppermute | solution.py:429
  157.2 2.7 %collective-permute-start.38 = (bf16[160,2304]{1,0:T(8,128)(2,1)}, bf16[160,2304]{1,0:T(8,128)(2,1)S(1)}, u32[]{:S(2)}, u32[]{:S(2)}) collective-permute-start(bf16[160,2304]{1,0:T(8,128)(2,1)} %get-tuple-element.103), channel_id=1, source_target_pairs={{0,24},{8,0},{16,8},{24,16},{32,56},{40,32},{48,40},{56,48},{64,88... | collective-permute-start | bytes 2211848 | tf_op jit(solution)/shard_map/ppermute | solution.py:429
  159.9 10.3 %expert.3 = (bf16[80,2304]{1,0:T(8,128)(2,1)}, bf16[80,2304]{1,0:T(8,128)(2,1)}, bf16[80,2304]{1,0:T(8,128)(2,1)}, bf16[80,2304]{1,0:T(8,128)(2,1)}, bf16[80,230...) custom-call(s32[1]{0:T(128)} %bitcast.place, ...), custom_call_target="tpu_custom_call" | custom-call | flops 3185049600 | bytes 10874880 | tf_op jit(solution)/shard_map/expert/pallas_call | solution.py:325
  173.6 2.7 %collective-permute-start.32 = (bf16[80,2304]{1,0:T(8,128)(2,1)S(1)}, bf16[80,2304]{1,0:T(8,128)(2,1)S(1)}, u32[]{:S(2)}, u32[]{:S(2)}) collective-permute-start(bf16[80,2304]{1,0:T(8,128)(2,1)S(1)} %add_convert_fusion.2), channel_id=1, source_target_pairs={{0,96},{8,104},{16,112},{24,120},{32,0},{40,8},{48,16},{56,24},{64... | collective-permute-start | bytes 1105928 | tf_op jit(solution)/shard_map/ppermute | solution.py:429
  176.6 2.7 %collective-permute-start.39 = (bf16[80,2304]{1,0:T(8,128)(2,1)S(1)}, bf16[80,2304]{1,0:T(8,128)(2,1)S(1)}, u32[]{:S(2)}, u32[]{:S(2)}) collective-permute-start(bf16[80,2304]{1,0:T(8,128)(2,1)S(1)} %add_convert_fusion), channel_id=1, source_target_pairs={{0,24},{8,0},{16,8},{24,16},{32,56},{40,32},{48,40},{56,48},{64,88... | collective-permute-start | bytes 1105928 | tf_op jit(solution)/shard_map/ppermute | solution.py:429
  185.8 2.0 collective-permute-start.40
  190.1 3.0 %collective-permute-done.34.refs_2_ = bf16[40,2304]{1,0:T(8,128)(2,1)S(1)} collective-permute-done((bf16[40,2304]{1,0:T(8,128)(2,1)S(1)}, bf16[40,2304]{1,0:T(8,128)(2,1)S(1)}, u32[]{:S(2)}, u32[]{:S(2)}) %collective-permute-start.34) | collective-permute-done | bytes 184352 | tf_op jit(solution)/shard_map/ppermute | solution.py:429
  193.1 2.0 collective-permute-done.35.refs_3_
  196.2 20.7 %all_to_all.15 = bf16[8,80,288]{2,1,0:T(8,128)(2,1)S(1)} all-to-all(bf16[8,80,288]{2,1,0:T(8,128)(2,1)S(1)} %finish.1), channel_id=1, replica_groups=mesh['wide'=16,'narrow'=8] {'narrow'}, dimensions={0} | all-to-all | bytes 737280 | tf_op jit(solution)/shard_map/all_to_all | solution.py:454
  (135 shorter events, 35.7 us)
Async XLA Ops:
  0.0 28.7 %all-to-all-start = ((bf16[8,288,360]{2,1,0:T(8,128)(2,1)}), bf16[8,288,360]{2,1,0:T(8,128)(2,1)}, u32[]{:S(2)}, u32[]{:S(2)}) async-start(bf16[8,288,360]{2,1,0:T(8,128)(2,1)} %bitcast.32), calls=%async_computation | async-start | bytes 3538944 | tf_op jit(solution)/shard_map/all_to_all | solution.py:454
  24.8 8.2 %collective-permute-start.1 = (bf16[304,256]{1,0:T(8,128)(2,1)S(1)}, bf16[304,256]{1,0:T(8,128)(2,1)S(1)}, u32[]{:S(2)}, u32[]{:S(2)}) collective-permute-start(bf16[304,256]{1,0:T(8,128)(2,1)S(1)} %get-tuple-element.63), channel_id=1, source_target_pairs={{0,2},{1,3},{2,4},{3,5},{4,6},{5,7},{6,0},{7,1},{8,10},{9,11},{10,... | collective-permute-start | bytes 466952 | tf_op jit(solution)/shard_map/ppermute | solution.py:462
  33.0 111.1 %all-to-all-start.1 = ((bf16[8,2,288,360]{3,2,1,0:T(8,128)(2,1)}), bf16[8,2,288,360]{3,2,1,0:T(8,128)(2,1)}, u32[]{:S(2)}, u32[]{:S(2)}) async-start(bf16[8,2,288,360]{3,2,1,0:T(8,128)(2,1)} %bitcast.31), calls=%async_computation.1 | async-start | bytes 7077888 | tf_op jit(solution)/shard_map/all_to_all | solution.py:454
  40.5 43.0 %collective-permute-start.2 = (bf16[304,256]{1,0:T(8,128)(2,1)S(1)}, bf16[304,256]{1,0:T(8,128)(2,1)S(1)}, u32[]{:S(2)}, u32[]{:S(2)}) collective-permute-start(bf16[304,256]{1,0:T(8,128)(2,1)S(1)} %get-tuple-element.65), channel_id=1, source_target_pairs={{0,4},{1,5},{2,6},{3,7},{4,0},{5,1},{6,2},{7,3},{8,12},{9,13},{10,... | collective-permute-start | bytes 466952 | tf_op jit(solution)/shard_map/ppermute | solution.py:462
  43.5 41.9 %collective-permute-start.3 = (bf16[304,256]{1,0:T(8,128)(2,1)S(1)}, bf16[304,256]{1,0:T(8,128)(2,1)S(1)}, u32[]{:S(2)}, u32[]{:S(2)}) collective-permute-start(bf16[304,256]{1,0:T(8,128)(2,1)S(1)} %get-tuple-element.66), channel_id=1, source_target_pairs={{0,6},{1,7},{2,0},{3,1},{4,2},{5,3},{6,4},{7,5},{8,14},{9,15},{10,... | collective-permute-start | bytes 466952 | tf_op jit(solution)/shard_map/ppermute | solution.py:462
  99.3 11.6 %collective-permute-start.13 = (bf16[40,2304]{1,0:T(8,128)(2,1)S(1)}, bf16[40,2304]{1,0:T(8,128)(2,1)S(1)}, u32[]{:S(2)}, u32[]{:S(2)}) collective-permute-start(bf16[40,2304]{1,0:T(8,128)(2,1)S(1)} %get-tuple-element.112.refs_0_), channel_id=1, source_target_pairs={{0,24},{8,0},{16,8},{24,16},{32,56},{40,32},{48,40},{56,48},{64,88... | collective-permute-start | bytes 552968 | tf_op jit(solution)/shard_map/ppermute | solution.py:429
  103.1 11.0 %collective-permute-start.12 = (bf16[40,2304]{1,0:T(8,128)(2,1)S(1)}, bf16[40,2304]{1,0:T(8,128)(2,1)S(1)}, u32[]{:S(2)}, u32[]{:S(2)}) collective-permute-start(bf16[40,2304]{1,0:T(8,128)(2,1)S(1)} %get-tuple-element.112.refs_0_), channel_id=1, source_target_pairs={{0,8},{8,16},{16,24},{24,0},{32,40},{40,48},{48,56},{56,32},{64,72... | collective-permute-start | bytes 552968 | tf_op jit(solution)/shard_map/ppermute | solution.py:429
  103.1 11.0 %collective-permute-start.11 = (bf16[40,2304]{1,0:T(8,128)(2,1)S(1)}, bf16[40,2304]{1,0:T(8,128)(2,1)S(1)}, u32[]{:S(2)}, u32[]{:S(2)}) collective-permute-start(bf16[40,2304]{1,0:T(8,128)(2,1)S(1)} %get-tuple-element.112.refs_0_), channel_id=1, source_target_pairs={{0,16},{8,24},{16,0},{24,8},{32,48},{40,56},{48,32},{56,40},{64,80... | collective-permute-start | bytes 552968 | tf_op jit(solution)/shard_map/ppermute | solution.py:429
  104.4 12.6 %collective-permute-start.20 = (bf16[40,2304]{1,0:T(8,128)(2,1)S(1)}, bf16[40,2304]{1,0:T(8,128)(2,1)S(1)}, u32[]{:S(2)}, u32[]{:S(2)}) collective-permute-start(bf16[40,2304]{1,0:T(8,128)(2,1)S(1)} %get-tuple-element.111.refs_0_), channel_id=1, source_target_pairs={{0,96},{8,104},{16,112},{24,120},{32,0},{40,8},{48,16},{56,24},{64... | collective-permute-start | bytes 552968 | tf_op jit(solution)/shard_map/ppermute | solution.py:429
  107.2 9.9 %collective-permute-start.19 = (bf16[40,2304]{1,0:T(8,128)(2,1)S(1)}, bf16[40,2304]{1,0:T(8,128)(2,1)S(1)}, u32[]{:S(2)}, u32[]{:S(2)}) collective-permute-start(bf16[40,2304]{1,0:T(8,128)(2,1)S(1)} %get-tuple-element.111.refs_0_), channel_id=1, source_target_pairs={{0,32},{8,40},{16,48},{24,56},{32,64},{40,72},{48,80},{56,88},{64,... | collective-permute-start | bytes 552968 | tf_op jit(solution)/shard_map/ppermute | solution.py:429
  114.2 11.6 %collective-permute-start.16 = (bf16[80,2304]{1,0:T(8,128)(2,1)S(1)}, bf16[80,2304]{1,0:T(8,128)(2,1)S(1)}, u32[]{:S(2)}, u32[]{:S(2)}) collective-permute-start(bf16[80,2304]{1,0:T(8,128)(2,1)S(1)} %bitcast.22), channel_id=1, source_target_pairs={{0,96},{8,104},{16,112},{24,120},{32,0},{40,8},{48,16},{56,24},{64... | collective-permute-start | bytes 1105928 | tf_op jit(solution)/shard_map/ppermute | solution.py:429
  117.0 12.2 %collective-permute-start.14 = (bf16[80,2304]{1,0:T(8,128)(2,1)S(1)}, bf16[80,2304]{1,0:T(8,128)(2,1)S(1)}, u32[]{:S(2)}, u32[]{:S(2)}) collective-permute-start(bf16[80,2304]{1,0:T(8,128)(2,1)S(1)} %bitcast.19), channel_id=1, source_target_pairs={{0,32},{8,40},{16,48},{24,56},{32,64},{40,72},{48,80},{56,88},{64,... | collective-permute-start | bytes 1105928 | tf_op jit(solution)/shard_map/ppermute | solution.py:429
  117.6 11.6 %collective-permute-start.23 = (bf16[80,2304]{1,0:T(8,128)(2,1)S(1)}, bf16[80,2304]{1,0:T(8,128)(2,1)S(1)}, u32[]{:S(2)}, u32[]{:S(2)}) collective-permute-start(bf16[80,2304]{1,0:T(8,128)(2,1)S(1)} %bitcast.28), channel_id=1, source_target_pairs={{0,24},{8,0},{16,8},{24,16},{32,56},{40,32},{48,40},{56,48},{64,88... | collective-permute-start | bytes 1105928 | tf_op jit(solution)/shard_map/ppermute | solution.py:429
  121.4 11.9 %collective-permute-start.21 = (bf16[80,2304]{1,0:T(8,128)(2,1)S(1)}, bf16[80,2304]{1,0:T(8,128)(2,1)S(1)}, u32[]{:S(2)}, u32[]{:S(2)}) collective-permute-start(bf16[80,2304]{1,0:T(8,128)(2,1)S(1)} %bitcast.25), channel_id=1, source_target_pairs={{0,8},{8,16},{16,24},{24,0},{32,40},{40,48},{48,56},{56,32},{64,72... | collective-permute-start | bytes 1105928 | tf_op jit(solution)/shard_map/ppermute | solution.py:429
  125.8 10.1 %collective-permute-start.17 = (bf16[80,2304]{1,0:T(8,128)(2,1)S(1)}, bf16[80,2304]{1,0:T(8,128)(2,1)S(1)}, u32[]{:S(2)}, u32[]{:S(2)}) collective-permute-start(bf16[80,2304]{1,0:T(8,128)(2,1)S(1)} %collective-permute-done.16.refs_1_), channel_id=1, source_target_pairs={{0,96},{8,104},{16,112},{24,120},{32,0},{40,8},{48,16},{56,24},{64... | collective-permute-start | bytes 1105928 | tf_op jit(solution)/shard_map/ppermute | solution.py:429
  129.2 10.1 %collective-permute-start.15 = (bf16[80,2304]{1,0:T(8,128)(2,1)S(1)}, bf16[80,2304]{1,0:T(8,128)(2,1)S(1)}, u32[]{:S(2)}, u32[]{:S(2)}) collective-permute-start(bf16[80,2304]{1,0:T(8,128)(2,1)S(1)} %collective-permute-done.14.refs_3_), channel_id=1, source_target_pairs={{0,32},{8,40},{16,48},{24,56},{32,64},{40,72},{48,80},{56,88},{64,... | collective-permute-start | bytes 1105928 | tf_op jit(solution)/shard_map/ppermute | solution.py:429
  129.3 11.2 %collective-permute-start.24 = (bf16[80,2304]{1,0:T(8,128)(2,1)S(1)}, bf16[80,2304]{1,0:T(8,128)(2,1)S(1)}, u32[]{:S(2)}, u32[]{:S(2)}) collective-permute-start(bf16[80,2304]{1,0:T(8,128)(2,1)S(1)} %collective-permute-done.23.refs_5_), channel_id=1, source_target_pairs={{0,24},{8,0},{16,8},{24,16},{32,56},{40,32},{48,40},{56,48},{64,88... | collective-permute-start | bytes 1105928 | tf_op jit(solution)/shard_map/ppermute | solution.py:429
  133.3 10.9 %collective-permute-start.22 = (bf16[80,2304]{1,0:T(8,128)(2,1)S(1)}, bf16[80,2304]{1,0:T(8,128)(2,1)}, u32[]{:S(2)}, u32[]{:S(2)}) collective-permute-start(bf16[80,2304]{1,0:T(8,128)(2,1)S(1)} %collective-permute-done.21.refs_7_), channel_id=1, source_target_pairs={{0,8},{8,16},{16,24},{24,0},{32,40},{40,48},{48,56},{56,32},{64,72... | collective-permute-start | bytes 1105928 | tf_op jit(solution)/shard_map/ppermute | solution.py:429
  133.3 21.2 %collective-permute-start.26 = (bf16[80,2304]{1,0:T(8,128)(2,1)S(1)}, bf16[80,2304]{1,0:T(8,128)(2,1)}, u32[]{:S(2)}, u32[]{:S(2)}) collective-permute-start(bf16[80,2304]{1,0:T(8,128)(2,1)S(1)} %bitcast.23), channel_id=1, source_target_pairs={{0,32},{8,40},{16,48},{24,56},{32,64},{40,72},{48,80},{56,88},{64,... | collective-permute-start | bytes 1105928 | tf_op jit(solution)/shard_map/ppermute | solution.py:429
  136.0 18.5 %collective-permute-start.25 = (bf16[80,2304]{1,0:T(8,128)(2,1)S(1)}, bf16[80,2304]{1,0:T(8,128)(2,1)}, u32[]{:S(2)}, u32[]{:S(2)}) collective-permute-start(bf16[80,2304]{1,0:T(8,128)(2,1)S(1)} %bitcast.20), channel_id=1, source_target_pairs={{0,96},{8,104},{16,112},{24,120},{32,0},{40,8},{48,16},{56,24},{64... | collective-permute-start | bytes 1105928 | tf_op jit(solution)/shard_map/ppermute | solution.py:429
  139.4 15.1 %collective-permute-start.28 = (bf16[80,2304]{1,0:T(8,128)(2,1)S(1)}, bf16[80,2304]{1,0:T(8,128)(2,1)}, u32[]{:S(2)}, u32[]{:S(2)}) collective-permute-start(bf16[80,2304]{1,0:T(8,128)(2,1)S(1)} %bitcast.29), channel_id=1, source_target_pairs={{0,8},{8,16},{16,24},{24,0},{32,40},{40,48},{48,56},{56,32},{64,72... | collective-permute-start | bytes 1105928 | tf_op jit(solution)/shard_map/ppermute | solution.py:429
  140.4 14.0 %collective-permute-start.27 = (bf16[80,2304]{1,0:T(8,128)(2,1)S(1)}, bf16[80,2304]{1,0:T(8,128)(2,1)}, u32[]{:S(2)}, u32[]{:S(2)}) collective-permute-start(bf16[80,2304]{1,0:T(8,128)(2,1)S(1)} %bitcast.26), channel_id=1, source_target_pairs={{0,24},{8,0},{16,8},{24,16},{32,56},{40,32},{48,40},{56,48},{64,88... | collective-permute-start | bytes 1105928 | tf_op jit(solution)/shard_map/ppermute | solution.py:429
  154.5 16.7 %collective-permute-start.29 = (bf16[160,2304]{1,0:T(8,128)(2,1)}, bf16[160,2304]{1,0:T(8,128)(2,1)S(1)}, u32[]{:S(2)}, u32[]{:S(2)}) collective-permute-start(bf16[160,2304]{1,0:T(8,128)(2,1)} %get-tuple-element.92), channel_id=1, source_target_pairs={{0,32},{8,40},{16,48},{24,56},{32,64},{40,72},{48,80},{56,88},{64,... | collective-permute-start | bytes 2211848 | tf_op jit(solution)/shard_map/ppermute | solution.py:429
  154.5 17.8 %collective-permute-start.31 = (bf16[160,2304]{1,0:T(8,128)(2,1)}, bf16[160,2304]{1,0:T(8,128)(2,1)}, u32[]{:S(2)}, u32[]{:S(2)}) collective-permute-start(bf16[160,2304]{1,0:T(8,128)(2,1)} %get-tuple-element.93), channel_id=1, source_target_pairs={{0,96},{8,104},{16,112},{24,120},{32,0},{40,8},{48,16},{56,24},{64... | collective-permute-start | bytes 2211848 | tf_op jit(solution)/shard_map/ppermute | solution.py:429
  157.2 19.1 %collective-permute-start.36 = (bf16[160,2304]{1,0:T(8,128)(2,1)}, bf16[160,2304]{1,0:T(8,128)(2,1)S(1)}, u32[]{:S(2)}, u32[]{:S(2)}) collective-permute-start(bf16[160,2304]{1,0:T(8,128)(2,1)} %get-tuple-element.102), channel_id=1, source_target_pairs={{0,8},{8,16},{16,24},{24,0},{32,40},{40,48},{48,56},{56,32},{64,72... | collective-permute-start | bytes 2211848 | tf_op jit(solution)/shard_map/ppermute | solution.py:429
  157.2 19.2 %collective-permute-start.38 = (bf16[160,2304]{1,0:T(8,128)(2,1)}, bf16[160,2304]{1,0:T(8,128)(2,1)S(1)}, u32[]{:S(2)}, u32[]{:S(2)}) collective-permute-start(bf16[160,2304]{1,0:T(8,128)(2,1)} %get-tuple-element.103), channel_id=1, source_target_pairs={{0,24},{8,0},{16,8},{24,16},{32,56},{40,32},{48,40},{56,48},{64,88... | collective-permute-start | bytes 2211848 | tf_op jit(solution)/shard_map/ppermute | solution.py:429
  176.4 9.1 %collective-permute-start.37 = (bf16[80,2304]{1,0:T(8,128)(2,1)S(1)}, bf16[80,2304]{1,0:T(8,128)(2,1)S(1)}, u32[]{:S(2)}, u32[]{:S(2)}) collective-permute-start(bf16[80,2304]{1,0:T(8,128)(2,1)S(1)} %add_convert_fusion.1), channel_id=1, source_target_pairs={{0,8},{8,16},{16,24},{24,0},{32,40},{40,48},{48,56},{56,32},{64,72... | collective-permute-start | bytes 1105928 | tf_op jit(solution)/shard_map/ppermute | solution.py:429
  176.6 8.9 %collective-permute-start.39 = (bf16[80,2304]{1,0:T(8,128)(2,1)S(1)}, bf16[80,2304]{1,0:T(8,128)(2,1)S(1)}, u32[]{:S(2)}, u32[]{:S(2)}) collective-permute-start(bf16[80,2304]{1,0:T(8,128)(2,1)S(1)} %add_convert_fusion), channel_id=1, source_target_pairs={{0,24},{8,0},{16,8},{24,16},{32,56},{40,32},{48,40},{56,48},{64,88... | collective-permute-start | bytes 1105928 | tf_op jit(solution)/shard_map/ppermute | solution.py:429
  182.1 8.0 %collective-permute-start.33 = (bf16[40,2304]{1,0:T(8,128)(2,1)S(1)}, bf16[40,2304]{1,0:T(8,128)(2,1)S(1)}, u32[]{:S(2)}, u32[]{:S(2)}) collective-permute-start(bf16[40,2304]{1,0:T(8,128)(2,1)S(1)} %get-tuple-element.97), channel_id=1, source_target_pairs={{0,16},{8,24},{16,0},{24,8},{32,48},{40,56},{48,32},{56,40},{64,80... | collective-permute-start | bytes 552968 | tf_op jit(solution)/shard_map/ppermute | solution.py:429
  184.0 9.1 %collective-permute-start.34 = (bf16[40,2304]{1,0:T(8,128)(2,1)S(1)}, bf16[40,2304]{1,0:T(8,128)(2,1)S(1)}, u32[]{:S(2)}, u32[]{:S(2)}) collective-permute-start(bf16[40,2304]{1,0:T(8,128)(2,1)S(1)} %get-tuple-element.98), channel_id=1, source_target_pairs={{0,24},{8,0},{16,8},{24,16},{32,56},{40,32},{48,40},{56,48},{64,88... | collective-permute-start | bytes 552968 | tf_op jit(solution)/shard_map/ppermute | solution.py:429
  184.0 11.1 %collective-permute-start.35 = (bf16[40,2304]{1,0:T(8,128)(2,1)S(1)}, bf16[40,2304]{1,0:T(8,128)(2,1)S(1)}, u32[]{:S(2)}, u32[]{:S(2)}) collective-permute-start(bf16[40,2304]{1,0:T(8,128)(2,1)S(1)} %get-tuple-element.99), channel_id=1, source_target_pairs={{0,8},{8,16},{16,24},{24,0},{32,40},{40,48},{48,56},{56,32},{64,72... | collective-permute-start | bytes 552968 | tf_op jit(solution)/shard_map/ppermute | solution.py:429
  185.8 9.3 %collective-permute-start.40 = (bf16[40,2304]{1,0:T(8,128)(2,1)S(1)}, bf16[40,2304]{1,0:T(8,128)(2,1)S(1)}, u32[]{:S(2)}, u32[]{:S(2)}) collective-permute-start(bf16[40,2304]{1,0:T(8,128)(2,1)S(1)} %get-tuple-element.107), channel_id=1, source_target_pairs={{0,64},{8,72},{16,80},{24,88},{32,96},{40,104},{48,112},{56,120},{... | collective-permute-start | bytes 552968 | tf_op jit(solution)/shard_map/ppermute | solution.py:429
  (36 other events, 454.3 us)

commit v6 on v5

--- a/solution.py
+++ b/solution.py
@@ -44,8 +44,9 @@
     new_col = lax.broadcasted_iota(jnp.int32, (local_new, 2 * new_len), 1) % new_len
     new_valid = new_row <= new_col
     logical = [place[0] + i * groups for i in range(pages)]
-    places = [table[req, j] - place[0] * pages for j in logical]
-    limits = [length[req] - j * page_len for j in logical]
+    homes = [table[req, j] - place[0] * pages for j in logical]
+    ends = [length[req] - j * page_len for j in logical]
+    limits = [sum(jnp.where(home == slot, end, 0) for home, end in zip(homes, ends)) for slot in range(pages)]
 
     @pl.when((req == 0) & (group == 0))
     def _():
@@ -63,7 +64,7 @@
         both = jnp.concatenate([jnp.where(col < HD, q, 0.0), jnp.where(col < HD, 0.0, q)], axis=0).astype(BF16)
         wide = jnp.concatenate([both, one], axis=1)
         for i in range(pages):
-            keys = jnp.concatenate([k_ref[0, places[i], 0, :, at], biases[i]], axis=1)
+            keys = jnp.concatenate([k_ref[0, i, 0, :, at], biases[i]], axis=1)
             score_sc[pair % 2, i * page_len : (i + 1) * page_len, :] = nt_dot(keys, wide)
         score_sc[pair % 2, pages * page_len :, :] = jnp.where(new_valid, nt_dot(nk_ref[0, 0, :, at], both), NEG_FILL)
 
@@ -78,7 +79,7 @@
         weights = [jnp.exp(score_sc[pair % 2, cut, :] - top) for cut in cuts]
         den = functools.reduce(jnp.add, [jnp.sum(w, axis=0, keepdims=True) for w in weights])
         low = jnp.concatenate([w.astype(BF16) for w in weights[:-1]], axis=0)
-        values = jnp.concatenate([v_ref[0, places[i], 0, :, at] for i in range(pages)], axis=0)
+        values = jnp.concatenate([v_ref[0, i, 0, :, at] for i in range(pages)], axis=0)
         num = tn_dot(values, low) + tn_dot(nv_ref[0, 0, :, at], weights[-1].astype(BF16))
         num = jnp.where(row < HD, num[:, :new_len], num[:, new_len:]).astype(BF16)
         for piece in range(4):

time: 219 us -> 219 us (level)
  no operation moved by 1% of the time
where the time goes in v6:
time: 219 us; the launch traced here: 218 us
  starting transfers between devices  75.6 us (35%)
  waiting for transfers between devices  70.8 us (32%)
  Pallas kernels  39.8 us (18%)
  blocking collectives  20.7 us (9%)
  local copies, waits for them, and re-layouts  7.82 us (4%)
  other arithmetic  2.53 us (1%)
    ppermute x32, starting transfers between devices, shift(): return lax.ppermute(x, 'wide', ring_pairs(axis, step))  49.6 us
    ppermute x10, waiting for transfers between devices, along(): lax.ppermute(x, 'narrow', [(i, (i + step) % narrow_count) for i in range(...  43.9 us
    ppermute x32, waiting for transfers between devices, shift(): return lax.ppermute(x, 'wide', ring_pairs(axis, step))  21.9 us
    all_to_all x1, blocking collectives, exchange(): return lax.all_to_all(x, 'narrow', 0, 0, tiled=True)  20.7 us
    pallas_call x2, Pallas kernels, expert(): pl.pallas_call(functools.partial(expert_kernel, count=count), in_specs=[p...  20.4 us
    pallas_call x1, Pallas kernels, attend(): pl.pallas_call(functools.partial(attend_kernel, share=share), grid_spec=p...  14.7 us
    ppermute x10, starting transfers between devices, along(): lax.ppermute(x, 'narrow', [(i, (i + step) % narrow_count) for i in range(...  14.6 us
    all_to_all x2, starting transfers between devices, exchange(): return lax.all_to_all(x, 'narrow', 0, 0, tiled=True)  11.5 us
  transfers between devices with their start and end apart: 45, of which 20 were waited for; matrix products, arithmetic and copies ran while one was open for 4% of the time, Pallas kernels for 18%

profile of v6, /device:TPU:1, one launch (start us, length us, event | category | flops | bytes accessed | tf_op | source)
XLA Modules:
  0.0 218.0 jit_solution(17999252060528117062)
XLA Ops:
  0.0 5.9 %all-to-all-start = ((bf16[8,288,360]{2,1,0:T(8,128)(2,1)}), bf16[8,288,360]{2,1,0:T(8,128)(2,1)}, u32[]{:S(2)}, u32[]{:S(2)}) async-start(bf16[8,288,360]{2,1,0:T(8,128)(2,1)} %bitcast.32), calls=%async_computation | async-start | bytes 3538944 | tf_op jit(solution)/shard_map/all_to_all | solution.py:455
  5.9 14.7 %attend.1 = (bf16[4,304,256]{2,1,0:T(8,128)(2,1)}, bf16[4,304,256]{2,1,0:T(8,128)(2,1)}) custom-call(s32[2,32]{1,0:T(2,128)} %table.1, s32[2]{0:T(128)} %length.1, s32[1]{0:T(128)} %bitcast.place, bf16[2,128,2304]{2,1,0:T(8,128)(2,1)} %q_ref.1, bf16[2,4,2,128,2304]{4,3,2,1,0:T(8,128)(2,1)} %v_ref.1, bf16[2,4,2,128,2304]{4,3,2,1,0:T(8,128)(2,1)} %v_ref.1, ...), custom_call_target="tpu_custom_call" | custom-call | flops 1245708288 | bytes 10616832 | tf_op jit(solution)/shard_map/attend/pallas_call | solution.py:116
  20.7 2.3 %collective-permute-done.other_ref = bf16[4,304,256]{2,1,0:T(8,128)(2,1)S(1)} collective-permute-done((bf16[4,304,256]{2,1,0:T(8,128)(2,1)}, bf16[4,304,256]{2,1,0:T(8,128)(2,1)S(1)}, u32[]{:S(2)}, u32[]{:S(2)}) %collective-permute-start) | collective-permute-done | bytes 622624 | tf_op jit(solution)/shard_map/ppermute | solution.py:460
  26.0 2.7 %all-to-all-done = bf16[8,288,360]{2,1,0:T(8,128)(2,1)} async-done(((bf16[8,288,360]{2,1,0:T(8,128)(2,1)}), bf16[8,288,360]{2,1,0:T(8,128)(2,1)}, u32[]{:S(2)}, u32[]{:S(2)}) %all-to-all-start) | async-done | bytes 1658912 | tf_op jit(solution)/shard_map/all_to_all | solution.py:455
  28.7 4.3 %copy.21 = bf16[8,288,2,360]{3,1,2,0:T(8,128)(2,1)} copy(bf16[8,288,2,360]{3,2,1,0:T(2,128)(2,1)} %param.20) | data formatting | bytes 6635520 | tf_op jit(solution)/shard_map/optimization_barrier | solution.py:466
  33.0 5.5 %all-to-all-start.1 = ((bf16[8,2,288,360]{3,2,1,0:T(8,128)(2,1)}), bf16[8,2,288,360]{3,2,1,0:T(8,128)(2,1)}, u32[]{:S(2)}, u32[]{:S(2)}) async-start(bf16[8,2,288,360]{3,2,1,0:T(8,128)(2,1)} %bitcast.31), calls=%async_computation.1 | async-start | bytes 7077888 | tf_op jit(solution)/shard_map/all_to_all | solution.py:455
  40.5 3.0 %collective-permute-start.2 = (bf16[304,256]{1,0:T(8,128)(2,1)S(1)}, bf16[304,256]{1,0:T(8,128)(2,1)S(1)}, u32[]{:S(2)}, u32[]{:S(2)}) collective-permute-start(bf16[304,256]{1,0:T(8,128)(2,1)S(1)} %get-tuple-element.65), channel_id=1, source_target_pairs={{0,4},{1,5},{2,6},{3,7},{4,0},{5,1},{6,2},{7,3},{8,12},{9,13},{10,... | collective-permute-start | bytes 466952 | tf_op jit(solution)/shard_map/ppermute | solution.py:463
  44.4 39.2 %collective-permute-done.2.refs_2_ = bf16[304,256]{1,0:T(8,128)(2,1)S(1)} collective-permute-done((bf16[304,256]{1,0:T(8,128)(2,1)S(1)}, bf16[304,256]{1,0:T(8,128)(2,1)S(1)}, u32[]{:S(2)}, u32[]{:S(2)}) %collective-permute-start.2) | collective-permute-done | bytes 155680 | tf_op jit(solution)/shard_map/ppermute | solution.py:463
  86.8 2.0 collective-permute-start.4
  92.1 2.1 collective-permute-start.8
  99.3 3.8 %collective-permute-start.13 = (bf16[40,2304]{1,0:T(8,128)(2,1)S(1)}, bf16[40,2304]{1,0:T(8,128)(2,1)S(1)}, u32[]{:S(2)}, u32[]{:S(2)}) collective-permute-start(bf16[40,2304]{1,0:T(8,128)(2,1)S(1)} %get-tuple-element.112.refs_0_), channel_id=1, source_target_pairs={{0,24},{8,0},{16,8},{24,16},{32,56},{40,32},{48,40},{56,48},{64,88... | collective-permute-start | bytes 552968 | tf_op jit(solution)/shard_map/ppermute | solution.py:430
  104.5 2.7 %collective-permute-start.20 = (bf16[40,2304]{1,0:T(8,128)(2,1)S(1)}, bf16[40,2304]{1,0:T(8,128)(2,1)S(1)}, u32[]{:S(2)}, u32[]{:S(2)}) collective-permute-start(bf16[40,2304]{1,0:T(8,128)(2,1)S(1)} %get-tuple-element.111.refs_0_), channel_id=1, source_target_pairs={{0,96},{8,104},{16,112},{24,120},{32,0},{40,8},{48,16},{56,24},{64... | collective-permute-start | bytes 552968 | tf_op jit(solution)/shard_map/ppermute | solution.py:430
  107.2 3.7 %collective-permute-done.13.refs_3_ = bf16[40,2304]{1,0:T(8,128)(2,1)S(1)} collective-permute-done((bf16[40,2304]{1,0:T(8,128)(2,1)S(1)}, bf16[40,2304]{1,0:T(8,128)(2,1)S(1)}, u32[]{:S(2)}, u32[]{:S(2)}) %collective-permute-start.13) | collective-permute-done | bytes 184352 | tf_op jit(solution)/shard_map/ppermute | solution.py:430
  110.9 2.9 %collective-permute-start.18 = (bf16[40,2304]{1,0:T(8,128)(2,1)S(1)}, bf16[40,2304]{1,0:T(8,128)(2,1)S(1)}, u32[]{:S(2)}, u32[]{:S(2)}) collective-permute-start(bf16[40,2304]{1,0:T(8,128)(2,1)S(1)} %get-tuple-element.111.refs_0_), channel_id=1, source_target_pairs={{0,64},{8,72},{16,80},{24,88},{32,96},{40,104},{48,112},{56,120},{... | collective-permute-start | bytes 552968 | tf_op jit(solution)/shard_map/ppermute | solution.py:430
  114.3 2.8 %collective-permute-start.16 = (bf16[80,2304]{1,0:T(8,128)(2,1)S(1)}, bf16[80,2304]{1,0:T(8,128)(2,1)S(1)}, u32[]{:S(2)}, u32[]{:S(2)}) collective-permute-start(bf16[80,2304]{1,0:T(8,128)(2,1)S(1)} %bitcast.22), channel_id=1, source_target_pairs={{0,96},{8,104},{16,112},{24,120},{32,0},{40,8},{48,16},{56,24},{64... | collective-permute-start | bytes 1105928 | tf_op jit(solution)/shard_map/ppermute | solution.py:430
  117.6 3.8 %collective-permute-start.23 = (bf16[80,2304]{1,0:T(8,128)(2,1)S(1)}, bf16[80,2304]{1,0:T(8,128)(2,1)S(1)}, u32[]{:S(2)}, u32[]{:S(2)}) collective-permute-start(bf16[80,2304]{1,0:T(8,128)(2,1)S(1)} %bitcast.28), channel_id=1, source_target_pairs={{0,24},{8,0},{16,8},{24,16},{32,56},{40,32},{48,40},{56,48},{64,88... | collective-permute-start | bytes 1105928 | tf_op jit(solution)/shard_map/ppermute | solution.py:430
  121.4 4.4 %collective-permute-done.16.refs_1_ = bf16[80,2304]{1,0:T(8,128)(2,1)S(1)} collective-permute-done((bf16[80,2304]{1,0:T(8,128)(2,1)S(1)}, bf16[80,2304]{1,0:T(8,128)(2,1)S(1)}, u32[]{:S(2)}, u32[]{:S(2)}) %collective-permute-start.16) | collective-permute-done | bytes 368672 | tf_op jit(solution)/shard_map/ppermute | solution.py:430
  125.8 3.4 %collective-permute-start.17 = (bf16[80,2304]{1,0:T(8,128)(2,1)S(1)}, bf16[80,2304]{1,0:T(8,128)(2,1)S(1)}, u32[]{:S(2)}, u32[]{:S(2)}) collective-permute-start(bf16[80,2304]{1,0:T(8,128)(2,1)S(1)} %collective-permute-done.16.refs_1_), channel_id=1, source_target_pairs={{0,96},{8,104},{16,112},{24,120},{32,0},{40,8},{48,16},{56,24},{64... | collective-permute-start | bytes 1105928 | tf_op jit(solution)/shard_map/ppermute | solution.py:430
  129.3 4.0 %collective-permute-start.24 = (bf16[80,2304]{1,0:T(8,128)(2,1)S(1)}, bf16[80,2304]{1,0:T(8,128)(2,1)S(1)}, u32[]{:S(2)}, u32[]{:S(2)}) collective-permute-start(bf16[80,2304]{1,0:T(8,128)(2,1)S(1)} %collective-permute-done.23.refs_5_), channel_id=1, source_target_pairs={{0,24},{8,0},{16,8},{24,16},{32,56},{40,32},{48,40},{56,48},{64,88... | collective-permute-start | bytes 1105928 | tf_op jit(solution)/shard_map/ppermute | solution.py:430
  133.4 2.6 %collective-permute-done.17.refs_2_ = bf16[80,2304]{1,0:T(8,128)(2,1)S(1)} collective-permute-done((bf16[80,2304]{1,0:T(8,128)(2,1)S(1)}, bf16[80,2304]{1,0:T(8,128)(2,1)S(1)}, u32[]{:S(2)}, u32[]{:S(2)}) %collective-permute-start.17) | collective-permute-done | bytes 368672 | tf_op jit(solution)/shard_map/ppermute | solution.py:430
  136.0 3.4 %collective-permute-start.25 = (bf16[80,2304]{1,0:T(8,128)(2,1)S(1)}, bf16[80,2304]{1,0:T(8,128)(2,1)}, u32[]{:S(2)}, u32[]{:S(2)}) collective-permute-start(bf16[80,2304]{1,0:T(8,128)(2,1)S(1)} %bitcast.20), channel_id=1, source_target_pairs={{0,96},{8,104},{16,112},{24,120},{32,0},{40,8},{48,16},{56,24},{64... | collective-permute-start | bytes 1105928 | tf_op jit(solution)/shard_map/ppermute | solution.py:430
  140.4 3.7 %collective-permute-start.27 = (bf16[80,2304]{1,0:T(8,128)(2,1)S(1)}, bf16[80,2304]{1,0:T(8,128)(2,1)}, u32[]{:S(2)}, u32[]{:S(2)}) collective-permute-start(bf16[80,2304]{1,0:T(8,128)(2,1)S(1)} %bitcast.26), channel_id=1, source_target_pairs={{0,24},{8,0},{16,8},{24,16},{32,56},{40,32},{48,40},{56,48},{64,88... | collective-permute-start | bytes 1105928 | tf_op jit(solution)/shard_map/ppermute | solution.py:430
  144.2 10.2 %expert.2 = (bf16[160,2304]{1,0:T(8,128)(2,1)}, bf16[160,2304]{1,0:T(8,128)(2,1)}, bf16[160,2304]{1,0:T(8,128)(2,1)}, bf16[160,2304]{1,0:T(8,128)(2,1)}) custom-call(s32[1]{0:T(128)} %bitcast.place, bf16[80,2304]{1,0:T(8,128)(2,1)} %copy-done.21, bf16[80,2304]{1,0:T(8,128)(2,1)} %copy-done.16, bf16[80,2304]{1,0:T(8,128)(2,1)} %copy-done.20, ...), custom_call_target="tpu_custom_call" | custom-call | flops 3185049600 | bytes 10874880 | tf_op jit(solution)/shard_map/expert/pallas_call | solution.py:326
  154.6 2.7 %collective-permute-start.31 = (bf16[160,2304]{1,0:T(8,128)(2,1)}, bf16[160,2304]{1,0:T(8,128)(2,1)}, u32[]{:S(2)}, u32[]{:S(2)}) collective-permute-start(bf16[160,2304]{1,0:T(8,128)(2,1)} %get-tuple-element.93), channel_id=1, source_target_pairs={{0,96},{8,104},{16,112},{24,120},{32,0},{40,8},{48,16},{56,24},{64... | collective-permute-start | bytes 2211848 | tf_op jit(solution)/shard_map/ppermute | solution.py:430
  157.2 2.7 %collective-permute-start.38 = (bf16[160,2304]{1,0:T(8,128)(2,1)}, bf16[160,2304]{1,0:T(8,128)(2,1)S(1)}, u32[]{:S(2)}, u32[]{:S(2)}) collective-permute-start(bf16[160,2304]{1,0:T(8,128)(2,1)} %get-tuple-element.103), channel_id=1, source_target_pairs={{0,24},{8,0},{16,8},{24,16},{32,56},{40,32},{48,40},{56,48},{64,88... | collective-permute-start | bytes 2211848 | tf_op jit(solution)/shard_map/ppermute | solution.py:430
  159.9 10.3 %expert.3 = (bf16[80,2304]{1,0:T(8,128)(2,1)}, bf16[80,2304]{1,0:T(8,128)(2,1)}, bf16[80,2304]{1,0:T(8,128)(2,1)}, bf16[80,2304]{1,0:T(8,128)(2,1)}, bf16[80,230...) custom-call(s32[1]{0:T(128)} %bitcast.place, ...), custom_call_target="tpu_custom_call" | custom-call | flops 3185049600 | bytes 10874880 | tf_op jit(solution)/shard_map/expert/pallas_call | solution.py:326
  173.6 2.7 %collective-permute-start.32 = (bf16[80,2304]{1,0:T(8,128)(2,1)S(1)}, bf16[80,2304]{1,0:T(8,128)(2,1)S(1)}, u32[]{:S(2)}, u32[]{:S(2)}) collective-permute-start(bf16[80,2304]{1,0:T(8,128)(2,1)S(1)} %add_convert_fusion.2), channel_id=1, source_target_pairs={{0,96},{8,104},{16,112},{24,120},{32,0},{40,8},{48,16},{56,24},{64... | collective-permute-start | bytes 1105928 | tf_op jit(solution)/shard_map/ppermute | solution.py:430
  176.6 2.7 %collective-permute-start.39 = (bf16[80,2304]{1,0:T(8,128)(2,1)S(1)}, bf16[80,2304]{1,0:T(8,128)(2,1)S(1)}, u32[]{:S(2)}, u32[]{:S(2)}) collective-permute-start(bf16[80,2304]{1,0:T(8,128)(2,1)S(1)} %add_convert_fusion), channel_id=1, source_target_pairs={{0,24},{8,0},{16,8},{24,16},{32,56},{40,32},{48,40},{56,48},{64,88... | collective-permute-start | bytes 1105928 | tf_op jit(solution)/shard_map/ppermute | solution.py:430
  185.8 2.0 collective-permute-start.40
  190.1 3.0 %collective-permute-done.34.refs_2_ = bf16[40,2304]{1,0:T(8,128)(2,1)S(1)} collective-permute-done((bf16[40,2304]{1,0:T(8,128)(2,1)S(1)}, bf16[40,2304]{1,0:T(8,128)(2,1)S(1)}, u32[]{:S(2)}, u32[]{:S(2)}) %collective-permute-start.34) | collective-permute-done | bytes 184352 | tf_op jit(solution)/shard_map/ppermute | solution.py:430
  193.1 2.0 collective-permute-done.35.refs_3_
  196.2 20.7 %all_to_all.15 = bf16[8,80,288]{2,1,0:T(8,128)(2,1)S(1)} all-to-all(bf16[8,80,288]{2,1,0:T(8,128)(2,1)S(1)} %finish.1), channel_id=1, replica_groups=mesh['wide'=16,'narrow'=8] {'narrow'}, dimensions={0} | all-to-all | bytes 737280 | tf_op jit(solution)/shard_map/all_to_all | solution.py:455
  (135 shorter events, 35.7 us)
Async XLA Ops:
  0.0 28.7 %all-to-all-start = ((bf16[8,288,360]{2,1,0:T(8,128)(2,1)}), bf16[8,288,360]{2,1,0:T(8,128)(2,1)}, u32[]{:S(2)}, u32[]{:S(2)}) async-start(bf16[8,288,360]{2,1,0:T(8,128)(2,1)} %bitcast.32), calls=%async_computation | async-start | bytes 3538944 | tf_op jit(solution)/shard_map/all_to_all | solution.py:455
  24.5 8.5 %collective-permute-start.1 = (bf16[304,256]{1,0:T(8,128)(2,1)S(1)}, bf16[304,256]{1,0:T(8,128)(2,1)S(1)}, u32[]{:S(2)}, u32[]{:S(2)}) collective-permute-start(bf16[304,256]{1,0:T(8,128)(2,1)S(1)} %get-tuple-element.63), channel_id=1, source_target_pairs={{0,2},{1,3},{2,4},{3,5},{4,6},{5,7},{6,0},{7,1},{8,10},{9,11},{10,... | collective-permute-start | bytes 466952 | tf_op jit(solution)/shard_map/ppermute | solution.py:463
  33.0 111.2 %all-to-all-start.1 = ((bf16[8,2,288,360]{3,2,1,0:T(8,128)(2,1)}), bf16[8,2,288,360]{3,2,1,0:T(8,128)(2,1)}, u32[]{:S(2)}, u32[]{:S(2)}) async-start(bf16[8,2,288,360]{3,2,1,0:T(8,128)(2,1)} %bitcast.31), calls=%async_computation.1 | async-start | bytes 7077888 | tf_op jit(solution)/shard_map/all_to_all | solution.py:455
  40.5 43.0 %collective-permute-start.2 = (bf16[304,256]{1,0:T(8,128)(2,1)S(1)}, bf16[304,256]{1,0:T(8,128)(2,1)S(1)}, u32[]{:S(2)}, u32[]{:S(2)}) collective-permute-start(bf16[304,256]{1,0:T(8,128)(2,1)S(1)} %get-tuple-element.65), channel_id=1, source_target_pairs={{0,4},{1,5},{2,6},{3,7},{4,0},{5,1},{6,2},{7,3},{8,12},{9,13},{10,... | collective-permute-start | bytes 466952 | tf_op jit(solution)/shard_map/ppermute | solution.py:463
  43.5 41.9 %collective-permute-start.3 = (bf16[304,256]{1,0:T(8,128)(2,1)S(1)}, bf16[304,256]{1,0:T(8,128)(2,1)S(1)}, u32[]{:S(2)}, u32[]{:S(2)}) collective-permute-start(bf16[304,256]{1,0:T(8,128)(2,1)S(1)} %get-tuple-element.66), channel_id=1, source_target_pairs={{0,6},{1,7},{2,0},{3,1},{4,2},{5,3},{6,4},{7,5},{8,14},{9,15},{10,... | collective-permute-start | bytes 466952 | tf_op jit(solution)/shard_map/ppermute | solution.py:463
  99.3 11.6 %collective-permute-start.13 = (bf16[40,2304]{1,0:T(8,128)(2,1)S(1)}, bf16[40,2304]{1,0:T(8,128)(2,1)S(1)}, u32[]{:S(2)}, u32[]{:S(2)}) collective-permute-start(bf16[40,2304]{1,0:T(8,128)(2,1)S(1)} %get-tuple-element.112.refs_0_), channel_id=1, source_target_pairs={{0,24},{8,0},{16,8},{24,16},{32,56},{40,32},{48,40},{56,48},{64,88... | collective-permute-start | bytes 552968 | tf_op jit(solution)/shard_map/ppermute | solution.py:430
  103.1 11.0 %collective-permute-start.12 = (bf16[40,2304]{1,0:T(8,128)(2,1)S(1)}, bf16[40,2304]{1,0:T(8,128)(2,1)S(1)}, u32[]{:S(2)}, u32[]{:S(2)}) collective-permute-start(bf16[40,2304]{1,0:T(8,128)(2,1)S(1)} %get-tuple-element.112.refs_0_), channel_id=1, source_target_pairs={{0,8},{8,16},{16,24},{24,0},{32,40},{40,48},{48,56},{56,32},{64,72... | collective-permute-start | bytes 552968 | tf_op jit(solution)/shard_map/ppermute | solution.py:430
  103.2 11.0 %collective-permute-start.11 = (bf16[40,2304]{1,0:T(8,128)(2,1)S(1)}, bf16[40,2304]{1,0:T(8,128)(2,1)S(1)}, u32[]{:S(2)}, u32[]{:S(2)}) collective-permute-start(bf16[40,2304]{1,0:T(8,128)(2,1)S(1)} %get-tuple-element.112.refs_0_), channel_id=1, source_target_pairs={{0,16},{8,24},{16,0},{24,8},{32,48},{40,56},{48,32},{56,40},{64,80... | collective-permute-start | bytes 552968 | tf_op jit(solution)/shard_map/ppermute | solution.py:430
  104.5 12.6 %collective-permute-start.20 = (bf16[40,2304]{1,0:T(8,128)(2,1)S(1)}, bf16[40,2304]{1,0:T(8,128)(2,1)S(1)}, u32[]{:S(2)}, u32[]{:S(2)}) collective-permute-start(bf16[40,2304]{1,0:T(8,128)(2,1)S(1)} %get-tuple-element.111.refs_0_), channel_id=1, source_target_pairs={{0,96},{8,104},{16,112},{24,120},{32,0},{40,8},{48,16},{56,24},{64... | collective-permute-start | bytes 552968 | tf_op jit(solution)/shard_map/ppermute | solution.py:430
  107.2 9.9 %collective-permute-start.19 = (bf16[40,2304]{1,0:T(8,128)(2,1)S(1)}, bf16[40,2304]{1,0:T(8,128)(2,1)S(1)}, u32[]{:S(2)}, u32[]{:S(2)}) collective-permute-start(bf16[40,2304]{1,0:T(8,128)(2,1)S(1)} %get-tuple-element.111.refs_0_), channel_id=1, source_target_pairs={{0,32},{8,40},{16,48},{24,56},{32,64},{40,72},{48,80},{56,88},{64,... | collective-permute-start | bytes 552968 | tf_op jit(solution)/shard_map/ppermute | solution.py:430
  114.3 11.6 %collective-permute-start.16 = (bf16[80,2304]{1,0:T(8,128)(2,1)S(1)}, bf16[80,2304]{1,0:T(8,128)(2,1)S(1)}, u32[]{:S(2)}, u32[]{:S(2)}) collective-permute-start(bf16[80,2304]{1,0:T(8,128)(2,1)S(1)} %bitcast.22), channel_id=1, source_target_pairs={{0,96},{8,104},{16,112},{24,120},{32,0},{40,8},{48,16},{56,24},{64... | collective-permute-start | bytes 1105928 | tf_op jit(solution)/shard_map/ppermute | solution.py:430
  117.1 12.2 %collective-permute-start.14 = (bf16[80,2304]{1,0:T(8,128)(2,1)S(1)}, bf16[80,2304]{1,0:T(8,128)(2,1)S(1)}, u32[]{:S(2)}, u32[]{:S(2)}) collective-permute-start(bf16[80,2304]{1,0:T(8,128)(2,1)S(1)} %bitcast.19), channel_id=1, source_target_pairs={{0,32},{8,40},{16,48},{24,56},{32,64},{40,72},{48,80},{56,88},{64,... | collective-permute-start | bytes 1105928 | tf_op jit(solution)/shard_map/ppermute | solution.py:430
  117.6 11.6 %collective-permute-start.23 = (bf16[80,2304]{1,0:T(8,128)(2,1)S(1)}, bf16[80,2304]{1,0:T(8,128)(2,1)S(1)}, u32[]{:S(2)}, u32[]{:S(2)}) collective-permute-start(bf16[80,2304]{1,0:T(8,128)(2,1)S(1)} %bitcast.28), channel_id=1, source_target_pairs={{0,24},{8,0},{16,8},{24,16},{32,56},{40,32},{48,40},{56,48},{64,88... | collective-permute-start | bytes 1105928 | tf_op jit(solution)/shard_map/ppermute | solution.py:430
  121.4 11.9 %collective-permute-start.21 = (bf16[80,2304]{1,0:T(8,128)(2,1)S(1)}, bf16[80,2304]{1,0:T(8,128)(2,1)S(1)}, u32[]{:S(2)}, u32[]{:S(2)}) collective-permute-start(bf16[80,2304]{1,0:T(8,128)(2,1)S(1)} %bitcast.25), channel_id=1, source_target_pairs={{0,8},{8,16},{16,24},{24,0},{32,40},{40,48},{48,56},{56,32},{64,72... | collective-permute-start | bytes 1105928 | tf_op jit(solution)/shard_map/ppermute | solution.py:430
  125.8 10.1 %collective-permute-start.17 = (bf16[80,2304]{1,0:T(8,128)(2,1)S(1)}, bf16[80,2304]{1,0:T(8,128)(2,1)S(1)}, u32[]{:S(2)}, u32[]{:S(2)}) collective-permute-start(bf16[80,2304]{1,0:T(8,128)(2,1)S(1)} %collective-permute-done.16.refs_1_), channel_id=1, source_target_pairs={{0,96},{8,104},{16,112},{24,120},{32,0},{40,8},{48,16},{56,24},{64... | collective-permute-start | bytes 1105928 | tf_op jit(solution)/shard_map/ppermute | solution.py:430
  129.3 10.1 %collective-permute-start.15 = (bf16[80,2304]{1,0:T(8,128)(2,1)S(1)}, bf16[80,2304]{1,0:T(8,128)(2,1)S(1)}, u32[]{:S(2)}, u32[]{:S(2)}) collective-permute-start(bf16[80,2304]{1,0:T(8,128)(2,1)S(1)} %collective-permute-done.14.refs_3_), channel_id=1, source_target_pairs={{0,32},{8,40},{16,48},{24,56},{32,64},{40,72},{48,80},{56,88},{64,... | collective-permute-start | bytes 1105928 | tf_op jit(solution)/shard_map/ppermute | solution.py:430
  129.3 11.2 %collective-permute-start.24 = (bf16[80,2304]{1,0:T(8,128)(2,1)S(1)}, bf16[80,2304]{1,0:T(8,128)(2,1)S(1)}, u32[]{:S(2)}, u32[]{:S(2)}) collective-permute-start(bf16[80,2304]{1,0:T(8,128)(2,1)S(1)} %collective-permute-done.23.refs_5_), channel_id=1, source_target_pairs={{0,24},{8,0},{16,8},{24,16},{32,56},{40,32},{48,40},{56,48},{64,88... | collective-permute-start | bytes 1105928 | tf_op jit(solution)/shard_map/ppermute | solution.py:430
  133.3 10.9 %collective-permute-start.22 = (bf16[80,2304]{1,0:T(8,128)(2,1)S(1)}, bf16[80,2304]{1,0:T(8,128)(2,1)}, u32[]{:S(2)}, u32[]{:S(2)}) collective-permute-start(bf16[80,2304]{1,0:T(8,128)(2,1)S(1)} %collective-permute-done.21.refs_7_), channel_id=1, source_target_pairs={{0,8},{8,16},{16,24},{24,0},{32,40},{40,48},{48,56},{56,32},{64,72... | collective-permute-start | bytes 1105928 | tf_op jit(solution)/shard_map/ppermute | solution.py:430
  133.3 21.2 %collective-permute-start.26 = (bf16[80,2304]{1,0:T(8,128)(2,1)S(1)}, bf16[80,2304]{1,0:T(8,128)(2,1)}, u32[]{:S(2)}, u32[]{:S(2)}) collective-permute-start(bf16[80,2304]{1,0:T(8,128)(2,1)S(1)} %bitcast.23), channel_id=1, source_target_pairs={{0,32},{8,40},{16,48},{24,56},{32,64},{40,72},{48,80},{56,88},{64,... | collective-permute-start | bytes 1105928 | tf_op jit(solution)/shard_map/ppermute | solution.py:430
  136.0 18.5 %collective-permute-start.25 = (bf16[80,2304]{1,0:T(8,128)(2,1)S(1)}, bf16[80,2304]{1,0:T(8,128)(2,1)}, u32[]{:S(2)}, u32[]{:S(2)}) collective-permute-start(bf16[80,2304]{1,0:T(8,128)(2,1)S(1)} %bitcast.20), channel_id=1, source_target_pairs={{0,96},{8,104},{16,112},{24,120},{32,0},{40,8},{48,16},{56,24},{64... | collective-permute-start | bytes 1105928 | tf_op jit(solution)/shard_map/ppermute | solution.py:430
  139.4 15.1 %collective-permute-start.28 = (bf16[80,2304]{1,0:T(8,128)(2,1)S(1)}, bf16[80,2304]{1,0:T(8,128)(2,1)}, u32[]{:S(2)}, u32[]{:S(2)}) collective-permute-start(bf16[80,2304]{1,0:T(8,128)(2,1)S(1)} %bitcast.29), channel_id=1, source_target_pairs={{0,8},{8,16},{16,24},{24,0},{32,40},{40,48},{48,56},{56,32},{64,72... | collective-permute-start | bytes 1105928 | tf_op jit(solution)/shard_map/ppermute | solution.py:430
  140.4 14.0 %collective-permute-start.27 = (bf16[80,2304]{1,0:T(8,128)(2,1)S(1)}, bf16[80,2304]{1,0:T(8,128)(2,1)}, u32[]{:S(2)}, u32[]{:S(2)}) collective-permute-start(bf16[80,2304]{1,0:T(8,128)(2,1)S(1)} %bitcast.26), channel_id=1, source_target_pairs={{0,24},{8,0},{16,8},{24,16},{32,56},{40,32},{48,40},{56,48},{64,88... | collective-permute-start | bytes 1105928 | tf_op jit(solution)/shard_map/ppermute | solution.py:430
  154.5 16.7 %collective-permute-start.29 = (bf16[160,2304]{1,0:T(8,128)(2,1)}, bf16[160,2304]{1,0:T(8,128)(2,1)S(1)}, u32[]{:S(2)}, u32[]{:S(2)}) collective-permute-start(bf16[160,2304]{1,0:T(8,128)(2,1)} %get-tuple-element.92), channel_id=1, source_target_pairs={{0,32},{8,40},{16,48},{24,56},{32,64},{40,72},{48,80},{56,88},{64,... | collective-permute-start | bytes 2211848 | tf_op jit(solution)/shard_map/ppermute | solution.py:430
  154.6 17.8 %collective-permute-start.31 = (bf16[160,2304]{1,0:T(8,128)(2,1)}, bf16[160,2304]{1,0:T(8,128)(2,1)}, u32[]{:S(2)}, u32[]{:S(2)}) collective-permute-start(bf16[160,2304]{1,0:T(8,128)(2,1)} %get-tuple-element.93), channel_id=1, source_target_pairs={{0,96},{8,104},{16,112},{24,120},{32,0},{40,8},{48,16},{56,24},{64... | collective-permute-start | bytes 2211848 | tf_op jit(solution)/shard_map/ppermute | solution.py:430
  157.2 19.1 %collective-permute-start.36 = (bf16[160,2304]{1,0:T(8,128)(2,1)}, bf16[160,2304]{1,0:T(8,128)(2,1)S(1)}, u32[]{:S(2)}, u32[]{:S(2)}) collective-permute-start(bf16[160,2304]{1,0:T(8,128)(2,1)} %get-tuple-element.102), channel_id=1, source_target_pairs={{0,8},{8,16},{16,24},{24,0},{32,40},{40,48},{48,56},{56,32},{64,72... | collective-permute-start | bytes 2211848 | tf_op jit(solution)/shard_map/ppermute | solution.py:430
  157.2 19.2 %collective-permute-start.38 = (bf16[160,2304]{1,0:T(8,128)(2,1)}, bf16[160,2304]{1,0:T(8,128)(2,1)S(1)}, u32[]{:S(2)}, u32[]{:S(2)}) collective-permute-start(bf16[160,2304]{1,0:T(8,128)(2,1)} %get-tuple-element.103), channel_id=1, source_target_pairs={{0,24},{8,0},{16,8},{24,16},{32,56},{40,32},{48,40},{56,48},{64,88... | collective-permute-start | bytes 2211848 | tf_op jit(solution)/shard_map/ppermute | solution.py:430
  176.4 9.1 %collective-permute-start.37 = (bf16[80,2304]{1,0:T(8,128)(2,1)S(1)}, bf16[80,2304]{1,0:T(8,128)(2,1)S(1)}, u32[]{:S(2)}, u32[]{:S(2)}) collective-permute-start(bf16[80,2304]{1,0:T(8,128)(2,1)S(1)} %add_convert_fusion.1), channel_id=1, source_target_pairs={{0,8},{8,16},{16,24},{24,0},{32,40},{40,48},{48,56},{56,32},{64,72... | collective-permute-start | bytes 1105928 | tf_op jit(solution)/shard_map/ppermute | solution.py:430
  176.6 8.9 %collective-permute-start.39 = (bf16[80,2304]{1,0:T(8,128)(2,1)S(1)}, bf16[80,2304]{1,0:T(8,128)(2,1)S(1)}, u32[]{:S(2)}, u32[]{:S(2)}) collective-permute-start(bf16[80,2304]{1,0:T(8,128)(2,1)S(1)} %add_convert_fusion), channel_id=1, source_target_pairs={{0,24},{8,0},{16,8},{24,16},{32,56},{40,32},{48,40},{56,48},{64,88... | collective-permute-start | bytes 1105928 | tf_op jit(solution)/shard_map/ppermute | solution.py:430
  182.1 7.9 %collective-permute-start.33 = (bf16[40,2304]{1,0:T(8,128)(2,1)S(1)}, bf16[40,2304]{1,0:T(8,128)(2,1)S(1)}, u32[]{:S(2)}, u32[]{:S(2)}) collective-permute-start(bf16[40,2304]{1,0:T(8,128)(2,1)S(1)} %get-tuple-element.97), channel_id=1, source_target_pairs={{0,16},{8,24},{16,0},{24,8},{32,48},{40,56},{48,32},{56,40},{64,80... | collective-permute-start | bytes 552968 | tf_op jit(solution)/shard_map/ppermute | solution.py:430
  184.0 9.1 %collective-permute-start.34 = (bf16[40,2304]{1,0:T(8,128)(2,1)S(1)}, bf16[40,2304]{1,0:T(8,128)(2,1)S(1)}, u32[]{:S(2)}, u32[]{:S(2)}) collective-permute-start(bf16[40,2304]{1,0:T(8,128)(2,1)S(1)} %get-tuple-element.98), channel_id=1, source_target_pairs={{0,24},{8,0},{16,8},{24,16},{32,56},{40,32},{48,40},{56,48},{64,88... | collective-permute-start | bytes 552968 | tf_op jit(solution)/shard_map/ppermute | solution.py:430
  184.0 11.1 %collective-permute-start.35 = (bf16[40,2304]{1,0:T(8,128)(2,1)S(1)}, bf16[40,2304]{1,0:T(8,128)(2,1)S(1)}, u32[]{:S(2)}, u32[]{:S(2)}) collective-permute-start(bf16[40,2304]{1,0:T(8,128)(2,1)S(1)} %get-tuple-element.99), channel_id=1, source_target_pairs={{0,8},{8,16},{16,24},{24,0},{32,40},{40,48},{48,56},{56,32},{64,72... | collective-permute-start | bytes 552968 | tf_op jit(solution)/shard_map/ppermute | solution.py:430
  185.8 9.3 %collective-permute-start.40 = (bf16[40,2304]{1,0:T(8,128)(2,1)S(1)}, bf16[40,2304]{1,0:T(8,128)(2,1)S(1)}, u32[]{:S(2)}, u32[]{:S(2)}) collective-permute-start(bf16[40,2304]{1,0:T(8,128)(2,1)S(1)} %get-tuple-element.107), channel_id=1, source_target_pairs={{0,64},{8,72},{16,80},{24,88},{32,96},{40,104},{48,112},{56,120},{... | collective-permute-start | bytes 552968 | tf_op jit(solution)/shard_map/ppermute | solution.py:430
  (36 other events, 454.3 us)
